TPU v7x, 32 devices: a whole 2x2x4 slice. The times are simulated.
32 devices in a mesh: wide: 4 (over z), narrow: 8 (over y, x, core).
Axes of the slice: x: 2, y: 2, z: 4, core: 2. Of those that a mesh axis runs over, the one named last changes fastest.
Arguments:
- layer_entry_input: bfloat16 [4096, 2048], P('wide'), may hold values from -6 to 6
- ln1_gain: float32 [2048], replicated, may hold values from 0.5 to 1.5
- ln1_bias: float32 [2048], replicated, may hold values from -1 to 1
- w_qkv: bfloat16 [2048, 3, 2048], P(None, None, 'narrow'), may hold values from -0.125 to 0.125
- b_qv: float32 [2, 2048], P(None, 'narrow'), may hold values from -1.5 to 1.5
- w_out: bfloat16 [2048, 2048], P('narrow'), may hold values from -2 to 2
- b_out: float32 [2048], replicated, may hold values from -1.5 to 1.5
- ln2_gain: float32 [2048], replicated, may hold values from 0.5 to 1.5
- ln2_bias: float32 [2048], replicated, may hold values from -1 to 1
- w_up: bfloat16 [2048, 8192], P(None, 'narrow'), may hold values from -0.125 to 0.125
- b_up: float32 [8192], P('narrow'), may hold values from -2.5 to 2.5
- w_down: bfloat16 [8192, 2048], P('narrow'), may hold values from -0.0625 to 0.0625
- b_down: float32 [2048], replicated, may hold values from -1.5 to 1.5
- document_index: int32 [4096], replicated, may hold values from 0 to 8, as said below
- positions: int32 [4096], replicated, may hold values from 0 to 767, as said below
- valid: int32 [4096], replicated, may hold values from 0 to 1, as said below
- cotangent: bfloat16 [4096, 2048], P('wide'), may hold values from -6 to 6
Outputs:
- output: bfloat16 [4096, 2048], P('wide')
- grad_input: bfloat16 [4096, 2048], P('wide')
- grad_ln1_gain: float32 [2048], replicated
- grad_ln1_bias: float32 [2048], replicated
- grad_w_qkv: float32 [2048, 3, 2048], P(None, None, 'narrow')
- grad_b_qv: float32 [2, 2048], P(None, 'narrow')
- grad_w_out: float32 [2048, 2048], P('narrow')
- grad_b_out: float32 [2048], replicated
- grad_ln2_gain: float32 [2048], replicated
- grad_ln2_bias: float32 [2048], replicated
- grad_w_up: float32 [2048, 8192], P(None, 'narrow')
- grad_b_up: float32 [8192], P('narrow')
- grad_w_down: float32 [8192, 2048], P('narrow')
- grad_b_down: float32 [2048], replicated
Inputs may be any that keep to these rules, and one draw needn't show every extreme that they name: `document_index`: documents are contiguous and numbered in order from 0; each block of 1024 tokens of one index of wide holds exactly two document starts, and every document has at most 768 tokens. `positions`: counts from 0 at the first token of each document, padding included. `valid`: 0 exactly on the last 1 to 64 tokens of each document.
All inputs are finite; a program needn't handle non-finite values.
Results may differ from a plain program's by a relative error of at most 0.019.
Values may be sent and summed in bfloat16 or wider, within the bound.
No kernel may reach another device: no remote copies, remote signals or barrier semaphores. Data moves between devices by JAX's collectives and lax.ppermute only.
A program may use at most 192 MiB of HBM per device.

v0:
```python
import jax
import jax.numpy as jnp
from jax import lax
from jax.experimental import pallas as pl
from jax.sharding import PartitionSpec as P


HEAD_DIM = 128
MAX_DOCUMENT = 768
QUERY_BLOCK = 256
WINDOW = MAX_DOCUMENT + QUERY_BLOCK
LAG = 3
f32 = jnp.float32
bf16 = jnp.bfloat16


def add_low(a, b):
    return (a.astype(f32) + b.astype(f32)).astype(a.dtype)


def pick(value, index, dim):
    return lax.dynamic_index_in_dim(value, index, dim, keepdims=False)


def narrow_bit(bit):
    return (lax.axis_index("narrow") >> bit) & 1


def narrow_bits():
    return lax.axis_size("narrow").bit_length() - 1


def swap(value, bit):
    count = lax.axis_size("narrow")
    return lax.ppermute(value, "narrow", [(i, i ^ (1 << bit)) for i in range(count)])


def bit_orders():
    later = list(range(1, narrow_bits()))
    return later, later[::-1]


def row_block():
    bits = narrow_bits()
    return sum(narrow_bit(b) << (bits - 1 - b) for b in range(bits))


def as_is(*values):
    return values


def at_calls(sync, *which):
    count = iter(range(99))
    return lambda *values: sync(*values) if next(count) in which else values


def reduce_rows(value, sync=as_is):
    bits = narrow_bits()
    rows, width = value.shape
    half_rows = rows >> (bits + 1)
    value = value.reshape(2, rows // 2, width)
    mine = narrow_bit(0)
    got = swap(pick(value, 1 - mine, 0), 0)
    value = add_low(pick(value, mine, 0), got)
    (value,) = sync(value)
    value = value.reshape((2,) * (bits - 1) + (2, half_rows, width))
    orders = bit_orders()
    parts = [lax.index_in_dim(value, half, bits - 1, keepdims=False) for half in range(2)]
    left = [list(range(1, bits)) for _ in orders]
    for step in range(bits - 1):
        for half, order in enumerate(orders):
            b = order[step]
            at = left[half].index(b)
            mine = narrow_bit(b)
            piece = parts[half]
            got = swap(pick(piece, 1 - mine, at), b)
            parts[half] = add_low(pick(piece, mine, at), got)
            left[half].pop(at)
        parts = list(sync(*parts))
    return jnp.concatenate(parts, axis=0)


def pair(value, other, bit, dim):
    return jnp.where(
        narrow_bit(bit) == 0, jnp.stack([value, other], axis=dim), jnp.stack([other, value], axis=dim)
    )


def gather_rows(block, sync=as_is):
    bits = narrow_bits()
    rows, width = block.shape
    orders = [order[::-1] for order in bit_orders()]
    parts = [block[half * (rows // 2) : (half + 1) * (rows // 2)] for half in range(2)]
    for step in range(bits - 1):
        for half, order in enumerate(orders):
            b = order[step]
            at = sum(1 for x in order[:step] if x < b)
            got = swap(parts[half], b)
            parts[half] = pair(parts[half], got, b, at)
        parts = list(sync(*parts))
    value = jnp.stack(parts, axis=bits - 1)
    value = pair(value, swap(value, 0), 0, 0)
    return value.reshape(rows << bits, width)


def narrow_total(value):
    for b in range(narrow_bits()):
        value = value + swap(value, b)
    return value


class Line:
    def __init__(self):
        self.count = lax.axis_size("wide")
        self.half = self.count // 2
        self.at = lax.axis_index("wide")
        self.depth = jnp.minimum(self.at, self.count - 1 - self.at)

    def exchange(self, value, kind):
        moves = {i: i for i in range(self.count)}
        for i in range(kind, self.count - 1, 2):
            moves[i], moves[i + 1] = i + 1, i
        return lax.ppermute(value, "wide", list(moves.items()))

    def swaps(self, kind, slot, count):
        n, half = self.count, self.half
        plan = []
        for e in range(half):
            if e % 2 == kind:
                sent = slot - LAG * (e // 2)
                add = e == half - 1
                got = sent if add else slot - LAG * ((n - 2 - e) // 2)
            elif e:
                sent, got, add = slot - LAG * ((n - 1 - e) // 2), slot - LAG * ((e - 1) // 2), True
            else:
                continue
            sent = sent if 0 <= sent < count else None
            got = got if 0 <= got < count else None
            plan.append((e, sent, got, add))
        return plan

    def whole(self, value):
        stream = Stream(self, 1)
        stream.feed(value)
        for slot in range(stream.slots()):
            for kind in range(2):
                stream.start(kind, slot)
                stream.take(kind, slot, stream.waiting(kind, slot))
        return stream.chunks[0]


class Stream:
    def __init__(self, line, count):
        self.line = line
        self.count = count
        self.chunks = []
        self.flying = {}
        self.turn = 0

    def slots(self):
        return self.count + LAG * ((self.line.count - 2) // 2)

    def feed(self, chunk):
        self.chunks.append(chunk)

    def start(self, kind, slot):
        plan = self.line.swaps(kind, slot, self.count)
        sends = [(e, sent) for e, sent, _, _ in plan if sent is not None]
        if not sends:
            return
        value = self.chunks[sends[0][1]]
        for e, sent in sends[1:]:
            value = jnp.where(self.line.depth == e, self.chunks[sent], value)
        got = self.line.exchange(value, kind)
        self.flying[kind, slot] = got, plan

    def waiting(self, kind, slot):
        flight = self.flying.get((kind, slot))
        return () if flight is None else flight[:1]

    def take(self, kind, slot, values):
        short = self.line.half == 2
        for got in values:
            for e, _, k, add in self.flying[kind, slot][1]:
                if k is None:
                    continue
                held = self.chunks[k]
                new = add_low(held, got) if add else got
                if not (add and short):
                    new = jnp.where(self.line.depth == e, new, held)
                self.chunks[k] = new

    def begin(self):
        self.start(0, 0)
        self.start(0, 1)

    def sync(self, *values):
        n = self.turn
        self.turn += 1
        outer, inner = self.waiting(0, n), self.waiting(1, n - 1)
        held = lax.optimization_barrier(outer + inner + tuple(values))
        self.take(0, n, held[: len(outer)])
        self.take(1, n - 1, held[len(outer) : len(outer) + len(inner)])
        self.start(1, n)
        self.start(0, n + 2)
        return held[len(outer) + len(inner) :]

    def finish(self):
        while self.turn < self.slots():
            self.sync()


def norm_stats(values):
    center = values - jnp.mean(values, axis=-1, keepdims=True)
    spread = jnp.mean(center * center, axis=-1, keepdims=True)
    inverse = lax.rsqrt(spread + 1e-05)
    return (center * inverse, inverse)


def norm_back(grad_out, normed_raw, inverse, gain):
    scaled = grad_out * gain
    grad_in = inverse * (
        scaled
        - jnp.mean(scaled, axis=-1, keepdims=True)
        - normed_raw * jnp.mean(scaled * normed_raw, axis=-1, keepdims=True)
    )
    return (grad_in, jnp.sum(grad_out * normed_raw, axis=0), jnp.sum(grad_out, axis=0))


def dot(a, b, dims):
    return lax.dot_general(a, b, (dims, ((), ())), preferred_element_type=f32)


def window_probs(query, keys, pos, valid):
    scores = dot(query, keys, ((1,), (1,))) * HEAD_DIM**-0.5
    own = lax.broadcasted_iota(jnp.int32, scores.shape, 0) + MAX_DOCUMENT
    key = lax.broadcasted_iota(jnp.int32, scores.shape, 1)
    back = own - key
    allowed = ((back >= 0) & (back <= pos) & (valid == 1)) | (back == 0)
    scores = jnp.where(allowed, scores, -1e30)
    exps = jnp.exp(scores - jnp.max(scores, axis=-1, keepdims=True))
    return exps * (1.0 / jnp.sum(exps, axis=-1, keepdims=True))


def attend_kernel(q_ref, k_ref, v_ref, pos_ref, valid_ref, out_ref):
    start = pl.multiple_of(pl.program_id(1) * QUERY_BLOCK, QUERY_BLOCK)
    window = pl.ds(start, WINDOW)
    probs = window_probs(q_ref[...], k_ref[window, :], pos_ref[...], valid_ref[0])
    out_ref[...] = dot(probs.astype(bf16), v_ref[window, :], ((1,), (0,))).astype(bf16)


def attend_back_kernel(q_ref, k_ref, v_ref, do_ref, pos_ref, valid_ref, dq_ref, dk_ref, dv_ref):
    start = pl.multiple_of(pl.program_id(1) * QUERY_BLOCK, QUERY_BLOCK)
    window = pl.ds(start, WINDOW)

    @pl.when(pl.program_id(1) == 0)
    def _():
        dk_ref[...] = jnp.zeros_like(dk_ref)
        dv_ref[...] = jnp.zeros_like(dv_ref)

    query, keys, out = q_ref[...], k_ref[window, :], do_ref[...]
    probs = window_probs(query, keys, pos_ref[...], valid_ref[0])
    dprob = dot(out, v_ref[window, :], ((1,), (1,)))
    dscore = probs * (dprob - jnp.sum(probs * dprob, axis=-1, keepdims=True))
    dscore = dscore.astype(bf16)
    dq_ref[...] = (dot(dscore, keys, ((1,), (0,))) * HEAD_DIM**-0.5).astype(bf16)
    dk_ref[window, :] += dot(dscore, query, ((0,), (0,))) * HEAD_DIM**-0.5
    dv_ref[window, :] += dot(probs.astype(bf16), out, ((0,), (0,)))


def attend_specs(rows, heads):
    block = pl.BlockSpec((QUERY_BLOCK, HEAD_DIM), lambda h, i: (i, h))
    keys = pl.BlockSpec((rows + MAX_DOCUMENT, HEAD_DIM), lambda h, i: (0, h))
    vals = pl.BlockSpec((rows + MAX_DOCUMENT, HEAD_DIM), lambda h, i: (0, h + heads))
    pos = pl.BlockSpec((QUERY_BLOCK, 1), lambda h, i: (i, 0))
    valid = pl.BlockSpec((1, 1, WINDOW), lambda h, i: (i, 0, 0))
    return block, keys, vals, pos, valid


def attend(query, keys_vals, pos, valid):
    rows, width = query.shape
    heads = width // HEAD_DIM
    block, keys_spec, vals_spec, pos_spec, valid_spec = attend_specs(rows, heads)
    return pl.pallas_call(
        attend_kernel,
        grid=(heads, rows // QUERY_BLOCK),
        in_specs=[block, keys_spec, vals_spec, pos_spec, valid_spec],
        out_specs=block,
        out_shape=jax.ShapeDtypeStruct((rows, width), bf16),
        name="attend",
    )(query, keys_vals, keys_vals, pos, valid)


def attend_back(query, keys_vals, out, pos, valid):
    rows, width = query.shape
    heads = width // HEAD_DIM
    block, keys_spec, vals_spec, pos_spec, valid_spec = attend_specs(rows, heads)
    wide_shape = jax.ShapeDtypeStruct((rows + MAX_DOCUMENT, width), f32)
    return pl.pallas_call(
        attend_back_kernel,
        grid=(heads, rows // QUERY_BLOCK),
        in_specs=[block, keys_spec, vals_spec, block, pos_spec, valid_spec],
        out_specs=[block, keys_spec, keys_spec],
        out_shape=[jax.ShapeDtypeStruct((rows, width), bf16), wide_shape, wide_shape],
        name="attend_back",
    )(query, keys_vals, keys_vals, out, pos, valid)


def on_device(
    layer_entry_input,
    ln1_gain,
    ln1_bias,
    w_qkv,
    b_qv,
    w_out,
    b_out,
    ln2_gain,
    ln2_bias,
    w_up,
    b_up,
    w_down,
    b_down,
    document_index,
    positions,
    valid,
    cotangent,
):
    rows, width = layer_entry_input.shape
    local_width = w_qkv.shape[2]
    hidden = w_up.shape[1]
    line = Line()
    start = line.at * rows
    ahead = [(i, i + 1) for i in range(line.count - 1)]
    behind = [(i + 1, i) for i in range(line.count - 1)]
    block_rows = rows // lax.axis_size("narrow")
    block_start = row_block() * block_rows

    def rows_of(value):
        return lax.dynamic_slice_in_dim(value, block_start, block_rows, 0)

    pos = lax.dynamic_slice_in_dim(positions, start, rows, 0).reshape(rows, 1)
    padded_valid = jnp.concatenate([jnp.zeros((MAX_DOCUMENT,), jnp.int32), valid])
    valid_near = lax.dynamic_slice_in_dim(padded_valid, start, rows + MAX_DOCUMENT, 0)
    valid_windows = jnp.stack(
        [valid_near[i : i + WINDOW] for i in range(0, rows, QUERY_BLOCK)]
    ).reshape(rows // QUERY_BLOCK, 1, WINDOW)

    inputs = layer_entry_input.astype(f32)
    raw_one, _ = norm_stats(inputs)
    normed_one = (raw_one * ln1_gain + ln1_bias).astype(bf16)
    w_flat = w_qkv.reshape(width, 3 * local_width)
    mixed = dot(normed_one, w_flat[:, local_width:], ((1,), (0,)))
    bias = jnp.concatenate([jnp.zeros_like(b_qv[1]), b_qv[1]])
    keys_vals = (mixed + bias).astype(bf16)
    halo = lax.ppermute(keys_vals[rows - MAX_DOCUMENT :], "wide", ahead)
    query = (dot(normed_one, w_flat[:, :local_width], ((1,), (0,))) + b_qv[0]).astype(bf16)
    grad_active = dot(cotangent, w_down, ((1,), (1,))).astype(bf16)
    halo, query, grad_active = lax.optimization_barrier((halo, query, grad_active))
    keys_vals = jnp.concatenate([halo, keys_vals])
    attended = attend(query, keys_vals, pos, valid_windows)
    attn_part = dot(attended, w_out, ((1,), (0,))).astype(bf16)
    attn_total = reduce_rows(attn_part).astype(f32)
    inputs_rows = rows_of(layer_entry_input).astype(f32)
    after_attn = inputs_rows + b_out + attn_total
    raw_two, inv_two = norm_stats(after_attn)
    normed_two = gather_rows((raw_two * ln2_gain + ln2_bias).astype(bf16))

    upper = dot(normed_two, w_up, ((1,), (0,))) + b_up
    active, gelu_pull = jax.vjp(jax.nn.gelu, upper)
    active = active.astype(bf16)
    grad_upper = gelu_pull(grad_active.astype(f32))[0].astype(bf16)

    bulk = Stream(line, 12)
    step = width // 4
    places = [(i, j) for i in range(0, hidden, step) for j in range(0, width, hidden)]
    for i, j in places:
        bulk.feed(
            dot(active[:, i : i + step], cotangent[:, j : j + hidden], ((0,), (0,))).astype(bf16)
        )
    bulk.begin()
    for i in range(4):
        bulk.feed(
            dot(normed_two[:, i * step : (i + 1) * step], grad_upper, ((0,), (0,))).astype(bf16)
        )
    grad_b_up = jnp.sum(grad_upper.astype(f32), axis=0)
    back_part = dot(grad_upper, w_up, ((1,), (1,))).astype(bf16)
    grad_norm_two = reduce_rows(back_part, at_calls(bulk.sync, 1)).astype(f32)
    grad_resid, grad_ln2_gain, grad_ln2_bias = norm_back(grad_norm_two, raw_two, inv_two, ln2_gain)
    grad_out_rows = rows_of(cotangent).astype(f32)
    grad_mid = grad_out_rows + grad_resid
    grad_mid_low = gather_rows(grad_mid.astype(bf16), at_calls(bulk.sync, 0))
    grad_attended = dot(grad_mid_low, w_out, ((1,), (1,))).astype(bf16)
    bulk.feed(
        jnp.concatenate(
            [
                dot(attended, grad_mid_low[:, j : j + hidden], ((0,), (0,))).astype(bf16)
                for j in range(0, width, hidden)
            ]
        ),
    )
    (grad_attended,) = bulk.sync(grad_attended)
    grad_query, grad_keys, grad_vals = attend_back(
        query, keys_vals, grad_attended, pos, valid_windows
    )
    grad_kv = jnp.concatenate([grad_keys, grad_vals], axis=1)
    got = lax.ppermute(grad_kv[:MAX_DOCUMENT].astype(bf16), "wide", behind)
    own = grad_kv[MAX_DOCUMENT:]
    mlp_part = dot(active, w_down, ((1,), (0,))).astype(bf16)
    own, mlp_part = bulk.sync(own, mlp_part)
    held = [own]

    def sync_own(*values):
        *values, held[0] = bulk.sync(*values, held[0])
        return values

    mlp_total = reduce_rows(mlp_part, at_calls(sync_own, 1)).astype(f32)
    own = held[0]
    low = rows - MAX_DOCUMENT
    grad_kv = jnp.concatenate([own[:low], own[low:] + got.astype(f32)]).astype(bf16)
    grad_mixed = jnp.concatenate([grad_query, grad_kv], axis=1)
    parts = [
        dot(normed_one[:, i * step : (i + 1) * step], grad_mixed, ((0,), (0,))).astype(bf16)
        for i in range(3)
    ]
    rest = dot(normed_one[:, 3 * step :], grad_mixed, ((0,), (0,))).astype(bf16)
    for i in range(3):
        extra = rest[:, i * local_width : (i + 1) * local_width]
        bulk.feed(jnp.concatenate([parts[i], extra], axis=1))
    grad_mixed, mlp_total = bulk.sync(grad_mixed, mlp_total)
    grad_b_qv = jnp.sum(grad_mixed.astype(f32), axis=0)
    grad_b_qv = [grad_b_qv[i * local_width : (i + 1) * local_width] for i in (0, 2)]
    back_part = dot(grad_mixed, w_flat, ((1,), (1,))).astype(bf16)
    output = gather_rows((after_attn + b_down + mlp_total).astype(bf16))
    grad_norm_one = reduce_rows(back_part, at_calls(bulk.sync, 1)).astype(f32)
    raw_rows, inv_rows = norm_stats(inputs_rows)
    grad_resid, grad_ln1_gain, grad_ln1_bias = norm_back(
        grad_norm_one, raw_rows, inv_rows, ln1_gain
    )
    grad_input = gather_rows((grad_mid + grad_resid).astype(bf16), at_calls(bulk.sync, 0))

    sums = narrow_total(
        jnp.stack(
            [
                grad_ln2_gain,
                grad_ln2_bias,
                jnp.sum(grad_mid, axis=0),
                jnp.sum(grad_out_rows, axis=0),
                grad_ln1_gain,
                grad_ln1_bias,
            ]
        )
    )
    sums = jnp.concatenate([sums.reshape(-1), grad_b_up] + grad_b_qv)
    sums = line.whole(sums.reshape(-1, 128)).reshape(-1)
    bulk.finish()
    grad_ln2_gain, grad_ln2_bias, grad_b_out, grad_b_down, grad_ln1_gain, grad_ln1_bias = sums[
        : 6 * width
    ].reshape(6, width)
    grad_b_up = sums[6 * width : 6 * width + hidden]
    grad_b_qv = sums[6 * width + hidden :].reshape(2, local_width)

    done = [value.astype(f32) for value in bulk.chunks]
    per_row = width // hidden
    grad_w_down = jnp.concatenate(
        [jnp.concatenate(done[i : i + per_row], axis=1) for i in range(0, 4, per_row)]
    )
    grad_w_up = jnp.concatenate(done[4:8])
    grad_w_out = jnp.concatenate(
        [done[8][i * local_width : (i + 1) * local_width] for i in range(per_row)], axis=1
    )
    mixed_done = done[9:12]
    grad_w_qkv = jnp.stack(
        [
            jnp.concatenate(
                [value[:, c * local_width : (c + 1) * local_width] for value in mixed_done]
                + [mixed_done[c][:, 3 * local_width :]]
            )
            for c in range(3)
        ],
        axis=1,
    )
    return (
        output,
        grad_input,
        grad_ln1_gain,
        grad_ln1_bias,
        grad_w_qkv,
        grad_b_qv,
        grad_w_out,
        grad_b_out,
        grad_ln2_gain,
        grad_ln2_bias,
        grad_w_up,
        grad_b_up,
        grad_w_down,
        grad_b_down,
    )


def solution(mesh):
    return jax.shard_map(
        on_device,
        mesh=mesh,
        in_specs=(
            P("wide", None),
            P(),
            P(),
            P(None, None, "narrow"),
            P(None, "narrow"),
            P("narrow", None),
            P(),
            P(),
            P(),
            P(None, "narrow"),
            P("narrow"),
            P("narrow", None),
            P(),
            P(),
            P(),
            P(),
            P("wide", None),
        ),
        out_specs=(
            P("wide", None),
            P("wide", None),
            P(),
            P(),
            P(None, None, "narrow"),
            P(None, "narrow"),
            P("narrow", None),
            P(),
            P(),
            P(),
            P(None, "narrow"),
            P("narrow"),
            P("narrow", None),
            P(),
        ),
        check_vma=False,
    )
```

profile of v0, /device:TPU:0, one launch (start us, length us, event | category | flops | bytes accessed | tf_op | source)
XLA Modules:
  0.0 643.9 jit_solution(12845012978551730059)
XLA Ops:
  6.2 4.7 copy.56
  17.7 5.0 collective-permute-start
  25.2 4.6 fusion.54.q_ref
  29.8 9.3 %convolution_convert_fusion.4 = bf16[1024,1024]{1,0:T(8,128)(2,1)} fusion(bf16[1024,2048]{1,0:T(8,128)(2,1)} %param.32, bf16[1024,2048]{1,0:T(8,128)(2,1)} %param.28), kind=kOutput, calls=%fused_computation.87 | convolution fusion | flops 4296015872 | bytes 10485760 | tf_op jit(solution)/shard_map/dot_general | solution.py:231
  41.1 9.8 %attend.1 = bf16[1024,256]{1,0:T(8,128)(2,1)} custom-call(bf16[1024,256]{1,0:T(8,128)(2,1)} %fusion.54.q_ref, bf16[1792,512]{1,0:T(8,128)(2,1)} %pad_maximum_fusion.6.k_ref.v_ref, bf16[1792,512]{1,0:T(8,128)(2,1)} %pad_maximum_fusion.6.k_ref.v_ref, s32[1024,1]{1,0:T(8,128)} %copy.57.pos_ref, s32[4,1,1024]{2,1,0:T(1,128)} %reshape.1183.valid_ref), custom_call_target="tpu_custom_call" | custom-call | tf_op jit(solution)/shard_map/attend/pallas_call | solution.py:284
  66.8 11.2 %collective-permute-done.4 = bf16[2,64,2048]{2,1,0:T(8,128)(2,1)} collective-permute-done((bf16[2,64,2048]{2,1,0:T(8,128)(2,1)}, bf16[2,64,2048]{2,1,0:T(8,128)(2,1)}, u32[]{:S(2)}, u32[]{:S(2)}) %collective-permute-start.4) | collective-permute-done | bytes 524320 | tf_op jit(solution)/shard_map/ppermute | solution.py:35
  103.1 9.3 %collective-permute-done.7 = bf16[2,64,2048]{2,1,0:T(8,128)(2,1)S(1)} collective-permute-done((bf16[2,64,2048]{2,1,0:T(8,128)(2,1)S(1)}, bf16[2,64,2048]{2,1,0:T(8,128)(2,1)S(1)}, u32[]{:S(2)}, u32[]{:S(2)}) %collective-permute-start.7) | collective-permute-done | bytes 524320 | tf_op jit(solution)/shard_map/ppermute | solution.py:35
  128.3 7.8 %convert_reduce_fusion.1 = (f32[1024]{0:T(1024)S(1)}, bf16[1024,1024]{1,0:T(8,128)(2,1)S(1)}, bf16[1024,1024]{1,0:T(8,128)(2,1)S(1)}) fusion(f32[1024]{0:T(1024)S(1)} %copy-done.68, bf16[1024,1024]{1,0:T(8,128)(2,1)S(1)} %copy-done.74, bf16[1024,2048]{1,0:T(8,128)(2,1)S(1)} %bitcast.286, bf16[2048,1024]{1,0:T(8,128)(2,1)S(1)} %copy-done.66), kind=kOutput, calls=%fused_computation.37 | convolution fusion | flops 4322229248 | bytes 14688256 | tf_op jit(solution)/shard_map/dot_general | solution.py:231
  136.1 5.3 convolution_convert_fusion.3
  152.4 9.7 %collective-permute-done.15 = bf16[2,64,2048]{2,1,0:T(8,128)(2,1)S(1)} collective-permute-done((bf16[2,64,2048]{2,1,0:T(8,128)(2,1)S(1)}, bf16[2,64,2048]{2,1,0:T(8,128)(2,1)S(1)}, u32[]{:S(2)}, u32[]{:S(2)}) %collective-permute-start.15) | collective-permute-done | bytes 524320 | tf_op jit(solution)/shard_map/ppermute | solution.py:35
  162.6 8.8 %collective-permute-done.13 = bf16[512,1024]{1,0:T(8,128)(2,1)S(1)} collective-permute-done((bf16[512,1024]{1,0:T(8,128)(2,1)S(1)}, bf16[512,1024]{1,0:T(8,128)(2,1)S(1)}, u32[]{:S(2)}, u32[]{:S(2)}) %collective-permute-start.13) | collective-permute-done | bytes 1048608 | tf_op jit(solution)/shard_map/ppermute | solution.py:123
  195.0 11.7 %collective-permute-done.23 = bf16[2,64,2048]{2,1,0:T(8,128)(2,1)S(1)} collective-permute-done((bf16[2,64,2048]{2,1,0:T(8,128)(2,1)S(1)}, bf16[2,64,2048]{2,1,0:T(8,128)(2,1)S(1)}, u32[]{:S(2)}, u32[]{:S(2)}) %collective-permute-start.23) | collective-permute-done | bytes 524320 | tf_op jit(solution)/shard_map/ppermute | solution.py:35
  212.8 5.0 collective-permute-start.11
  230.7 11.1 %collective-permute-done.11 = bf16[512,1024]{1,0:T(8,128)(2,1)S(1)} collective-permute-done((bf16[512,1024]{1,0:T(8,128)(2,1)S(1)}, bf16[512,1024]{1,0:T(8,128)(2,1)S(1)}, u32[]{:S(2)}, u32[]{:S(2)}) %collective-permute-start.11) | collective-permute-done | bytes 1048608 | tf_op jit(solution)/shard_map/ppermute | solution.py:123
  244.9 6.1 convolution_convert_fusion.2
  251.0 14.1 %attend_back.1 = (bf16[1024,256]{1,0:T(8,128)(2,1)}, f32[1792,256]{1,0:T(8,128)}, f32[1792,256]{1,0:T(8,128)}) custom-call(bf16[1024,256]{1,0:T(8,128)(2,1)} %fusion.54.q_ref, bf16[1792,512]{1,0:T(8,128)(2,1)} %pad_maximum_fusion.6.k_ref.v_ref, bf16[1792,512]{1,0:T(8,128)(2,1)} %pad_maximum_fusion.6.k_ref.v_ref, ...), custom_call_target="tpu_custom_call" | custom-call | tf_op jit(solution)/shard_map/attend_back/pallas_call | solution.py:299
  279.8 6.7 %collective-permute-start.29 = (bf16[512,1024]{1,0:T(8,128)(2,1)S(1)}, bf16[512,1024]{1,0:T(8,128)(2,1)S(1)}, u32[]{:S(2)}, u32[]{:S(2)}) collective-permute-start(bf16[512,1024]{1,0:T(8,128)(2,1)S(1)} %get-tuple-element.194), channel_id=1, source_target_pairs={{0,8},{8,0},{16,24},{24,16},{1,9},{9,1},{17,25},{25,17},{2,10},{10... | collective-permute-start | bytes 3145736 | tf_op jit(solution)/shard_map/ppermute | solution.py:123
  301.1 10.0 %collective-permute-done.32 = bf16[2,64,2048]{2,1,0:T(8,128)(2,1)S(1)} collective-permute-done((bf16[2,64,2048]{2,1,0:T(8,128)(2,1)S(1)}, bf16[2,64,2048]{2,1,0:T(8,128)(2,1)S(1)}, u32[]{:S(2)}, u32[]{:S(2)}) %collective-permute-start.32) | collective-permute-done | bytes 524320 | tf_op jit(solution)/shard_map/ppermute | solution.py:35
  314.3 9.4 %collective-permute-done.29 = bf16[512,1024]{1,0:T(8,128)(2,1)S(1)} collective-permute-done((bf16[512,1024]{1,0:T(8,128)(2,1)S(1)}, bf16[512,1024]{1,0:T(8,128)(2,1)S(1)}, u32[]{:S(2)}, u32[]{:S(2)}) %collective-permute-start.29) | collective-permute-done | bytes 1048608 | tf_op jit(solution)/shard_map/ppermute | solution.py:123
  335.4 10.6 %collective-permute-done.28 = bf16[512,1024]{1,0:T(8,128)(2,1)S(1)} collective-permute-done((bf16[512,1024]{1,0:T(8,128)(2,1)S(1)}, bf16[512,1024]{1,0:T(8,128)(2,1)S(1)}, u32[]{:S(2)}, u32[]{:S(2)}) %collective-permute-start.28) | collective-permute-done | bytes 1048608 | tf_op jit(solution)/shard_map/ppermute | solution.py:123
  351.6 9.6 %collective-permute-start.44 = (bf16[512,1024]{1,0:T(8,128)(2,1)S(1)}, bf16[512,1024]{1,0:T(8,128)(2,1)S(1)}, u32[]{:S(2)}, u32[]{:S(2)}) collective-permute-start(bf16[512,1024]{1,0:T(8,128)(2,1)S(1)} %get-tuple-element.198), channel_id=1, source_target_pairs={{0,8},{8,0},{16,24},{24,16},{1,9},{9,1},{17,25},{25,17},{2,10},{10... | collective-permute-start | bytes 3145736 | tf_op jit(solution)/shard_map/ppermute | solution.py:123
  377.0 8.3 %collective-permute-done.47 = bf16[2,64,2048]{2,1,0:T(8,128)(2,1)S(1)} collective-permute-done((bf16[2,64,2048]{2,1,0:T(8,128)(2,1)S(1)}, bf16[2,64,2048]{2,1,0:T(8,128)(2,1)S(1)}, u32[]{:S(2)}, u32[]{:S(2)}) %collective-permute-start.47) | collective-permute-done | bytes 524320 | tf_op jit(solution)/shard_map/ppermute | solution.py:35
  392.3 12.4 %collective-permute-start.64 = (bf16[512,1024]{1,0:T(8,128)(2,1)}, bf16[512,1024]{1,0:T(8,128)(2,1)}, u32[]{:S(2)}, u32[]{:S(2)}) collective-permute-start(bf16[512,1024]{1,0:T(8,128)(2,1)} %broadcast_select_fusion.10), channel_id=1, source_target_pairs={{0,8},{8,0},{16,24},{24,16},{1,9},{9,1},{17,25},{25,17},{2,10},{10... | collective-permute-start | bytes 3145736 | tf_op jit(solution)/shard_map/ppermute | solution.py:123
  406.5 18.5 %maximum_convert_fusion.1 = f32[1024,2048]{1,0:T(8,128)} fusion(bf16[512,1024]{1,0:T(8,128)(2,1)S(1)} %broadcast_select_fusion, bf16[512,1024]{1,0:T(8,128)(2,1)S(1)} %broadcast_select_fusion.1, bf16[512,1024]{1,0:T(8,128)(2,1)S(1)} %broadcast_select_fusion.2, bf16[512,1024]{1,0:T(8,128)(2,1)S(1)} %broadcast_select_fusion.3), kind=kLoop, calls=%fused_computation.28 | loop fusion | flops 16777216 | bytes 12582912 | tf_op jit(solution)/shard_map/concatenate | solution.py:464
  455.7 4.7 collective-permute-start.62
  469.8 10.3 %collective-permute-done.41 = bf16[2,64,2048]{2,1,0:T(8,128)(2,1)} collective-permute-done((bf16[2,64,2048]{2,1,0:T(8,128)(2,1)}, bf16[2,64,2048]{2,1,0:T(8,128)(2,1)}, u32[]{:S(2)}, u32[]{:S(2)}) %collective-permute-start.41) | collective-permute-done | bytes 524320 | tf_op jit(solution)/shard_map/ppermute | solution.py:35
  496.7 22.8 %collective-permute-start.67 = (bf16[512,1024]{1,0:T(8,128)(2,1)S(1)}, bf16[512,1024]{1,0:T(8,128)(2,1)S(1)}, u32[]{:S(2)}, u32[]{:S(2)}) collective-permute-start(bf16[512,1024]{1,0:T(8,128)(2,1)S(1)} %broadcast_select_fusion.9), channel_id=1, source_target_pairs={{0,8},{8,0},{16,24},{24,16},{1,9},{9,1},{17,25},{25,17},{2,10},{10... | collective-permute-start | bytes 3145736 | tf_op jit(solution)/shard_map/ppermute | solution.py:123
  526.0 20.2 %collective-permute-start.70 = (bf16[512,1024]{1,0:T(8,128)(2,1)S(1)}, bf16[512,1024]{1,0:T(8,128)(2,1)S(1)}, u32[]{:S(2)}, u32[]{:S(2)}) collective-permute-start(bf16[512,1024]{1,0:T(8,128)(2,1)S(1)} %broadcast_select_fusion.8), channel_id=1, source_target_pairs={{0,8},{8,0},{16,24},{24,16},{1,9},{9,1},{17,25},{25,17},{2,10},{10... | collective-permute-start | bytes 3145736 | tf_op jit(solution)/shard_map/ppermute | solution.py:123
  552.6 19.4 %collective-permute-start.69 = (bf16[512,1024]{1,0:T(8,128)(2,1)S(1)}, bf16[512,1024]{1,0:T(8,128)(2,1)S(1)}, u32[]{:S(2)}, u32[]{:S(2)}) collective-permute-start(bf16[512,1024]{1,0:T(8,128)(2,1)S(1)} %add_convert_fusion.5), channel_id=1, source_target_pairs={{0,8},{8,0},{16,24},{24,16},{1,9},{9,1},{17,25},{25,17},{2,10},{10... | collective-permute-start | bytes 3145736 | tf_op jit(solution)/shard_map/ppermute | solution.py:123
  578.3 18.8 %collective-permute-start.73 = (bf16[512,1024]{1,0:T(8,128)(2,1)S(1)}, bf16[512,1024]{1,0:T(8,128)(2,1)S(1)}, u32[]{:S(2)}, u32[]{:S(2)}) collective-permute-start(bf16[512,1024]{1,0:T(8,128)(2,1)S(1)} %add_convert_fusion.1), channel_id=1, source_target_pairs={{0,8},{8,0},{16,24},{24,16},{1,9},{9,1},{17,25},{25,17},{2,10},{10... | collective-permute-start | bytes 3145736 | tf_op jit(solution)/shard_map/ppermute | solution.py:123
  599.8 17.8 %collective-permute-start.74 = (bf16[512,1024]{1,0:T(8,128)(2,1)S(1)}, bf16[512,1024]{1,0:T(8,128)(2,1)S(1)}, u32[]{:S(2)}, u32[]{:S(2)}) collective-permute-start(bf16[512,1024]{1,0:T(8,128)(2,1)S(1)} %add_convert_fusion), channel_id=1, source_target_pairs={{0,8},{8,0},{16,24},{24,16},{1,9},{9,1},{17,25},{25,17},{2,10},{10... | collective-permute-start | bytes 3145736 | tf_op jit(solution)/shard_map/ppermute | solution.py:123
  620.1 19.4 %collective-permute-done.74 = bf16[512,1024]{1,0:T(8,128)(2,1)S(1)} collective-permute-done((bf16[512,1024]{1,0:T(8,128)(2,1)S(1)}, bf16[512,1024]{1,0:T(8,128)(2,1)S(1)}, u32[]{:S(2)}, u32[]{:S(2)}) %collective-permute-start.74) | collective-permute-done | bytes 1048608 | tf_op jit(solution)/shard_map/ppermute | solution.py:123
  (467 shorter events, 288.9 us)
Async XLA Ops:
  17.7 22.0 %collective-permute-start = (bf16[768,512]{1,0:T(8,128)(2,1)}, bf16[768,512]{1,0:T(8,128)(2,1)S(1)}, u32[]{:S(2)}, u32[]{:S(2)}) collective-permute-start(bf16[768,512]{1,0:T(8,128)(2,1)} %slice.282), channel_id=1, source_target_pairs={{0,8},{8,16},{16,24},{1,9},{9,17},{17,25},{2,10},{10,18},{18,26},{... | collective-permute-start | bytes 2359304 | tf_op jit(solution)/shard_map/ppermute | solution.py:355
  144.9 26.5 %collective-permute-start.13 = (bf16[512,1024]{1,0:T(8,128)(2,1)S(1)}, bf16[512,1024]{1,0:T(8,128)(2,1)S(1)}, u32[]{:S(2)}, u32[]{:S(2)}) collective-permute-start(bf16[512,1024]{1,0:T(8,128)(2,1)S(1)} %fusion.39), channel_id=1, source_target_pairs={{0,8},{8,0},{16,24},{24,16},{1,9},{9,1},{17,25},{25,17},{2,10},{10... | collective-permute-start | bytes 3145736 | tf_op jit(solution)/shard_map/ppermute | solution.py:123
  151.5 41.8 %collective-permute-start.12 = (bf16[512,1024]{1,0:T(8,128)(2,1)S(1)}, bf16[512,1024]{1,0:T(8,128)(2,1)S(1)}, u32[]{:S(2)}, u32[]{:S(2)}) collective-permute-start(bf16[512,1024]{1,0:T(8,128)(2,1)S(1)} %fusion.42), channel_id=1, source_target_pairs={{0,8},{8,0},{16,24},{24,16},{1,9},{9,1},{17,25},{25,17},{2,10},{10... | collective-permute-start | bytes 3145736 | tf_op jit(solution)/shard_map/ppermute | solution.py:123
  212.8 29.0 %collective-permute-start.11 = (bf16[512,1024]{1,0:T(8,128)(2,1)S(1)}, bf16[512,1024]{1,0:T(8,128)(2,1)S(1)}, u32[]{:S(2)}, u32[]{:S(2)}) collective-permute-start(bf16[512,1024]{1,0:T(8,128)(2,1)S(1)} %fusion.36), channel_id=1, source_target_pairs={{0,8},{8,0},{16,24},{24,16},{1,9},{9,1},{17,25},{25,17},{2,10},{10... | collective-permute-start | bytes 3145736 | tf_op jit(solution)/shard_map/ppermute | solution.py:123
  218.2 23.6 %collective-permute-start.22 = (bf16[512,1024]{1,0:T(8,128)(2,1)S(1)}, bf16[512,1024]{1,0:T(8,128)(2,1)S(1)}, u32[]{:S(2)}, u32[]{:S(2)}) collective-permute-start(bf16[512,1024]{1,0:T(8,128)(2,1)S(1)} %add_convert_fusion.22), channel_id=1, source_target_pairs={{0,0},{8,16},{16,8},{24,24},{1,1},{9,17},{17,9},{25,25},{2,2},{10,... | collective-permute-start | bytes 3145736 | tf_op jit(solution)/shard_map/ppermute | solution.py:123
  221.9 48.4 %collective-permute-start.26 = (bf16[512,1024]{1,0:T(8,128)(2,1)}, bf16[512,1024]{1,0:T(8,128)(2,1)}, u32[]{:S(2)}, u32[]{:S(2)}) collective-permute-start(bf16[512,1024]{1,0:T(8,128)(2,1)} %get-tuple-element.196), channel_id=1, source_target_pairs={{0,8},{8,0},{16,24},{24,16},{1,9},{9,1},{17,25},{25,17},{2,10},{10... | collective-permute-start | bytes 3145736 | tf_op jit(solution)/shard_map/ppermute | solution.py:123
  243.2 27.1 %collective-permute-start.27 = (bf16[512,1024]{1,0:T(8,128)(2,1)S(1)}, bf16[512,1024]{1,0:T(8,128)(2,1)}, u32[]{:S(2)}, u32[]{:S(2)}) collective-permute-start(bf16[512,1024]{1,0:T(8,128)(2,1)S(1)} %add_convert_fusion.21), channel_id=1, source_target_pairs={{0,0},{8,16},{16,8},{24,24},{1,1},{9,17},{17,9},{25,25},{2,2},{10,... | collective-permute-start | bytes 3145736 | tf_op jit(solution)/shard_map/ppermute | solution.py:123
  273.2 21.2 %collective-permute-start.31 = (bf16[512,2048]{1,0:T(8,128)(2,1)}, bf16[512,2048]{1,0:T(8,128)(2,1)}, u32[]{:S(2)}, u32[]{:S(2)}) collective-permute-start(bf16[512,2048]{1,0:T(8,128)(2,1)} %dynamic-slice_bitcast_fusion.1), channel_id=1, source_target_pairs={{0,1},{1,0},{2,3},{3,2},{4,5},{5,4},{6,7},{7,6},{8,9},{9,8},{10,11... | collective-permute-start | bytes 6291464 | tf_op jit(solution)/shard_map/ppermute | solution.py:35
  274.8 49.1 %collective-permute-start.35 = (bf16[768,512]{1,0:T(8,128)(2,1)S(1)}, bf16[768,512]{1,0:T(8,128)(2,1)S(1)}, u32[]{:S(2)}, u32[]{:S(2)}) collective-permute-start(bf16[768,512]{1,0:T(8,128)(2,1)S(1)} %slice.404), channel_id=1, source_target_pairs={{8,0},{16,8},{24,16},{9,1},{17,9},{25,17},{10,2},{18,10},{26,18},{... | collective-permute-start | bytes 2359304 | tf_op jit(solution)/shard_map/ppermute | solution.py:406
  279.8 44.0 %collective-permute-start.29 = (bf16[512,1024]{1,0:T(8,128)(2,1)S(1)}, bf16[512,1024]{1,0:T(8,128)(2,1)S(1)}, u32[]{:S(2)}, u32[]{:S(2)}) collective-permute-start(bf16[512,1024]{1,0:T(8,128)(2,1)S(1)} %get-tuple-element.194), channel_id=1, source_target_pairs={{0,8},{8,0},{16,24},{24,16},{1,9},{9,1},{17,25},{25,17},{2,10},{10... | collective-permute-start | bytes 3145736 | tf_op jit(solution)/shard_map/ppermute | solution.py:123
  290.6 33.2 %collective-permute-start.30 = (bf16[512,1024]{1,0:T(8,128)(2,1)S(1)}, bf16[512,1024]{1,0:T(8,128)(2,1)S(1)}, u32[]{:S(2)}, u32[]{:S(2)}) collective-permute-start(bf16[512,1024]{1,0:T(8,128)(2,1)S(1)} %add_convert_fusion.17), channel_id=1, source_target_pairs={{0,0},{8,16},{16,8},{24,24},{1,1},{9,17},{17,9},{25,25},{2,2},{10,... | collective-permute-start | bytes 3145736 | tf_op jit(solution)/shard_map/ppermute | solution.py:123
  311.1 35.0 %collective-permute-start.28 = (bf16[512,1024]{1,0:T(8,128)(2,1)S(1)}, bf16[512,1024]{1,0:T(8,128)(2,1)S(1)}, u32[]{:S(2)}, u32[]{:S(2)}) collective-permute-start(bf16[512,1024]{1,0:T(8,128)(2,1)S(1)} %get-tuple-element.200), channel_id=1, source_target_pairs={{0,8},{8,0},{16,24},{24,16},{1,9},{9,1},{17,25},{25,17},{2,10},{10... | collective-permute-start | bytes 3145736 | tf_op jit(solution)/shard_map/ppermute | solution.py:123
  351.6 36.1 %collective-permute-start.44 = (bf16[512,1024]{1,0:T(8,128)(2,1)S(1)}, bf16[512,1024]{1,0:T(8,128)(2,1)S(1)}, u32[]{:S(2)}, u32[]{:S(2)}) collective-permute-start(bf16[512,1024]{1,0:T(8,128)(2,1)S(1)} %get-tuple-element.198), channel_id=1, source_target_pairs={{0,8},{8,0},{16,24},{24,16},{1,9},{9,1},{17,25},{25,17},{2,10},{10... | collective-permute-start | bytes 3145736 | tf_op jit(solution)/shard_map/ppermute | solution.py:123
  375.3 92.1 %collective-permute-start.43 = (bf16[512,1024]{1,0:T(8,128)(2,1)}, bf16[512,1024]{1,0:T(8,128)(2,1)}, u32[]{:S(2)}, u32[]{:S(2)}) collective-permute-start(bf16[512,1024]{1,0:T(8,128)(2,1)} %get-tuple-element.202), channel_id=1, source_target_pairs={{0,8},{8,0},{16,24},{24,16},{1,9},{9,1},{17,25},{25,17},{2,10},{10... | collective-permute-start | bytes 3145736 | tf_op jit(solution)/shard_map/ppermute | solution.py:123
  388.9 36.1 %collective-permute-start.51 = (bf16[64,2048]{1,0:T(8,128)(2,1)S(1)}, bf16[64,2048]{1,0:T(8,128)(2,1)S(1)}, u32[]{:S(2)}, u32[]{:S(2)}) collective-permute-start(bf16[64,2048]{1,0:T(8,128)(2,1)S(1)} %dynamic-slice_bitcast_fusion.12), channel_id=1, source_target_pairs={{0,2},{1,3},{2,0},{3,1},{4,6},{5,7},{6,4},{7,5},{8,10},{9,11},{10,... | collective-permute-start | bytes 786440 | tf_op jit(solution)/shard_map/ppermute | solution.py:35
  389.5 35.5 %collective-permute-start.50 = (bf16[64,2048]{1,0:T(8,128)(2,1)S(1)}, bf16[64,2048]{1,0:T(8,128)(2,1)S(1)}, u32[]{:S(2)}, u32[]{:S(2)}) collective-permute-start(bf16[64,2048]{1,0:T(8,128)(2,1)S(1)} %dynamic-slice_bitcast_fusion.13), channel_id=1, source_target_pairs={{0,4},{1,5},{2,6},{3,7},{4,0},{5,1},{6,2},{7,3},{8,12},{9,13},{10,... | collective-permute-start | bytes 786440 | tf_op jit(solution)/shard_map/ppermute | solution.py:35
  392.3 101.0 %collective-permute-start.64 = (bf16[512,1024]{1,0:T(8,128)(2,1)}, bf16[512,1024]{1,0:T(8,128)(2,1)}, u32[]{:S(2)}, u32[]{:S(2)}) collective-permute-start(bf16[512,1024]{1,0:T(8,128)(2,1)} %broadcast_select_fusion.10), channel_id=1, source_target_pairs={{0,8},{8,0},{16,24},{24,16},{1,9},{9,1},{17,25},{25,17},{2,10},{10... | collective-permute-start | bytes 3145736 | tf_op jit(solution)/shard_map/ppermute | solution.py:123
  404.6 62.7 %collective-permute-start.49 = (bf16[512,1024]{1,0:T(8,128)(2,1)S(1)}, bf16[512,1024]{1,0:T(8,128)(2,1)}, u32[]{:S(2)}, u32[]{:S(2)}) collective-permute-start(bf16[512,1024]{1,0:T(8,128)(2,1)S(1)} %add_convert_fusion.12), channel_id=1, source_target_pairs={{0,0},{8,16},{16,8},{24,24},{1,1},{9,17},{17,9},{25,25},{2,2},{10,... | collective-permute-start | bytes 3145736 | tf_op jit(solution)/shard_map/ppermute | solution.py:123
  467.4 25.1 %collective-permute-start.54 = (bf16[2,64,2048]{2,1,0:T(8,128)(2,1)}, bf16[2,64,2048]{2,1,0:T(8,128)(2,1)S(1)}, u32[]{:S(2)}, u32[]{:S(2)}) collective-permute-start(bf16[2,64,2048]{2,1,0:T(8,128)(2,1)} %maximum_select_fusion.22), channel_id=1, source_target_pairs={{0,2},{1,3},{2,0},{3,1},{4,6},{5,7},{6,4},{7,5},{8,10},{9,11},{10,... | collective-permute-start | bytes 1572872 | tf_op jit(solution)/shard_map/ppermute | solution.py:35
  468.6 21.7 %collective-permute-start.55 = (bf16[2,64,2048]{2,1,0:T(8,128)(2,1)S(1)}, bf16[2,64,2048]{2,1,0:T(8,128)(2,1)S(1)}, u32[]{:S(2)}, u32[]{:S(2)}) collective-permute-start(bf16[2,64,2048]{2,1,0:T(8,128)(2,1)S(1)} %maximum_select_fusion.23), channel_id=1, source_target_pairs={{0,4},{1,5},{2,6},{3,7},{4,0},{5,1},{6,2},{7,3},{8,12},{9,13},{10,... | collective-permute-start | bytes 1572872 | tf_op jit(solution)/shard_map/ppermute | solution.py:35
  483.9 37.4 %collective-permute-start.42 = (bf16[2,2,2,64,2048]{4,3,0,2,1:T(8,128)(2,1)S(1)}, bf16[2,2,2,64,2048]{4,3,0,2,1:T(8,128)(2,1)S(1)}, u32[]{:S(2)}, u32[]{:S(2)}) collective-permute-start(bf16[2,2,2,64,2048]{4,3,0,2,1:T(8,128)(2,1)S(1)} %get-tuple-element.146), channel_id=1, source_target_pairs={{0,1},{1,0},{2,3},{3,2},{4,5},{5,4},{6,7},{7,6},{8,9},{9,8},{10,11... | collective-permute-start | bytes 6291464 | tf_op jit(solution)/shard_map/ppermute | solution.py:35
  490.3 34.0 %collective-permute-start.63 = (bf16[512,1024]{1,0:T(8,128)(2,1)S(1)}, bf16[512,1024]{1,0:T(8,128)(2,1)S(1)}, u32[]{:S(2)}, u32[]{:S(2)}) collective-permute-start(bf16[512,1024]{1,0:T(8,128)(2,1)S(1)} %broadcast_select_fusion.11), channel_id=1, source_target_pairs={{0,8},{8,0},{16,24},{24,16},{1,9},{9,1},{17,25},{25,17},{2,10},{10... | collective-permute-start | bytes 3145736 | tf_op jit(solution)/shard_map/ppermute | solution.py:123
  493.2 54.9 %collective-permute-start.56 = (bf16[2,2,2,64,2048]{4,3,0,2,1:T(8,128)(2,1)S(1)}, bf16[2,2,2,64,2048]{4,3,0,2,1:T(8,128)(2,1)S(1)}, u32[]{:S(2)}, u32[]{:S(2)}) collective-permute-start(bf16[2,2,2,64,2048]{4,3,0,2,1:T(8,128)(2,1)S(1)} %get-tuple-element.142), channel_id=1, source_target_pairs={{0,1},{1,0},{2,3},{3,2},{4,5},{5,4},{6,7},{7,6},{8,9},{9,8},{10,11... | collective-permute-start | bytes 6291464 | tf_op jit(solution)/shard_map/ppermute | solution.py:35
  495.4 29.0 %collective-permute-start.66 = (bf16[512,1024]{1,0:T(8,128)(2,1)S(1)}, bf16[512,1024]{1,0:T(8,128)(2,1)S(1)}, u32[]{:S(2)}, u32[]{:S(2)}) collective-permute-start(bf16[512,1024]{1,0:T(8,128)(2,1)S(1)} %add_convert_fusion.8), channel_id=1, source_target_pairs={{0,0},{8,16},{16,8},{24,24},{1,1},{9,17},{17,9},{25,25},{2,2},{10,... | collective-permute-start | bytes 3145736 | tf_op jit(solution)/shard_map/ppermute | solution.py:123
  496.7 54.4 %collective-permute-start.67 = (bf16[512,1024]{1,0:T(8,128)(2,1)S(1)}, bf16[512,1024]{1,0:T(8,128)(2,1)S(1)}, u32[]{:S(2)}, u32[]{:S(2)}) collective-permute-start(bf16[512,1024]{1,0:T(8,128)(2,1)S(1)} %broadcast_select_fusion.9), channel_id=1, source_target_pairs={{0,8},{8,0},{16,24},{24,16},{1,9},{9,1},{17,25},{25,17},{2,10},{10... | collective-permute-start | bytes 3145736 | tf_op jit(solution)/shard_map/ppermute | solution.py:123
  524.7 26.4 %collective-permute-start.68 = (bf16[512,1024]{1,0:T(8,128)(2,1)S(1)}, bf16[512,1024]{1,0:T(8,128)(2,1)S(1)}, u32[]{:S(2)}, u32[]{:S(2)}) collective-permute-start(bf16[512,1024]{1,0:T(8,128)(2,1)S(1)} %add_convert_fusion.7), channel_id=1, source_target_pairs={{0,0},{8,16},{16,8},{24,24},{1,1},{9,17},{17,9},{25,25},{2,2},{10,... | collective-permute-start | bytes 3145736 | tf_op jit(solution)/shard_map/ppermute | solution.py:123
  526.0 50.5 %collective-permute-start.70 = (bf16[512,1024]{1,0:T(8,128)(2,1)S(1)}, bf16[512,1024]{1,0:T(8,128)(2,1)S(1)}, u32[]{:S(2)}, u32[]{:S(2)}) collective-permute-start(bf16[512,1024]{1,0:T(8,128)(2,1)S(1)} %broadcast_select_fusion.8), channel_id=1, source_target_pairs={{0,8},{8,0},{16,24},{24,16},{1,9},{9,1},{17,25},{25,17},{2,10},{10... | collective-permute-start | bytes 3145736 | tf_op jit(solution)/shard_map/ppermute | solution.py:123
  551.4 25.1 %collective-permute-start.71 = (bf16[512,1024]{1,0:T(8,128)(2,1)S(1)}, bf16[512,1024]{1,0:T(8,128)(2,1)S(1)}, u32[]{:S(2)}, u32[]{:S(2)}) collective-permute-start(bf16[512,1024]{1,0:T(8,128)(2,1)S(1)} %add_convert_fusion.3), channel_id=1, source_target_pairs={{0,0},{8,16},{16,8},{24,24},{1,1},{9,17},{17,9},{25,25},{2,2},{10,... | collective-permute-start | bytes 3145736 | tf_op jit(solution)/shard_map/ppermute | solution.py:123
  552.6 46.8 %collective-permute-start.69 = (bf16[512,1024]{1,0:T(8,128)(2,1)S(1)}, bf16[512,1024]{1,0:T(8,128)(2,1)S(1)}, u32[]{:S(2)}, u32[]{:S(2)}) collective-permute-start(bf16[512,1024]{1,0:T(8,128)(2,1)S(1)} %add_convert_fusion.5), channel_id=1, source_target_pairs={{0,8},{8,0},{16,24},{24,16},{1,9},{9,1},{17,25},{25,17},{2,10},{10... | collective-permute-start | bytes 3145736 | tf_op jit(solution)/shard_map/ppermute | solution.py:123
  576.9 22.5 %collective-permute-start.72 = (bf16[512,1024]{1,0:T(8,128)(2,1)S(1)}, bf16[512,1024]{1,0:T(8,128)(2,1)S(1)}, u32[]{:S(2)}, u32[]{:S(2)}) collective-permute-start(bf16[512,1024]{1,0:T(8,128)(2,1)S(1)} %add_convert_fusion.2), channel_id=1, source_target_pairs={{0,0},{8,16},{16,8},{24,24},{1,1},{9,17},{17,9},{25,25},{2,2},{10,... | collective-permute-start | bytes 3145736 | tf_op jit(solution)/shard_map/ppermute | solution.py:123
  578.3 41.2 %collective-permute-start.73 = (bf16[512,1024]{1,0:T(8,128)(2,1)S(1)}, bf16[512,1024]{1,0:T(8,128)(2,1)S(1)}, u32[]{:S(2)}, u32[]{:S(2)}) collective-permute-start(bf16[512,1024]{1,0:T(8,128)(2,1)S(1)} %add_convert_fusion.1), channel_id=1, source_target_pairs={{0,8},{8,0},{16,24},{24,16},{1,9},{9,1},{17,25},{25,17},{2,10},{10... | collective-permute-start | bytes 3145736 | tf_op jit(solution)/shard_map/ppermute | solution.py:123
  599.8 39.7 %collective-permute-start.74 = (bf16[512,1024]{1,0:T(8,128)(2,1)S(1)}, bf16[512,1024]{1,0:T(8,128)(2,1)S(1)}, u32[]{:S(2)}, u32[]{:S(2)}) collective-permute-start(bf16[512,1024]{1,0:T(8,128)(2,1)S(1)} %add_convert_fusion), channel_id=1, source_target_pairs={{0,8},{8,0},{16,24},{24,16},{1,9},{9,1},{17,25},{25,17},{2,10},{10... | collective-permute-start | bytes 3145736 | tf_op jit(solution)/shard_map/ppermute | solution.py:123
  (118 other events, 1371.1 us)
where the time goes:
time: 653 us; the launch traced here: 644 us
  starting transfers between devices  207 us (32%)
  waiting for transfers between devices  183 us (28%)
  other arithmetic  113 us (17%)
  matrix products  69.8 us (11%)
  local copies, waits for them, and re-layouts  45 us (7%)
  Pallas kernels  23.9 us (4%)
    ppermute x30, starting transfers between devices, exchange(): return lax.ppermute(value, 'wide', list(moves.items()))  164 us
    ppermute x43, waiting for transfers between devices, swap(): lax.ppermute(value, 'narrow', [(i, i ^ 1 << bit) for i in range(count)])  118 us
    dot_general x23, matrix products, dot(): return lax.dot_general(a, b, (dims, ((), ())), preferred_element_type=f32)  69.8 us
    ppermute x30, waiting for transfers between devices, exchange(): return lax.ppermute(value, 'wide', list(moves.items()))  64.2 us
    ppermute x43, starting transfers between devices, swap(): lax.ppermute(value, 'narrow', [(i, i ^ 1 << bit) for i in range(count)])  36.3 us
    unnamed x152, local copies, waits for them, and re-layouts  20.2 us
    convert_element_type x35, other arithmetic, add_low(): return (a.astype(f32) + b.astype(f32)).astype(a.dtype)  19.4 us
    concatenate x1, other arithmetic, on_device(): jnp.concatenate([jnp.concatenate(done[i:i + per_row], axis=1) for i in ra...  18.5 us
  transfers between devices with their start and end apart: 75, of which 36 were waited for; matrix products, arithmetic and copies ran while one was open for 24% of the time, Pallas kernels for 2%

commit v1 on v0

--- a/solution.py
+++ b/solution.py
@@ -99,7 +99,8 @@
             parts[half] = pair(parts[half], got, b, at)
         parts = list(sync(*parts))
     value = jnp.stack(parts, axis=bits - 1)
-    value = pair(value, swap(value, 0), 0, 0)
+    got = swap(value, 0)
+    value = pair(value, got, 0, 0)
     return value.reshape(rows << bits, width)
 
 
@@ -139,13 +140,15 @@
             plan.append((e, sent, got, add))
         return plan
 
-    def whole(self, value):
+    def whole(self, value, sync):
         stream = Stream(self, 1)
         stream.feed(value)
         for slot in range(stream.slots()):
             for kind in range(2):
                 stream.start(kind, slot)
-                stream.take(kind, slot, stream.waiting(kind, slot))
+                got = stream.waiting(kind, slot)
+                if got:
+                    stream.take(kind, slot, sync(*got))
         return stream.chunks[0]
 
 
@@ -197,13 +200,13 @@
     def sync(self, *values):
         n = self.turn
         self.turn += 1
-        outer, inner = self.waiting(0, n), self.waiting(1, n - 1)
-        held = lax.optimization_barrier(outer + inner + tuple(values))
+        outer = self.waiting(0, n)
+        held = lax.optimization_barrier(outer + tuple(values))
         self.take(0, n, held[: len(outer)])
-        self.take(1, n - 1, held[len(outer) : len(outer) + len(inner)])
         self.start(1, n)
+        self.take(1, n - 1, self.waiting(1, n - 1))
         self.start(0, n + 2)
-        return held[len(outer) + len(inner) :]
+        return held[len(outer) :]
 
     def finish(self):
         while self.turn < self.slots():
@@ -304,6 +307,27 @@
         out_shape=[jax.ShapeDtypeStruct((rows, width), bf16), wide_shape, wide_shape],
         name="attend_back",
     )(query, keys_vals, keys_vals, out, pos, valid)
+
+
+def tile_kernel(*refs):
+    *parts, out_ref = refs
+    for at, part in enumerate(parts):
+
+        @pl.when(pl.program_id(0) == at)
+        def _():
+            out_ref[...] = part[...].astype(f32)
+
+
+def tiled(parts, per_row):
+    rows, cols = parts[0].shape
+    return pl.pallas_call(
+        tile_kernel,
+        grid=(len(parts),),
+        in_specs=[pl.BlockSpec((rows, cols), lambda i: (0, 0)) for _ in parts],
+        out_specs=pl.BlockSpec((rows, cols), lambda i: (i // per_row, i % per_row)),
+        out_shape=jax.ShapeDtypeStruct((len(parts) // per_row * rows, per_row * cols), f32),
+        name="tiled",
+    )(*parts)
 
 
 def on_device(
@@ -405,8 +429,8 @@
     grad_kv = jnp.concatenate([grad_keys, grad_vals], axis=1)
     got = lax.ppermute(grad_kv[:MAX_DOCUMENT].astype(bf16), "wide", behind)
     own = grad_kv[MAX_DOCUMENT:]
+    own, active = bulk.sync(own, active)
     mlp_part = dot(active, w_down, ((1,), (0,))).astype(bf16)
-    own, mlp_part = bulk.sync(own, mlp_part)
     held = [own]
 
     def sync_own(*values):
@@ -431,12 +455,12 @@
     grad_b_qv = [grad_b_qv[i * local_width : (i + 1) * local_width] for i in (0, 2)]
     back_part = dot(grad_mixed, w_flat, ((1,), (1,))).astype(bf16)
     output = gather_rows((after_attn + b_down + mlp_total).astype(bf16))
-    grad_norm_one = reduce_rows(back_part, at_calls(bulk.sync, 1)).astype(f32)
+    grad_norm_one = reduce_rows(back_part, at_calls(bulk.sync, 0, 2)).astype(f32)
     raw_rows, inv_rows = norm_stats(inputs_rows)
     grad_resid, grad_ln1_gain, grad_ln1_bias = norm_back(
         grad_norm_one, raw_rows, inv_rows, ln1_gain
     )
-    grad_input = gather_rows((grad_mid + grad_resid).astype(bf16), at_calls(bulk.sync, 0))
+    grad_input = gather_rows((grad_mid + grad_resid).astype(bf16), at_calls(bulk.sync, 0, 1))
 
     sums = narrow_total(
         jnp.stack(
@@ -451,7 +475,7 @@
         )
     )
     sums = jnp.concatenate([sums.reshape(-1), grad_b_up] + grad_b_qv)
-    sums = line.whole(sums.reshape(-1, 128)).reshape(-1)
+    sums = line.whole(sums.reshape(-1, 128), bulk.sync).reshape(-1)
     bulk.finish()
     grad_ln2_gain, grad_ln2_bias, grad_b_out, grad_b_down, grad_ln1_gain, grad_ln1_bias = sums[
         : 6 * width
@@ -461,10 +485,8 @@
 
     done = [value.astype(f32) for value in bulk.chunks]
     per_row = width // hidden
-    grad_w_down = jnp.concatenate(
-        [jnp.concatenate(done[i : i + per_row], axis=1) for i in range(0, 4, per_row)]
-    )
-    grad_w_up = jnp.concatenate(done[4:8])
+    grad_w_down = tiled(bulk.chunks[:4], per_row)
+    grad_w_up = tiled(bulk.chunks[4:8], 1)
     grad_w_out = jnp.concatenate(
         [done[8][i * local_width : (i + 1) * local_width] for i in range(per_row)], axis=1
     )

time: 653 us -> 667 us (1.021)
  waiting for transfers between devices: 183 us -> 211 us
  starting transfers between devices: 207 us -> 182 us
  Pallas kernels: 23.9 us -> 35.4 us
    ppermute x30, waiting for transfers between devices: 64.2 us -> 94.4 us  [exchange(): return lax.ppermute(value, 'wide', list(moves.items()))]
    ppermute x30, starting transfers between devices: 164 us -> 140 us  [exchange(): return lax.ppermute(value, 'wide', list(moves.items()))]
    concatenate x2 -> x0, other arithmetic: 22.4 us -> none  [the longest x1 18.5 us: on_device(): jnp.concatenate([jnp.concatenate(done[i:i + per_row], axis=1) for i in ra...]
    pallas_call x0 -> x2, Pallas kernels: none -> 11.6 us  [tiled(): pl.pallas_call(tile_kernel, grid=(len(parts),), in_specs=[pl.BlockSpec((r...]
    select_n x9, other arithmetic: 11.3 us -> 21.9 us  [take(): new = jnp.where(self.line.depth == e, new, held)]
    select_n x18 -> x19, other arithmetic: 14.1 us -> 16.4 us  [pair(): jnp.where(narrow_bit(bit) == 0, jnp.stack([value, other], axis=dim), jnp....]
    unnamed x152 -> x150, local copies, waits for them, and re-layouts: 20.2 us -> 18.9 us
  transfers between devices with their start and end apart: 75 -> 75, of which waited for: 36 -> 37; matrix products, arithmetic and copies ran while one was open for 24% -> 24% of each run, Pallas kernels for 2% -> 4%
where the time goes in v1:
time: 667 us; the launch traced here: 657 us
  waiting for transfers between devices  211 us (32%)
  starting transfers between devices  182 us (27%)
  other arithmetic  116 us (17%)
  matrix products  67.2 us (10%)
  local copies, waits for them, and re-layouts  42.4 us (6%)
  Pallas kernels  35.4 us (5%)
    ppermute x30, starting transfers between devices, exchange(): return lax.ppermute(value, 'wide', list(moves.items()))  140 us
    ppermute x43, waiting for transfers between devices, swap(): lax.ppermute(value, 'narrow', [(i, i ^ 1 << bit) for i in range(count)])  116 us
    ppermute x30, waiting for transfers between devices, exchange(): return lax.ppermute(value, 'wide', list(moves.items()))  94.4 us
    dot_general x23, matrix products, dot(): return lax.dot_general(a, b, (dims, ((), ())), preferred_element_type=f32)  67.2 us
    ppermute x43, starting transfers between devices, swap(): lax.ppermute(value, 'narrow', [(i, i ^ 1 << bit) for i in range(count)])  35.8 us
    convert_element_type x35, other arithmetic, add_low(): return (a.astype(f32) + b.astype(f32)).astype(a.dtype)  25.5 us
    select_n x9, other arithmetic, take(): new = jnp.where(self.line.depth == e, new, held)  21.9 us
    unnamed x150, local copies, waits for them, and re-layouts  18.9 us
  transfers between devices with their start and end apart: 75, of which 37 were waited for; matrix products, arithmetic and copies ran while one was open for 24% of the time, Pallas kernels for 4%

profile of v1, /device:TPU:0, one launch (start us, length us, event | category | flops | bytes accessed | tf_op | source)
XLA Modules:
  0.0 656.7 jit_solution(12462206900750286833)
XLA Ops:
  29.8 9.3 %convolution_convert_fusion.4 = bf16[1024,1024]{1,0:T(8,128)(2,1)} fusion(bf16[1024,2048]{1,0:T(8,128)(2,1)} %param.32, bf16[1024,2048]{1,0:T(8,128)(2,1)} %param.28), kind=kOutput, calls=%fused_computation.85 | convolution fusion | flops 4296015872 | bytes 10485760 | tf_op jit(solution)/shard_map/dot_general | solution.py:234
  41.1 9.7 %attend.1 = bf16[1024,256]{1,0:T(8,128)(2,1)} custom-call(bf16[1024,256]{1,0:T(8,128)(2,1)} %fusion.54.q_ref, bf16[1792,512]{1,0:T(8,128)(2,1)} %pad_maximum_fusion.6.k_ref.v_ref, bf16[1792,512]{1,0:T(8,128)(2,1)} %pad_maximum_fusion.6.k_ref.v_ref, s32[1024,1]{1,0:T(8,128)} %copy.55.pos_ref, s32[4,1,1024]{2,1,0:T(1,128)} %reshape.1065.valid_ref), custom_call_target="tpu_custom_call" | custom-call | tf_op jit(solution)/shard_map/attend/pallas_call | solution.py:287
  66.7 11.2 %collective-permute-done.4 = bf16[2,64,2048]{2,1,0:T(8,128)(2,1)} collective-permute-done((bf16[2,64,2048]{2,1,0:T(8,128)(2,1)}, bf16[2,64,2048]{2,1,0:T(8,128)(2,1)}, u32[]{:S(2)}, u32[]{:S(2)}) %collective-permute-start.4) | collective-permute-done | bytes 524320 | tf_op jit(solution)/shard_map/ppermute | solution.py:35
  103.1 9.3 %collective-permute-done.7 = bf16[2,64,2048]{2,1,0:T(8,128)(2,1)S(1)} collective-permute-done((bf16[2,64,2048]{2,1,0:T(8,128)(2,1)S(1)}, bf16[2,64,2048]{2,1,0:T(8,128)(2,1)S(1)}, u32[]{:S(2)}, u32[]{:S(2)}) %collective-permute-start.7) | collective-permute-done | bytes 524320 | tf_op jit(solution)/shard_map/ppermute | solution.py:35
  128.1 7.8 %convert_reduce_fusion.1 = (f32[1024]{0:T(1024)S(1)}, bf16[1024,1024]{1,0:T(8,128)(2,1)S(1)}, bf16[1024,1024]{1,0:T(8,128)(2,1)S(1)}) fusion(f32[1024]{0:T(1024)S(1)} %copy-done.67, bf16[1024,1024]{1,0:T(8,128)(2,1)S(1)} %copy-done.73, bf16[1024,2048]{1,0:T(8,128)(2,1)S(1)} %bitcast.291, bf16[2048,1024]{1,0:T(8,128)(2,1)S(1)} %copy-done.65), kind=kOutput, calls=%fused_computation.35 | convolution fusion | flops 4322229248 | bytes 14688256 | tf_op jit(solution)/shard_map/dot_general | solution.py:234
  136.0 5.0 convolution_convert_fusion.3
  152.7 7.7 %collective-permute-done.15 = bf16[2,64,2048]{2,1,0:T(8,128)(2,1)S(1)} collective-permute-done((bf16[2,64,2048]{2,1,0:T(8,128)(2,1)S(1)}, bf16[2,64,2048]{2,1,0:T(8,128)(2,1)S(1)}, u32[]{:S(2)}, u32[]{:S(2)}) %collective-permute-start.15) | collective-permute-done | bytes 524320 | tf_op jit(solution)/shard_map/ppermute | solution.py:35
  160.6 5.3 collective-permute-done.16
  166.0 9.5 %collective-permute-done.13 = bf16[512,1024]{1,0:T(8,128)(2,1)S(1)} collective-permute-done((bf16[512,1024]{1,0:T(8,128)(2,1)S(1)}, bf16[512,1024]{1,0:T(8,128)(2,1)S(1)}, u32[]{:S(2)}, u32[]{:S(2)}) %collective-permute-start.13) | collective-permute-done | bytes 1048608 | tf_op jit(solution)/shard_map/ppermute | solution.py:124
  203.9 10.3 %collective-permute-done.21 = bf16[2,64,2048]{2,1,0:T(8,128)(2,1)S(1)} collective-permute-done((bf16[2,64,2048]{2,1,0:T(8,128)(2,1)S(1)}, bf16[2,64,2048]{2,1,0:T(8,128)(2,1)S(1)}, u32[]{:S(2)}, u32[]{:S(2)}) %collective-permute-start.21) | collective-permute-done | bytes 524320 | tf_op jit(solution)/shard_map/ppermute | solution.py:35
  219.2 9.5 %collective-permute-start.28 = (bf16[512,1024]{1,0:T(8,128)(2,1)}, bf16[512,1024]{1,0:T(8,128)(2,1)}, u32[]{:S(2)}, u32[]{:S(2)}) collective-permute-start(bf16[512,1024]{1,0:T(8,128)(2,1)} %add_convert_fusion.19), channel_id=1, source_target_pairs={{0,0},{8,16},{16,8},{24,24},{1,1},{9,17},{17,9},{25,25},{2,2},{10,... | collective-permute-start | bytes 3145736 | tf_op jit(solution)/shard_map/ppermute | solution.py:124
  238.9 13.8 %collective-permute-start.29 = (bf16[512,1024]{1,0:T(8,128)(2,1)}, bf16[512,1024]{1,0:T(8,128)(2,1)}, u32[]{:S(2)}, u32[]{:S(2)}) collective-permute-start(bf16[512,1024]{1,0:T(8,128)(2,1)} %get-tuple-element.184), channel_id=1, source_target_pairs={{0,8},{8,0},{16,24},{24,16},{1,9},{9,1},{17,25},{25,17},{2,10},{10... | collective-permute-start | bytes 3145736 | tf_op jit(solution)/shard_map/ppermute | solution.py:124
  258.4 14.1 %attend_back.1 = (bf16[1024,256]{1,0:T(8,128)(2,1)}, f32[1792,256]{1,0:T(8,128)}, f32[1792,256]{1,0:T(8,128)}) custom-call(bf16[1024,256]{1,0:T(8,128)(2,1)} %fusion.54.q_ref, bf16[1792,512]{1,0:T(8,128)(2,1)} %pad_maximum_fusion.6.k_ref.v_ref, bf16[1792,512]{1,0:T(8,128)(2,1)} %pad_maximum_fusion.6.k_ref.v_ref, ...), custom_call_target="tpu_custom_call" | custom-call | tf_op jit(solution)/shard_map/attend_back/pallas_call | solution.py:302
  275.0 5.2 collective-permute-done.29
  303.5 19.8 %collective-permute-start.42 = (bf16[512,1024]{1,0:T(8,128)(2,1)S(1)}, bf16[512,1024]{1,0:T(8,128)(2,1)S(1)}, u32[]{:S(2)}, u32[]{:S(2)}) collective-permute-start(bf16[512,1024]{1,0:T(8,128)(2,1)S(1)} %get-tuple-element.188), channel_id=1, source_target_pairs={{0,8},{8,0},{16,24},{24,16},{1,9},{9,1},{17,25},{25,17},{2,10},{10... | collective-permute-start | bytes 3145736 | tf_op jit(solution)/shard_map/ppermute | solution.py:124
  327.7 7.9 %collective-permute-done.31 = bf16[2,64,2048]{2,1,0:T(8,128)(2,1)S(1)} collective-permute-done((bf16[2,64,2048]{2,1,0:T(8,128)(2,1)S(1)}, bf16[2,64,2048]{2,1,0:T(8,128)(2,1)S(1)}, u32[]{:S(2)}, u32[]{:S(2)}) %collective-permute-start.31) | collective-permute-done | bytes 524320 | tf_op jit(solution)/shard_map/ppermute | solution.py:35
  335.6 10.6 %collective-permute-start.25 = (bf16[512,1024]{1,0:T(8,128)(2,1)S(1)}, bf16[512,1024]{1,0:T(8,128)(2,1)S(1)}, u32[]{:S(2)}, u32[]{:S(2)}) collective-permute-start(bf16[512,1024]{1,0:T(8,128)(2,1)S(1)} %get-tuple-element.190), channel_id=1, source_target_pairs={{0,8},{8,0},{16,24},{24,16},{1,9},{9,1},{17,25},{25,17},{2,10},{10... | collective-permute-start | bytes 3145736 | tf_op jit(solution)/shard_map/ppermute | solution.py:124
  362.6 13.6 %collective-permute-done.25 = bf16[512,1024]{1,0:T(8,128)(2,1)S(1)} collective-permute-done((bf16[512,1024]{1,0:T(8,128)(2,1)S(1)}, bf16[512,1024]{1,0:T(8,128)(2,1)S(1)}, u32[]{:S(2)}, u32[]{:S(2)}) %collective-permute-start.25) | collective-permute-done | bytes 1048608 | tf_op jit(solution)/shard_map/ppermute | solution.py:124
  389.7 7.8 %collective-permute-start.49 = (bf16[512,1024]{1,0:T(8,128)(2,1)}, bf16[512,1024]{1,0:T(8,128)(2,1)}, u32[]{:S(2)}, u32[]{:S(2)}) collective-permute-start(bf16[512,1024]{1,0:T(8,128)(2,1)} %get-tuple-element.186), channel_id=1, source_target_pairs={{0,8},{8,0},{16,24},{24,16},{1,9},{9,1},{17,25},{25,17},{2,10},{10... | collective-permute-start | bytes 3145736 | tf_op jit(solution)/shard_map/ppermute | solution.py:124
  399.1 17.7 %collective-permute-start.47 = (bf16[512,1024]{1,0:T(8,128)(2,1)}, bf16[512,1024]{1,0:T(8,128)(2,1)}, u32[]{:S(2)}, u32[]{:S(2)}) collective-permute-start(bf16[512,1024]{1,0:T(8,128)(2,1)} %broadcast_select_fusion.11), channel_id=1, source_target_pairs={{0,8},{8,0},{16,24},{24,16},{1,9},{9,1},{17,25},{25,17},{2,10},{10... | collective-permute-start | bytes 3145736 | tf_op jit(solution)/shard_map/ppermute | solution.py:124
  426.3 5.8 tiled.3
  462.8 9.5 %collective-permute-start.64 = (bf16[512,1024]{1,0:T(8,128)(2,1)}, bf16[512,1024]{1,0:T(8,128)(2,1)}, u32[]{:S(2)}, u32[]{:S(2)}) collective-permute-start(bf16[512,1024]{1,0:T(8,128)(2,1)} %add_convert_fusion.7), channel_id=1, source_target_pairs={{0,0},{8,16},{16,8},{24,24},{1,1},{9,17},{17,9},{25,25},{2,2},{10,... | collective-permute-start | bytes 3145736 | tf_op jit(solution)/shard_map/ppermute | solution.py:124
  490.2 6.0 collective-permute-done.39
  497.3 6.1 collective-permute-done.37
  513.7 14.1 %collective-permute-start.68 = (bf16[512,1024]{1,0:T(8,128)(2,1)}, bf16[512,1024]{1,0:T(8,128)(2,1)}, u32[]{:S(2)}, u32[]{:S(2)}) collective-permute-start(bf16[512,1024]{1,0:T(8,128)(2,1)} %broadcast_select_fusion.8), channel_id=1, source_target_pairs={{0,8},{8,0},{16,24},{24,16},{1,9},{9,1},{17,25},{25,17},{2,10},{10... | collective-permute-start | bytes 3145736 | tf_op jit(solution)/shard_map/ppermute | solution.py:124
  527.9 5.0 collective-permute-done.45
  540.3 15.1 %collective-permute-done.65 = bf16[512,1024]{1,0:T(8,128)(2,1)S(1)} collective-permute-done((bf16[512,1024]{1,0:T(8,128)(2,1)S(1)}, bf16[512,1024]{1,0:T(8,128)(2,1)S(1)}, u32[]{:S(2)}, u32[]{:S(2)}) %collective-permute-start.65) | collective-permute-done | bytes 1048608 | tf_op jit(solution)/shard_map/ppermute | solution.py:124
  559.7 5.8 tiled.2
  566.4 8.1 %collective-permute-done.68 = bf16[512,1024]{1,0:T(8,128)(2,1)} collective-permute-done((bf16[512,1024]{1,0:T(8,128)(2,1)}, bf16[512,1024]{1,0:T(8,128)(2,1)}, u32[]{:S(2)}, u32[]{:S(2)}) %collective-permute-start.68) | collective-permute-done | bytes 1048608 | tf_op jit(solution)/shard_map/ppermute | solution.py:124
  599.7 11.6 %collective-permute-start.74 = (bf16[512,1024]{1,0:T(8,128)(2,1)S(1)}, bf16[512,1024]{1,0:T(8,128)(2,1)}, u32[]{:S(2)}, u32[]{:S(2)}) collective-permute-start(bf16[512,1024]{1,0:T(8,128)(2,1)S(1)} %add_convert_fusion), channel_id=1, source_target_pairs={{0,8},{8,0},{16,24},{24,16},{1,9},{9,1},{17,25},{25,17},{2,10},{10... | collective-permute-start | bytes 3145736 | tf_op jit(solution)/shard_map/ppermute | solution.py:124
  615.6 18.0 %collective-permute-done.72 = bf16[512,1024]{1,0:T(8,128)(2,1)} collective-permute-done((bf16[512,1024]{1,0:T(8,128)(2,1)S(1)}, bf16[512,1024]{1,0:T(8,128)(2,1)}, u32[]{:S(2)}, u32[]{:S(2)}) %collective-permute-start.72) | collective-permute-done | bytes 1048608 | tf_op jit(solution)/shard_map/ppermute | solution.py:124
  635.1 16.3 %collective-permute-done.74 = bf16[512,1024]{1,0:T(8,128)(2,1)} collective-permute-done((bf16[512,1024]{1,0:T(8,128)(2,1)S(1)}, bf16[512,1024]{1,0:T(8,128)(2,1)}, u32[]{:S(2)}, u32[]{:S(2)}) %collective-permute-start.74) | collective-permute-done | bytes 1048608 | tf_op jit(solution)/shard_map/ppermute | solution.py:124
  (466 shorter events, 327.3 us)
Async XLA Ops:
  149.7 25.9 %collective-permute-start.13 = (bf16[512,1024]{1,0:T(8,128)(2,1)S(1)}, bf16[512,1024]{1,0:T(8,128)(2,1)S(1)}, u32[]{:S(2)}, u32[]{:S(2)}) collective-permute-start(bf16[512,1024]{1,0:T(8,128)(2,1)S(1)} %fusion.39), channel_id=1, source_target_pairs={{0,8},{8,0},{16,24},{24,16},{1,9},{9,1},{17,25},{25,17},{2,10},{10... | collective-permute-start | bytes 3145736 | tf_op jit(solution)/shard_map/ppermute | solution.py:124
  177.5 24.4 %collective-permute-start.12 = (bf16[512,1024]{1,0:T(8,128)(2,1)S(1)}, bf16[512,1024]{1,0:T(8,128)(2,1)S(1)}, u32[]{:S(2)}, u32[]{:S(2)}) collective-permute-start(bf16[512,1024]{1,0:T(8,128)(2,1)S(1)} %fusion.42), channel_id=1, source_target_pairs={{0,8},{8,0},{16,24},{24,16},{1,9},{9,1},{17,25},{25,17},{2,10},{10... | collective-permute-start | bytes 3145736 | tf_op jit(solution)/shard_map/ppermute | solution.py:124
  217.8 35.0 %collective-permute-start.23 = (bf16[2,2,2,64,2048]{4,3,1,2,0:T(8,128)(2,1)}, bf16[2,2,2,64,2048]{4,3,1,2,0:T(8,128)(2,1)}, u32[]{:S(2)}, u32[]{:S(2)}) collective-permute-start(bf16[2,2,2,64,2048]{4,3,1,2,0:T(8,128)(2,1)} %get-tuple-element.138), channel_id=1, source_target_pairs={{0,1},{1,0},{2,3},{3,2},{4,5},{5,4},{6,7},{7,6},{8,9},{9,8},{10,11... | collective-permute-start | bytes 6291464 | tf_op jit(solution)/shard_map/ppermute | solution.py:35
  232.0 26.4 %collective-permute-start.11 = (bf16[512,1024]{1,0:T(8,128)(2,1)S(1)}, bf16[512,1024]{1,0:T(8,128)(2,1)}, u32[]{:S(2)}, u32[]{:S(2)}) collective-permute-start(bf16[512,1024]{1,0:T(8,128)(2,1)S(1)} %fusion.36), channel_id=1, source_target_pairs={{0,8},{8,0},{16,24},{24,16},{1,9},{9,1},{17,25},{25,17},{2,10},{10... | collective-permute-start | bytes 3145736 | tf_op jit(solution)/shard_map/ppermute | solution.py:124
  232.5 52.8 %collective-permute-start.26 = (bf16[512,1024]{1,0:T(8,128)(2,1)S(1)}, bf16[512,1024]{1,0:T(8,128)(2,1)}, u32[]{:S(2)}, u32[]{:S(2)}) collective-permute-start(bf16[512,1024]{1,0:T(8,128)(2,1)S(1)} %add_convert_fusion.21), channel_id=1, source_target_pairs={{0,0},{8,16},{16,8},{24,24},{1,1},{9,17},{17,9},{25,25},{2,2},{10,... | collective-permute-start | bytes 3145736 | tf_op jit(solution)/shard_map/ppermute | solution.py:124
  238.9 41.3 %collective-permute-start.29 = (bf16[512,1024]{1,0:T(8,128)(2,1)}, bf16[512,1024]{1,0:T(8,128)(2,1)}, u32[]{:S(2)}, u32[]{:S(2)}) collective-permute-start(bf16[512,1024]{1,0:T(8,128)(2,1)} %get-tuple-element.184), channel_id=1, source_target_pairs={{0,8},{8,0},{16,24},{24,16},{1,9},{9,1},{17,25},{25,17},{2,10},{10... | collective-permute-start | bytes 3145736 | tf_op jit(solution)/shard_map/ppermute | solution.py:124
  285.2 38.1 %collective-permute-start.30 = (bf16[512,2048]{1,0:T(8,128)(2,1)S(1)}, bf16[512,2048]{1,0:T(8,128)(2,1)S(1)}, u32[]{:S(2)}, u32[]{:S(2)}) collective-permute-start(bf16[512,2048]{1,0:T(8,128)(2,1)S(1)} %dynamic-slice_bitcast_fusion.1), channel_id=1, source_target_pairs={{0,1},{1,0},{2,3},{3,2},{4,5},{5,4},{6,7},{7,6},{8,9},{9,8},{10,11... | collective-permute-start | bytes 6291464 | tf_op jit(solution)/shard_map/ppermute | solution.py:35
  289.7 56.9 %collective-permute-start.27 = (bf16[512,1024]{1,0:T(8,128)(2,1)S(1)}, bf16[512,1024]{1,0:T(8,128)(2,1)S(1)}, u32[]{:S(2)}, u32[]{:S(2)}) collective-permute-start(bf16[512,1024]{1,0:T(8,128)(2,1)S(1)} %get-tuple-element.182), channel_id=1, source_target_pairs={{0,8},{8,0},{16,24},{24,16},{1,9},{9,1},{17,25},{25,17},{2,10},{10... | collective-permute-start | bytes 3145736 | tf_op jit(solution)/shard_map/ppermute | solution.py:124
  294.7 30.4 %collective-permute-start.24 = (bf16[512,1024]{1,0:T(8,128)(2,1)S(1)}, bf16[512,1024]{1,0:T(8,128)(2,1)S(1)}, u32[]{:S(2)}, u32[]{:S(2)}) collective-permute-start(bf16[512,1024]{1,0:T(8,128)(2,1)S(1)} %add_convert_fusion.23), channel_id=1, source_target_pairs={{0,0},{8,16},{16,8},{24,24},{1,1},{9,17},{17,9},{25,25},{2,2},{10,... | collective-permute-start | bytes 3145736 | tf_op jit(solution)/shard_map/ppermute | solution.py:124
  295.5 51.2 %collective-permute-start.33 = (bf16[768,512]{1,0:T(8,128)(2,1)S(1)}, bf16[768,512]{1,0:T(8,128)(2,1)S(1)}, u32[]{:S(2)}, u32[]{:S(2)}) collective-permute-start(bf16[768,512]{1,0:T(8,128)(2,1)S(1)} %slice.404), channel_id=1, source_target_pairs={{8,0},{16,8},{24,16},{9,1},{17,9},{25,17},{10,2},{18,10},{26,18},{... | collective-permute-start | bytes 2359304 | tf_op jit(solution)/shard_map/ppermute | solution.py:430
  303.5 114.3 %collective-permute-start.42 = (bf16[512,1024]{1,0:T(8,128)(2,1)S(1)}, bf16[512,1024]{1,0:T(8,128)(2,1)S(1)}, u32[]{:S(2)}, u32[]{:S(2)}) collective-permute-start(bf16[512,1024]{1,0:T(8,128)(2,1)S(1)} %get-tuple-element.188), channel_id=1, source_target_pairs={{0,8},{8,0},{16,24},{24,16},{1,9},{9,1},{17,25},{25,17},{2,10},{10... | collective-permute-start | bytes 3145736 | tf_op jit(solution)/shard_map/ppermute | solution.py:124
  335.6 40.6 %collective-permute-start.25 = (bf16[512,1024]{1,0:T(8,128)(2,1)S(1)}, bf16[512,1024]{1,0:T(8,128)(2,1)S(1)}, u32[]{:S(2)}, u32[]{:S(2)}) collective-permute-start(bf16[512,1024]{1,0:T(8,128)(2,1)S(1)} %get-tuple-element.190), channel_id=1, source_target_pairs={{0,8},{8,0},{16,24},{24,16},{1,9},{9,1},{17,25},{25,17},{2,10},{10... | collective-permute-start | bytes 3145736 | tf_op jit(solution)/shard_map/ppermute | solution.py:124
  356.4 30.6 %collective-permute-start.48 = (bf16[512,1024]{1,0:T(8,128)(2,1)S(1)}, bf16[512,1024]{1,0:T(8,128)(2,1)S(1)}, u32[]{:S(2)}, u32[]{:S(2)}) collective-permute-start(bf16[512,1024]{1,0:T(8,128)(2,1)S(1)} %add_convert_fusion.11), channel_id=1, source_target_pairs={{0,0},{8,16},{16,8},{24,24},{1,1},{9,17},{17,9},{25,25},{2,2},{10,... | collective-permute-start | bytes 3145736 | tf_op jit(solution)/shard_map/ppermute | solution.py:124
  380.2 36.7 %collective-permute-start.43 = (bf16[512,2048]{1,0:T(8,128)(2,1)S(1)}, bf16[512,2048]{1,0:T(8,128)(2,1)S(1)}, u32[]{:S(2)}, u32[]{:S(2)}) collective-permute-start(bf16[512,2048]{1,0:T(8,128)(2,1)S(1)} %dynamic-slice_bitcast_fusion), channel_id=1, source_target_pairs={{0,1},{1,0},{2,3},{3,2},{4,5},{5,4},{6,7},{7,6},{8,9},{9,8},{10,11... | collective-permute-start | bytes 6291464 | tf_op jit(solution)/shard_map/ppermute | solution.py:35
  389.7 52.1 %collective-permute-start.49 = (bf16[512,1024]{1,0:T(8,128)(2,1)}, bf16[512,1024]{1,0:T(8,128)(2,1)}, u32[]{:S(2)}, u32[]{:S(2)}) collective-permute-start(bf16[512,1024]{1,0:T(8,128)(2,1)} %get-tuple-element.186), channel_id=1, source_target_pairs={{0,8},{8,0},{16,24},{24,16},{1,9},{9,1},{17,25},{25,17},{2,10},{10... | collective-permute-start | bytes 3145736 | tf_op jit(solution)/shard_map/ppermute | solution.py:124
  399.1 77.7 %collective-permute-start.47 = (bf16[512,1024]{1,0:T(8,128)(2,1)}, bf16[512,1024]{1,0:T(8,128)(2,1)}, u32[]{:S(2)}, u32[]{:S(2)}) collective-permute-start(bf16[512,1024]{1,0:T(8,128)(2,1)} %broadcast_select_fusion.11), channel_id=1, source_target_pairs={{0,8},{8,0},{16,24},{24,16},{1,9},{9,1},{17,25},{25,17},{2,10},{10... | collective-permute-start | bytes 3145736 | tf_op jit(solution)/shard_map/ppermute | solution.py:124
  422.6 61.5 %collective-permute-start.44 = (bf16[512,1024]{1,0:T(8,128)(2,1)S(1)}, bf16[512,1024]{1,0:T(8,128)(2,1)}, u32[]{:S(2)}, u32[]{:S(2)}) collective-permute-start(bf16[512,1024]{1,0:T(8,128)(2,1)S(1)} %add_convert_fusion.15), channel_id=1, source_target_pairs={{0,0},{8,16},{16,8},{24,24},{1,1},{9,17},{17,9},{25,25},{2,2},{10,... | collective-permute-start | bytes 3145736 | tf_op jit(solution)/shard_map/ppermute | solution.py:124
  449.3 25.4 %collective-permute-start.54 = (bf16[64,2048]{1,0:T(8,128)(2,1)}, bf16[64,2048]{1,0:T(8,128)(2,1)}, u32[]{:S(2)}, u32[]{:S(2)}) collective-permute-start(bf16[64,2048]{1,0:T(8,128)(2,1)} %get-tuple-element.151), channel_id=1, source_target_pairs={{0,4},{1,5},{2,6},{3,7},{4,0},{5,1},{6,2},{7,3},{8,12},{9,13},{10,... | collective-permute-start | bytes 786440 | tf_op jit(solution)/shard_map/ppermute | solution.py:35
  462.8 45.4 %collective-permute-start.64 = (bf16[512,1024]{1,0:T(8,128)(2,1)}, bf16[512,1024]{1,0:T(8,128)(2,1)}, u32[]{:S(2)}, u32[]{:S(2)}) collective-permute-start(bf16[512,1024]{1,0:T(8,128)(2,1)} %add_convert_fusion.7), channel_id=1, source_target_pairs={{0,0},{8,16},{16,8},{24,24},{1,1},{9,17},{17,9},{25,25},{2,2},{10,... | collective-permute-start | bytes 3145736 | tf_op jit(solution)/shard_map/ppermute | solution.py:124
  476.8 63.5 %collective-permute-start.66 = (f32[108,128]{1,0:T(8,128)S(1)}, f32[108,128]{1,0:T(8,128)S(1)}, u32[]{:S(2)}, u32[]{:S(2)}) collective-permute-start(f32[108,128]{1,0:T(8,128)S(1)} %maximum_bitcast_fusion.3), channel_id=1, source_target_pairs={{0,8},{8,0},{16,24},{24,16},{1,9},{9,1},{17,25},{25,17},{2,10},{10... | collective-permute-start | bytes 165896 | tf_op jit(solution)/shard_map/ppermute | solution.py:124
  480.1 26.8 %collective-permute-start.56 = (bf16[2,64,2048]{2,1,0:T(8,128)(2,1)S(1)}, bf16[2,64,2048]{2,1,0:T(8,128)(2,1)S(1)}, u32[]{:S(2)}, u32[]{:S(2)}) collective-permute-start(bf16[2,64,2048]{2,1,0:T(8,128)(2,1)S(1)} %maximum_select_fusion.22), channel_id=1, source_target_pairs={{0,2},{1,3},{2,0},{3,1},{4,6},{5,7},{6,4},{7,5},{8,10},{9,11},{10,... | collective-permute-start | bytes 1572872 | tf_op jit(solution)/shard_map/ppermute | solution.py:35
  506.9 26.0 %collective-permute-start.45 = (bf16[512,1024]{1,0:T(8,128)(2,1)S(1)}, bf16[512,1024]{1,0:T(8,128)(2,1)S(1)}, u32[]{:S(2)}, u32[]{:S(2)}) collective-permute-start(bf16[512,1024]{1,0:T(8,128)(2,1)S(1)} %broadcast_select_fusion.12), channel_id=1, source_target_pairs={{0,8},{8,0},{16,24},{24,16},{1,9},{9,1},{17,25},{25,17},{2,10},{10... | collective-permute-start | bytes 3145736 | tf_op jit(solution)/shard_map/ppermute | solution.py:124
  507.9 74.8 %collective-permute-start.40 = (bf16[2,2,2,64,2048]{4,3,0,1,2:T(8,128)(2,1)}, bf16[2,2,2,64,2048]{4,3,0,1,2:T(8,128)(2,1)}, u32[]{:S(2)}, u32[]{:S(2)}) collective-permute-start(bf16[2,2,2,64,2048]{4,3,0,1,2:T(8,128)(2,1)} %get-tuple-element.134), channel_id=1, source_target_pairs={{0,1},{1,0},{2,3},{3,2},{4,5},{5,4},{6,7},{7,6},{8,9},{9,8},{10,11... | collective-permute-start | bytes 6291464 | tf_op jit(solution)/shard_map/ppermute | solution.py:35
  511.0 44.4 %collective-permute-start.65 = (bf16[512,1024]{1,0:T(8,128)(2,1)S(1)}, bf16[512,1024]{1,0:T(8,128)(2,1)S(1)}, u32[]{:S(2)}, u32[]{:S(2)}) collective-permute-start(bf16[512,1024]{1,0:T(8,128)(2,1)S(1)} %broadcast_select_fusion.9), channel_id=1, source_target_pairs={{0,8},{8,0},{16,24},{24,16},{1,9},{9,1},{17,25},{25,17},{2,10},{10... | collective-permute-start | bytes 3145736 | tf_op jit(solution)/shard_map/ppermute | solution.py:124
  513.7 60.7 %collective-permute-start.68 = (bf16[512,1024]{1,0:T(8,128)(2,1)}, bf16[512,1024]{1,0:T(8,128)(2,1)}, u32[]{:S(2)}, u32[]{:S(2)}) collective-permute-start(bf16[512,1024]{1,0:T(8,128)(2,1)} %broadcast_select_fusion.8), channel_id=1, source_target_pairs={{0,8},{8,0},{16,24},{24,16},{1,9},{9,1},{17,25},{25,17},{2,10},{10... | collective-permute-start | bytes 3145736 | tf_op jit(solution)/shard_map/ppermute | solution.py:124
  533.2 47.1 %collective-permute-start.59 = (bf16[512,1024]{1,0:T(8,128)(2,1)S(1)}, bf16[512,1024]{1,0:T(8,128)(2,1)}, u32[]{:S(2)}, u32[]{:S(2)}) collective-permute-start(bf16[512,1024]{1,0:T(8,128)(2,1)S(1)} %add_convert_fusion.9), channel_id=1, source_target_pairs={{0,0},{8,16},{16,8},{24,24},{1,1},{9,17},{17,9},{25,25},{2,2},{10,... | collective-permute-start | bytes 3145736 | tf_op jit(solution)/shard_map/ppermute | solution.py:124
  540.3 53.8 %collective-permute-start.58 = (bf16[2,2,2,64,2048]{4,3,0,1,2:T(8,128)(2,1)}, bf16[2,2,2,64,2048]{4,3,0,1,2:T(8,128)(2,1)}, u32[]{:S(2)}, u32[]{:S(2)}) collective-permute-start(bf16[2,2,2,64,2048]{4,3,0,1,2:T(8,128)(2,1)} %get-tuple-element.130), channel_id=1, source_target_pairs={{0,1},{1,0},{2,3},{3,2},{4,5},{5,4},{6,7},{7,6},{8,9},{9,8},{10,11... | collective-permute-start | bytes 6291464 | tf_op jit(solution)/shard_map/ppermute | solution.py:35
  565.6 26.5 %collective-permute-start.71 = (bf16[512,1024]{1,0:T(8,128)(2,1)S(1)}, bf16[512,1024]{1,0:T(8,128)(2,1)S(1)}, u32[]{:S(2)}, u32[]{:S(2)}) collective-permute-start(bf16[512,1024]{1,0:T(8,128)(2,1)S(1)} %add_convert_fusion.3), channel_id=1, source_target_pairs={{0,0},{8,16},{16,8},{24,24},{1,1},{9,17},{17,9},{25,25},{2,2},{10,... | collective-permute-start | bytes 3145736 | tf_op jit(solution)/shard_map/ppermute | solution.py:124
  578.4 32.8 %collective-permute-start.70 = (f32[108,128]{1,0:T(8,128)S(1)}, f32[108,128]{1,0:T(8,128)S(1)}, u32[]{:S(2)}, u32[]{:S(2)}) collective-permute-start(f32[108,128]{1,0:T(8,128)S(1)} %fusion.150), channel_id=1, source_target_pairs={{0,8},{8,0},{16,24},{24,16},{1,9},{9,1},{17,25},{25,17},{2,10},{10... | collective-permute-start | bytes 165896 | tf_op jit(solution)/shard_map/ppermute | solution.py:124
  582.8 28.5 %collective-permute-start.60 = (bf16[512,1024]{1,0:T(8,128)(2,1)S(1)}, bf16[512,1024]{1,0:T(8,128)(2,1)S(1)}, u32[]{:S(2)}, u32[]{:S(2)}) collective-permute-start(bf16[512,1024]{1,0:T(8,128)(2,1)S(1)} %add_convert_fusion.8), channel_id=1, source_target_pairs={{0,8},{8,0},{16,24},{24,16},{1,9},{9,1},{17,25},{25,17},{2,10},{10... | collective-permute-start | bytes 3145736 | tf_op jit(solution)/shard_map/ppermute | solution.py:124
  592.5 41.1 %collective-permute-start.72 = (bf16[512,1024]{1,0:T(8,128)(2,1)S(1)}, bf16[512,1024]{1,0:T(8,128)(2,1)}, u32[]{:S(2)}, u32[]{:S(2)}) collective-permute-start(bf16[512,1024]{1,0:T(8,128)(2,1)S(1)} %add_convert_fusion.2), channel_id=1, source_target_pairs={{0,8},{8,0},{16,24},{24,16},{1,9},{9,1},{17,25},{25,17},{2,10},{10... | collective-permute-start | bytes 3145736 | tf_op jit(solution)/shard_map/ppermute | solution.py:124
  599.7 51.8 %collective-permute-start.74 = (bf16[512,1024]{1,0:T(8,128)(2,1)S(1)}, bf16[512,1024]{1,0:T(8,128)(2,1)}, u32[]{:S(2)}, u32[]{:S(2)}) collective-permute-start(bf16[512,1024]{1,0:T(8,128)(2,1)S(1)} %add_convert_fusion), channel_id=1, source_target_pairs={{0,8},{8,0},{16,24},{24,16},{1,9},{9,1},{17,25},{25,17},{2,10},{10... | collective-permute-start | bytes 3145736 | tf_op jit(solution)/shard_map/ppermute | solution.py:124
  (117 other events, 1538.0 us)

commit v2 on v1

--- a/solution.py
+++ b/solution.py
@@ -2,6 +2,7 @@
 import jax.numpy as jnp
 from jax import lax
 from jax.experimental import pallas as pl
+from jax.experimental.pallas import tpu as pltpu
 from jax.sharding import PartitionSpec as P
 
 
@@ -118,10 +119,8 @@
         self.depth = jnp.minimum(self.at, self.count - 1 - self.at)
 
     def exchange(self, value, kind):
-        moves = {i: i for i in range(self.count)}
-        for i in range(kind, self.count - 1, 2):
-            moves[i], moves[i + 1] = i + 1, i
-        return lax.ppermute(value, "wide", list(moves.items()))
+        pairs = [(i, i + 1) for i in range(kind, self.count - 1, 2)]
+        return lax.ppermute(value, "wide", pairs + [(b, a) for a, b in pairs])
 
     def swaps(self, kind, slot, count):
         n, half = self.count, self.half
@@ -149,7 +148,7 @@
                 got = stream.waiting(kind, slot)
                 if got:
                     stream.take(kind, slot, sync(*got))
-        return stream.chunks[0]
+        return stream.result(0)
 
 
 class Stream:
@@ -157,6 +156,7 @@
         self.line = line
         self.count = count
         self.chunks = []
+        self.final = {}
         self.flying = {}
         self.turn = 0
 
@@ -165,6 +165,20 @@
 
     def feed(self, chunk):
         self.chunks.append(chunk)
+
+    def edge(self):
+        return (self.line.depth == 0).astype(jnp.int32).reshape(1)
+
+    def pair(self, k):
+        return self.chunks[k], self.final.get(k, self.chunks[k])
+
+    def result(self, k):
+        held, got = self.pair(k)
+        return held if held is got else jnp.where(self.line.depth == 0, got, held)
+
+    def tiles(self, start, stop, per_row):
+        held, got = zip(*[self.pair(k) for k in range(start, stop)])
+        return tiled(self.edge(), held, got, per_row)
 
     def start(self, kind, slot):
         plan = self.line.swaps(kind, slot, self.count)
@@ -188,8 +202,11 @@
                 if k is None:
                     continue
                 held = self.chunks[k]
+                if not add and short:
+                    self.final[k] = got
+                    continue
                 new = add_low(held, got) if add else got
-                if not (add and short):
+                if not short:
                     new = jnp.where(self.line.depth == e, new, held)
                 self.chunks[k] = new
 
@@ -290,6 +307,7 @@
         in_specs=[block, keys_spec, vals_spec, pos_spec, valid_spec],
         out_specs=block,
         out_shape=jax.ShapeDtypeStruct((rows, width), bf16),
+        compiler_params=pltpu.CompilerParams(vmem_limit_bytes=16 << 20),
         name="attend",
     )(query, keys_vals, keys_vals, pos, valid)
 
@@ -305,29 +323,35 @@
         in_specs=[block, keys_spec, vals_spec, block, pos_spec, valid_spec],
         out_specs=[block, keys_spec, keys_spec],
         out_shape=[jax.ShapeDtypeStruct((rows, width), bf16), wide_shape, wide_shape],
+        compiler_params=pltpu.CompilerParams(vmem_limit_bytes=24 << 20),
         name="attend_back",
     )(query, keys_vals, keys_vals, out, pos, valid)
 
 
-def tile_kernel(*refs):
+def tile_kernel(edge_ref, *refs):
     *parts, out_ref = refs
-    for at, part in enumerate(parts):
-
-        @pl.when(pl.program_id(0) == at)
-        def _():
-            out_ref[...] = part[...].astype(f32)
-
-
-def tiled(parts, per_row):
-    rows, cols = parts[0].shape
+    half = len(parts) // 2
+    for at in range(half):
+        for edge, part in enumerate((parts[at], parts[at + half])):
+
+            @pl.when((pl.program_id(0) == at) & (edge_ref[0] == edge))
+            def _(part=part):
+                out_ref[...] = part[...].astype(f32)
+
+
+def tiled(edge, held, got, per_row):
+    rows, cols = held[0].shape
+    parts = list(held) + list(got)
+    whole = pl.BlockSpec((rows, cols), lambda i: (0, 0), pipeline_mode=pl.Buffered(1))
     return pl.pallas_call(
         tile_kernel,
-        grid=(len(parts),),
-        in_specs=[pl.BlockSpec((rows, cols), lambda i: (0, 0)) for _ in parts],
+        grid=(len(held),),
+        in_specs=[pl.BlockSpec(memory_space=pltpu.SMEM)] + [whole for _ in parts],
         out_specs=pl.BlockSpec((rows, cols), lambda i: (i // per_row, i % per_row)),
-        out_shape=jax.ShapeDtypeStruct((len(parts) // per_row * rows, per_row * cols), f32),
+        out_shape=jax.ShapeDtypeStruct((len(held) // per_row * rows, per_row * cols), f32),
+        compiler_params=pltpu.CompilerParams(vmem_limit_bytes=16 << 20),
         name="tiled",
-    )(*parts)
+    )(edge, *parts)
 
 
 def on_device(
@@ -483,10 +507,10 @@
     grad_b_up = sums[6 * width : 6 * width + hidden]
     grad_b_qv = sums[6 * width + hidden :].reshape(2, local_width)
 
-    done = [value.astype(f32) for value in bulk.chunks]
+    done = [None] * 8 + [bulk.result(k).astype(f32) for k in range(8, 12)]
     per_row = width // hidden
-    grad_w_down = tiled(bulk.chunks[:4], per_row)
-    grad_w_up = tiled(bulk.chunks[4:8], 1)
+    grad_w_down = bulk.tiles(0, 4, per_row)
+    grad_w_up = bulk.tiles(4, 8, 1)
     grad_w_out = jnp.concatenate(
         [done[8][i * local_width : (i + 1) * local_width] for i in range(per_row)], axis=1
     )

time: 667 us -> 669 us (level)
  starting transfers between devices: 182 us -> 238 us
  other arithmetic: 116 us -> 85.1 us
  waiting for transfers between devices: 211 us -> 201 us
  Pallas kernels: 35.4 us -> 27.7 us
    ppermute x30, starting transfers between devices: 140 us -> 189 us  [exchange(): return lax.ppermute(value, 'wide', pairs + [(b, a) for a, b in pairs])]
    select_n x9 -> x1, other arithmetic: 21.9 us -> 0.01 us  [result(): return held if held is got else jnp.where(self.line.depth == 0, got, held)]
    ppermute x30, waiting for transfers between devices: 94.4 us -> 85.9 us  [exchange(): return lax.ppermute(value, 'wide', pairs + [(b, a) for a, b in pairs])]
    convert_element_type x35, other arithmetic: 25.5 us -> 17 us  [add_low(): return (a.astype(f32) + b.astype(f32)).astype(a.dtype)]
    unnamed x150 -> x156, local copies, waits for them, and re-layouts: 18.9 us -> 21.6 us
  transfers between devices with their start and end apart: 75 -> 75, of which waited for: 37 -> 35; matrix products, arithmetic and copies ran while one was open for 24% -> 18% of each run, Pallas kernels for 4% -> 3%
where the time goes in v2:
time: 669 us; the launch traced here: 660 us
  starting transfers between devices  238 us (36%)
  waiting for transfers between devices  201 us (30%)
  other arithmetic  85.1 us (13%)
  matrix products  62.1 us (9%)
  local copies, waits for them, and re-layouts  43.5 us (7%)
  Pallas kernels  27.7 us (4%)
    ppermute x30, starting transfers between devices, exchange(): return lax.ppermute(value, 'wide', pairs + [(b, a) for a, b in pairs])  189 us
    ppermute x43, waiting for transfers between devices, swap(): lax.ppermute(value, 'narrow', [(i, i ^ 1 << bit) for i in range(count)])  114 us
    ppermute x30, waiting for transfers between devices, exchange(): return lax.ppermute(value, 'wide', pairs + [(b, a) for a, b in pairs])  85.9 us
    dot_general x23, matrix products, dot(): return lax.dot_general(a, b, (dims, ((), ())), preferred_element_type=f32)  62.1 us
    ppermute x43, starting transfers between devices, swap(): lax.ppermute(value, 'narrow', [(i, i ^ 1 << bit) for i in range(count)])  41 us
    unnamed x156, local copies, waits for them, and re-layouts  21.6 us
    convert_element_type x35, other arithmetic, add_low(): return (a.astype(f32) + b.astype(f32)).astype(a.dtype)  17 us
    select_n x19, other arithmetic, pair(): jnp.where(narrow_bit(bit) == 0, jnp.stack([value, other], axis=dim), jnp....  16.2 us
  transfers between devices with their start and end apart: 75, of which 35 were waited for; matrix products, arithmetic and copies ran while one was open for 18% of the time, Pallas kernels for 3%

profile of v2, /device:TPU:0, one launch (start us, length us, event | category | flops | bytes accessed | tf_op | source)
XLA Modules:
  0.0 660.2 jit_solution(11038976652470887733)
XLA Ops:
  6.2 4.6 copy.54
  17.7 5.8 collective-permute-start
  24.6 4.6 fusion.54.q_ref
  29.2 9.4 %convolution_convert_fusion.4 = bf16[1024,1024]{1,0:T(8,128)(2,1)} fusion(bf16[1024,2048]{1,0:T(8,128)(2,1)} %param.32, bf16[1024,2048]{1,0:T(8,128)(2,1)} %param.28), kind=kOutput, calls=%fused_computation.85 | convolution fusion | flops 4296015872 | bytes 10485760 | tf_op jit(solution)/shard_map/dot_general | solution.py:251
  40.7 8.1 %attend.1 = bf16[1024,256]{1,0:T(8,128)(2,1)S(1)} custom-call(bf16[1024,256]{1,0:T(8,128)(2,1)S(1)} %copy-done.5, bf16[1792,512]{1,0:T(8,128)(2,1)S(1)} %pad_maximum_fusion.6.k_ref.v_ref, bf16[1792,512]{1,0:T(8,128)(2,1)S(1)} %pad_maximum_fusion.6.k_ref.v_ref, s32[1024,1]{1,0:T(8,128)S(1)} %copy.55.pos_ref, s32[4,1,1024]{2,1,0:T(1,128)S(1)} %reshape.1071.valid_ref), custom_call_target="tpu_custom_call" | custom-call | tf_op jit(solution)/shard_map/attend/pallas_call | solution.py:304
  52.8 4.5 collective-permute-done.1
  67.4 10.0 %collective-permute-done.4 = bf16[2,64,2048]{2,1,0:T(8,128)(2,1)} collective-permute-done((bf16[2,64,2048]{2,1,0:T(8,128)(2,1)}, bf16[2,64,2048]{2,1,0:T(8,128)(2,1)}, u32[]{:S(2)}, u32[]{:S(2)}) %collective-permute-start.4) | collective-permute-done | bytes 524320 | tf_op jit(solution)/shard_map/ppermute | solution.py:36
  95.5 4.6 collective-permute-done.6
  107.2 5.6 collective-permute-done.7
  129.8 7.8 %convert_reduce_fusion.1 = (f32[1024]{0:T(1024)S(1)}, bf16[1024,1024]{1,0:T(8,128)(2,1)S(1)}, bf16[1024,1024]{1,0:T(8,128)(2,1)S(1)}) fusion(f32[1024]{0:T(1024)S(1)} %copy-done.73, bf16[1024,1024]{1,0:T(8,128)(2,1)S(1)} %copy-done.76, bf16[1024,2048]{1,0:T(8,128)(2,1)S(1)} %bitcast.282, bf16[2048,1024]{1,0:T(8,128)(2,1)S(1)} %copy-done.71), kind=kOutput, calls=%fused_computation.35 | convolution fusion | flops 4322229248 | bytes 14688256 | tf_op jit(solution)/shard_map/dot_general | solution.py:251
  137.6 5.0 convolution_convert_fusion.3
  155.4 6.6 %collective-permute-done.15 = bf16[2,64,2048]{2,1,0:T(8,128)(2,1)S(1)} collective-permute-done((bf16[2,64,2048]{2,1,0:T(8,128)(2,1)S(1)}, bf16[2,64,2048]{2,1,0:T(8,128)(2,1)S(1)}, u32[]{:S(2)}, u32[]{:S(2)}) %collective-permute-start.15) | collective-permute-done | bytes 524320 | tf_op jit(solution)/shard_map/ppermute | solution.py:36
  162.2 5.5 collective-permute-done.16
  167.9 9.5 %collective-permute-done.13 = bf16[512,1024]{1,0:T(8,128)(2,1)S(1)} collective-permute-done((bf16[512,1024]{1,0:T(8,128)(2,1)S(1)}, bf16[512,1024]{1,0:T(8,128)(2,1)S(1)}, u32[]{:S(2)}, u32[]{:S(2)}) %collective-permute-start.13) | collective-permute-done | bytes 1048608 | tf_op jit(solution)/shard_map/ppermute | solution.py:123
  211.8 7.3 %collective-permute-done.21 = bf16[2,64,2048]{2,1,0:T(8,128)(2,1)} collective-permute-done((bf16[2,64,2048]{2,1,0:T(8,128)(2,1)}, bf16[2,64,2048]{2,1,0:T(8,128)(2,1)}, u32[]{:S(2)}, u32[]{:S(2)}) %collective-permute-start.21) | collective-permute-done | bytes 524320 | tf_op jit(solution)/shard_map/ppermute | solution.py:36
  235.0 23.3 %collective-permute-start.29 = (bf16[512,1024]{1,0:T(8,128)(2,1)S(1)}, bf16[512,1024]{1,0:T(8,128)(2,1)S(1)}, u32[]{:S(2)}, u32[]{:S(2)}) collective-permute-start(bf16[512,1024]{1,0:T(8,128)(2,1)S(1)} %get-tuple-element.121), channel_id=1, source_target_pairs={{0,8},{16,24},{8,0},{24,16},{1,9},{17,25},{9,1},{25,17},{2,10},{18... | collective-permute-start | bytes 3145736 | tf_op jit(solution)/shard_map/ppermute | solution.py:123
  260.9 12.2 %attend_back.1 = (bf16[1024,256]{1,0:T(8,128)(2,1)S(1)}, f32[1792,256]{1,0:T(8,128)S(1)}, f32[1792,256]{1,0:T(8,128)S(1)}) custom-call(bf16[1024,256]{1,0:T(8,128)(2,1)S(1)} %copy-done.6, bf16[1792,512]{1,0:T(8,128)(2,1)S(1)} %pad_maximum_fusion.6.k_ref.v_ref, bf16[1792,512]{1,0:T(8,128)(2,1)S(1)} %pad_maximum_fusion.6.k_ref.v_ref, ...), custom_call_target="tpu_custom_call" | custom-call | tf_op jit(solution)/shard_map/attend_back/pallas_call | solution.py:320
  275.9 6.3 convolution_convert_fusion.2
  296.8 18.1 %collective-permute-start.25 = (bf16[512,1024]{1,0:T(8,128)(2,1)S(1)}, bf16[512,1024]{1,0:T(8,128)(2,1)S(1)}, u32[]{:S(2)}, u32[]{:S(2)}) collective-permute-start(bf16[512,1024]{1,0:T(8,128)(2,1)S(1)} %get-tuple-element.125), channel_id=1, source_target_pairs={{0,8},{16,24},{8,0},{24,16},{1,9},{17,25},{9,1},{25,17},{2,10},{18... | collective-permute-start | bytes 3145736 | tf_op jit(solution)/shard_map/ppermute | solution.py:123
  318.9 9.5 %collective-permute-done.31 = bf16[2,64,2048]{2,1,0:T(8,128)(2,1)S(1)} collective-permute-done((bf16[2,64,2048]{2,1,0:T(8,128)(2,1)S(1)}, bf16[2,64,2048]{2,1,0:T(8,128)(2,1)S(1)}, u32[]{:S(2)}, u32[]{:S(2)}) %collective-permute-start.31) | collective-permute-done | bytes 524320 | tf_op jit(solution)/shard_map/ppermute | solution.py:36
  328.4 26.7 %collective-permute-start.42 = (bf16[512,1024]{1,0:T(8,128)(2,1)S(1)}, bf16[512,1024]{1,0:T(8,128)(2,1)S(1)}, u32[]{:S(2)}, u32[]{:S(2)}) collective-permute-start(bf16[512,1024]{1,0:T(8,128)(2,1)S(1)} %get-tuple-element.119), channel_id=1, source_target_pairs={{0,8},{16,24},{8,0},{24,16},{1,9},{17,25},{9,1},{25,17},{2,10},{18... | collective-permute-start | bytes 3145736 | tf_op jit(solution)/shard_map/ppermute | solution.py:123
  379.6 34.3 %collective-permute-start.49 = (bf16[512,1024]{1,0:T(8,128)(2,1)S(1)}, bf16[512,1024]{1,0:T(8,128)(2,1)S(1)}, u32[]{:S(2)}, u32[]{:S(2)}) collective-permute-start(bf16[512,1024]{1,0:T(8,128)(2,1)S(1)} %get-tuple-element.113), channel_id=1, source_target_pairs={{0,8},{16,24},{8,0},{24,16},{1,9},{17,25},{9,1},{25,17},{2,10},{18... | collective-permute-start | bytes 3145736 | tf_op jit(solution)/shard_map/ppermute | solution.py:123
  416.0 21.2 %collective-permute-start.47 = (bf16[512,1024]{1,0:T(8,128)(2,1)}, bf16[512,1024]{1,0:T(8,128)(2,1)S(1)}, u32[]{:S(2)}, u32[]{:S(2)}) collective-permute-start(bf16[512,1024]{1,0:T(8,128)(2,1)} %get-tuple-element.115), channel_id=1, source_target_pairs={{0,8},{16,24},{8,0},{24,16},{1,9},{17,25},{9,1},{25,17},{2,10},{18... | collective-permute-start | bytes 3145736 | tf_op jit(solution)/shard_map/ppermute | solution.py:123
  470.9 5.9 collective-permute-done.62
  497.0 6.9 %collective-permute-done.39 = bf16[2,64,2048]{2,1,0:T(8,128)(2,1)S(1)} collective-permute-done((bf16[2,64,2048]{2,1,0:T(8,128)(2,1)S(1)}, bf16[2,64,2048]{2,1,0:T(8,128)(2,1)S(1)}, u32[]{:S(2)}, u32[]{:S(2)}) %collective-permute-start.39) | collective-permute-done | bytes 524320 | tf_op jit(solution)/shard_map/ppermute | solution.py:36
  504.7 8.1 %collective-permute-done.37 = bf16[2,64,2048]{2,1,0:T(8,128)(2,1)S(1)} collective-permute-done((bf16[2,64,2048]{2,1,0:T(8,128)(2,1)S(1)}, bf16[2,64,2048]{2,1,0:T(8,128)(2,1)S(1)}, u32[]{:S(2)}, u32[]{:S(2)}) %collective-permute-start.37) | collective-permute-done | bytes 524320 | tf_op jit(solution)/shard_map/ppermute | solution.py:36
  522.0 16.4 %collective-permute-start.68 = (bf16[512,1024]{1,0:T(8,128)(2,1)S(1)}, bf16[512,1024]{1,0:T(8,128)(2,1)S(1)}, u32[]{:S(2)}, u32[]{:S(2)}) collective-permute-start(bf16[512,1024]{1,0:T(8,128)(2,1)S(1)} %broadcast_select_fusion), channel_id=1, source_target_pairs={{0,8},{16,24},{8,0},{24,16},{1,9},{17,25},{9,1},{25,17},{2,10},{18... | collective-permute-start | bytes 3145736 | tf_op jit(solution)/shard_map/ppermute | solution.py:123
  543.6 20.8 %collective-permute-done.65.refs_7_ = bf16[512,1024]{1,0:T(8,128)(2,1)S(1)} collective-permute-done((bf16[512,1024]{1,0:T(8,128)(2,1)S(1)}, bf16[512,1024]{1,0:T(8,128)(2,1)S(1)}, u32[]{:S(2)}, u32[]{:S(2)}) %collective-permute-start.65) | collective-permute-done | bytes 1048608 | tf_op jit(solution)/shard_map/ppermute | solution.py:123
  569.8 13.1 %collective-permute-done.68 = bf16[512,1024]{1,0:T(8,128)(2,1)S(1)} collective-permute-done((bf16[512,1024]{1,0:T(8,128)(2,1)S(1)}, bf16[512,1024]{1,0:T(8,128)(2,1)S(1)}, u32[]{:S(2)}, u32[]{:S(2)}) %collective-permute-start.68) | collective-permute-done | bytes 1048608 | tf_op jit(solution)/shard_map/ppermute | solution.py:123
  600.4 14.9 %collective-permute-start.74 = (bf16[512,1024]{1,0:T(8,128)(2,1)}, bf16[512,1024]{1,0:T(8,128)(2,1)}, u32[]{:S(2)}, u32[]{:S(2)}) collective-permute-start(bf16[512,1024]{1,0:T(8,128)(2,1)} %add_convert_fusion), channel_id=1, source_target_pairs={{0,8},{16,24},{8,0},{24,16},{1,9},{17,25},{9,1},{25,17},{2,10},{18... | collective-permute-start | bytes 3145736 | tf_op jit(solution)/shard_map/ppermute | solution.py:123
  619.6 17.9 %collective-permute-done.72 = bf16[512,1024]{1,0:T(8,128)(2,1)} collective-permute-done((bf16[512,1024]{1,0:T(8,128)(2,1)S(1)}, bf16[512,1024]{1,0:T(8,128)(2,1)}, u32[]{:S(2)}, u32[]{:S(2)}) %collective-permute-start.72) | collective-permute-done | bytes 1048608 | tf_op jit(solution)/shard_map/ppermute | solution.py:123
  639.1 15.8 %collective-permute-done.74 = bf16[512,1024]{1,0:T(8,128)(2,1)} collective-permute-done((bf16[512,1024]{1,0:T(8,128)(2,1)}, bf16[512,1024]{1,0:T(8,128)(2,1)}, u32[]{:S(2)}, u32[]{:S(2)}) %collective-permute-start.74) | collective-permute-done | bytes 1048608 | tf_op jit(solution)/shard_map/ppermute | solution.py:123
  (469 shorter events, 286.8 us)
Async XLA Ops:
  151.3 26.1 %collective-permute-start.13 = (bf16[512,1024]{1,0:T(8,128)(2,1)S(1)}, bf16[512,1024]{1,0:T(8,128)(2,1)S(1)}, u32[]{:S(2)}, u32[]{:S(2)}) collective-permute-start(bf16[512,1024]{1,0:T(8,128)(2,1)S(1)} %fusion.39), channel_id=1, source_target_pairs={{0,8},{16,24},{8,0},{24,16},{1,9},{17,25},{9,1},{25,17},{2,10},{18... | collective-permute-start | bytes 3145736 | tf_op jit(solution)/shard_map/ppermute | solution.py:123
  181.1 24.4 %collective-permute-start.12 = (bf16[512,1024]{1,0:T(8,128)(2,1)S(1)}, bf16[512,1024]{1,0:T(8,128)(2,1)S(1)}, u32[]{:S(2)}, u32[]{:S(2)}) collective-permute-start(bf16[512,1024]{1,0:T(8,128)(2,1)S(1)} %fusion.42), channel_id=1, source_target_pairs={{0,8},{16,24},{8,0},{24,16},{1,9},{17,25},{9,1},{25,17},{2,10},{18... | collective-permute-start | bytes 3145736 | tf_op jit(solution)/shard_map/ppermute | solution.py:123
  221.3 37.0 %collective-permute-start.23 = (bf16[2,2,2,64,2048]{4,3,1,2,0:T(8,128)(2,1)S(1)}, bf16[2,2,2,64,2048]{4,3,1,2,0:T(8,128)(2,1)S(1)}, u32[]{:S(2)}, u32[]{:S(2)}) collective-permute-start(bf16[2,2,2,64,2048]{4,3,1,2,0:T(8,128)(2,1)S(1)} %get-tuple-element.154), channel_id=1, source_target_pairs={{0,1},{1,0},{2,3},{3,2},{4,5},{5,4},{6,7},{7,6},{8,9},{9,8},{10,11... | collective-permute-start | bytes 6291464 | tf_op jit(solution)/shard_map/ppermute | solution.py:36
  225.1 35.8 %collective-permute-start.11 = (bf16[512,1024]{1,0:T(8,128)(2,1)S(1)}, bf16[512,1024]{1,0:T(8,128)(2,1)S(1)}, u32[]{:S(2)}, u32[]{:S(2)}) collective-permute-start(bf16[512,1024]{1,0:T(8,128)(2,1)S(1)} %fusion.36), channel_id=1, source_target_pairs={{0,8},{16,24},{8,0},{24,16},{1,9},{17,25},{9,1},{25,17},{2,10},{18... | collective-permute-start | bytes 3145736 | tf_op jit(solution)/shard_map/ppermute | solution.py:123
  232.6 52.5 %collective-permute-start.26 = (bf16[512,1024]{1,0:T(8,128)(2,1)S(1)}, bf16[512,1024]{1,0:T(8,128)(2,1)}, u32[]{:S(2)}, u32[]{:S(2)}) collective-permute-start(bf16[512,1024]{1,0:T(8,128)(2,1)S(1)} %add_convert_fusion.21), channel_id=1, source_target_pairs={{8,16},{16,8},{9,17},{17,9},{10,18},{18,10},{11,19},{19,11},{12,20... | collective-permute-start | bytes 3145736 | tf_op jit(solution)/shard_map/ppermute | solution.py:123
  235.0 40.9 %collective-permute-start.29 = (bf16[512,1024]{1,0:T(8,128)(2,1)S(1)}, bf16[512,1024]{1,0:T(8,128)(2,1)S(1)}, u32[]{:S(2)}, u32[]{:S(2)}) collective-permute-start(bf16[512,1024]{1,0:T(8,128)(2,1)S(1)} %get-tuple-element.121), channel_id=1, source_target_pairs={{0,8},{16,24},{8,0},{24,16},{1,9},{17,25},{9,1},{25,17},{2,10},{18... | collective-permute-start | bytes 3145736 | tf_op jit(solution)/shard_map/ppermute | solution.py:123
  282.4 32.4 %collective-permute-start.30 = (bf16[512,2048]{1,0:T(8,128)(2,1)S(1)}, bf16[512,2048]{1,0:T(8,128)(2,1)S(1)}, u32[]{:S(2)}, u32[]{:S(2)}) collective-permute-start(bf16[512,2048]{1,0:T(8,128)(2,1)S(1)} %dynamic-slice_bitcast_fusion.1), channel_id=1, source_target_pairs={{0,1},{1,0},{2,3},{3,2},{4,5},{5,4},{6,7},{7,6},{8,9},{9,8},{10,11... | collective-permute-start | bytes 6291464 | tf_op jit(solution)/shard_map/ppermute | solution.py:36
  287.1 68.3 %collective-permute-start.27 = (bf16[512,1024]{1,0:T(8,128)(2,1)S(1)}, bf16[512,1024]{1,0:T(8,128)(2,1)S(1)}, u32[]{:S(2)}, u32[]{:S(2)}) collective-permute-start(bf16[512,1024]{1,0:T(8,128)(2,1)S(1)} %get-tuple-element.123), channel_id=1, source_target_pairs={{0,8},{16,24},{8,0},{24,16},{1,9},{17,25},{9,1},{25,17},{2,10},{18... | collective-permute-start | bytes 3145736 | tf_op jit(solution)/shard_map/ppermute | solution.py:123
  291.6 63.8 %collective-permute-start.33 = (bf16[768,512]{1,0:T(8,128)(2,1)S(1)}, bf16[768,512]{1,0:T(8,128)(2,1)S(1)}, u32[]{:S(2)}, u32[]{:S(2)}) collective-permute-start(bf16[768,512]{1,0:T(8,128)(2,1)S(1)} %slice.404), channel_id=1, source_target_pairs={{8,0},{16,8},{24,16},{9,1},{17,9},{25,17},{10,2},{18,10},{26,18},{... | collective-permute-start | bytes 2359304 | tf_op jit(solution)/shard_map/ppermute | solution.py:454
  293.8 22.9 %collective-permute-start.41 = (bf16[512,1024]{1,0:T(8,128)(2,1)S(1)}, bf16[512,1024]{1,0:T(8,128)(2,1)S(1)}, u32[]{:S(2)}, u32[]{:S(2)}) collective-permute-start(bf16[512,1024]{1,0:T(8,128)(2,1)S(1)} %add_convert_fusion.17), channel_id=1, source_target_pairs={{8,16},{16,8},{9,17},{17,9},{10,18},{18,10},{11,19},{19,11},{12,20... | collective-permute-start | bytes 3145736 | tf_op jit(solution)/shard_map/ppermute | solution.py:123
  296.8 73.3 %collective-permute-start.25 = (bf16[512,1024]{1,0:T(8,128)(2,1)S(1)}, bf16[512,1024]{1,0:T(8,128)(2,1)S(1)}, u32[]{:S(2)}, u32[]{:S(2)}) collective-permute-start(bf16[512,1024]{1,0:T(8,128)(2,1)S(1)} %get-tuple-element.125), channel_id=1, source_target_pairs={{0,8},{16,24},{8,0},{24,16},{1,9},{17,25},{9,1},{25,17},{2,10},{18... | collective-permute-start | bytes 3145736 | tf_op jit(solution)/shard_map/ppermute | solution.py:123
  316.7 38.5 %collective-permute-start.32 = (bf16[2,64,2048]{2,1,0:T(8,128)(2,1)S(1)}, bf16[2,64,2048]{2,1,0:T(8,128)(2,1)S(1)}, u32[]{:S(2)}, u32[]{:S(2)}) collective-permute-start(bf16[2,64,2048]{2,1,0:T(8,128)(2,1)S(1)} %dynamic-slice_bitcast_fusion.6), channel_id=1, source_target_pairs={{0,4},{1,5},{2,6},{3,7},{4,0},{5,1},{6,2},{7,3},{8,12},{9,13},{10,... | collective-permute-start | bytes 1572872 | tf_op jit(solution)/shard_map/ppermute | solution.py:36
  328.4 109.7 %collective-permute-start.42 = (bf16[512,1024]{1,0:T(8,128)(2,1)S(1)}, bf16[512,1024]{1,0:T(8,128)(2,1)S(1)}, u32[]{:S(2)}, u32[]{:S(2)}) collective-permute-start(bf16[512,1024]{1,0:T(8,128)(2,1)S(1)} %get-tuple-element.119), channel_id=1, source_target_pairs={{0,8},{16,24},{8,0},{24,16},{1,9},{17,25},{9,1},{25,17},{2,10},{18... | collective-permute-start | bytes 3145736 | tf_op jit(solution)/shard_map/ppermute | solution.py:123
  374.0 63.2 %collective-permute-start.43 = (bf16[512,2048]{1,0:T(8,128)(2,1)S(1)}, bf16[512,2048]{1,0:T(8,128)(2,1)S(1)}, u32[]{:S(2)}, u32[]{:S(2)}) collective-permute-start(bf16[512,2048]{1,0:T(8,128)(2,1)S(1)} %dynamic-slice_bitcast_fusion), channel_id=1, source_target_pairs={{0,1},{1,0},{2,3},{3,2},{4,5},{5,4},{6,7},{7,6},{8,9},{9,8},{10,11... | collective-permute-start | bytes 6291464 | tf_op jit(solution)/shard_map/ppermute | solution.py:36
  375.6 38.3 %collective-permute-start.46 = (bf16[512,1024]{1,0:T(8,128)(2,1)S(1)}, bf16[512,1024]{1,0:T(8,128)(2,1)S(1)}, u32[]{:S(2)}, u32[]{:S(2)}) collective-permute-start(bf16[512,1024]{1,0:T(8,128)(2,1)S(1)} %add_convert_fusion.13), channel_id=1, source_target_pairs={{8,16},{16,8},{9,17},{17,9},{10,18},{18,10},{11,19},{19,11},{12,20... | collective-permute-start | bytes 3145736 | tf_op jit(solution)/shard_map/ppermute | solution.py:123
  379.6 80.5 %collective-permute-start.49 = (bf16[512,1024]{1,0:T(8,128)(2,1)S(1)}, bf16[512,1024]{1,0:T(8,128)(2,1)S(1)}, u32[]{:S(2)}, u32[]{:S(2)}) collective-permute-start(bf16[512,1024]{1,0:T(8,128)(2,1)S(1)} %get-tuple-element.113), channel_id=1, source_target_pairs={{0,8},{16,24},{8,0},{24,16},{1,9},{17,25},{9,1},{25,17},{2,10},{18... | collective-permute-start | bytes 3145736 | tf_op jit(solution)/shard_map/ppermute | solution.py:123
  416.0 72.0 %collective-permute-start.47 = (bf16[512,1024]{1,0:T(8,128)(2,1)}, bf16[512,1024]{1,0:T(8,128)(2,1)S(1)}, u32[]{:S(2)}, u32[]{:S(2)}) collective-permute-start(bf16[512,1024]{1,0:T(8,128)(2,1)} %get-tuple-element.115), channel_id=1, source_target_pairs={{0,8},{16,24},{8,0},{24,16},{1,9},{17,25},{9,1},{25,17},{2,10},{18... | collective-permute-start | bytes 3145736 | tf_op jit(solution)/shard_map/ppermute | solution.py:123
  442.8 48.7 %collective-permute-start.44 = (bf16[512,1024]{1,0:T(8,128)(2,1)}, bf16[512,1024]{1,0:T(8,128)(2,1)}, u32[]{:S(2)}, u32[]{:S(2)}) collective-permute-start(bf16[512,1024]{1,0:T(8,128)(2,1)} %add_convert_fusion.15), channel_id=1, source_target_pairs={{8,16},{16,8},{9,17},{17,9},{10,18},{18,10},{11,19},{19,11},{12,20... | collective-permute-start | bytes 3145736 | tf_op jit(solution)/shard_map/ppermute | solution.py:123
  481.2 37.1 %collective-permute-start.64 = (bf16[512,1024]{1,0:T(8,128)(2,1)}, bf16[512,1024]{1,0:T(8,128)(2,1)}, u32[]{:S(2)}, u32[]{:S(2)}) collective-permute-start(bf16[512,1024]{1,0:T(8,128)(2,1)} %add_convert_fusion.7), channel_id=1, source_target_pairs={{8,16},{16,8},{9,17},{17,9},{10,18},{18,10},{11,19},{19,11},{12,20... | collective-permute-start | bytes 3145736 | tf_op jit(solution)/shard_map/ppermute | solution.py:123
  488.0 55.5 %collective-permute-start.66 = (f32[108,128]{1,0:T(8,128)S(1)}, f32[108,128]{1,0:T(8,128)S(1)}, u32[]{:S(2)}, u32[]{:S(2)}) collective-permute-start(f32[108,128]{1,0:T(8,128)S(1)} %maximum_bitcast_fusion.3), channel_id=1, source_target_pairs={{0,8},{16,24},{8,0},{24,16},{1,9},{17,25},{9,1},{25,17},{2,10},{18... | collective-permute-start | bytes 165896 | tf_op jit(solution)/shard_map/ppermute | solution.py:123
  490.0 24.1 %collective-permute-start.56 = (bf16[2,64,2048]{2,1,0:T(8,128)(2,1)S(1)}, bf16[2,64,2048]{2,1,0:T(8,128)(2,1)S(1)}, u32[]{:S(2)}, u32[]{:S(2)}) collective-permute-start(bf16[2,64,2048]{2,1,0:T(8,128)(2,1)S(1)} %maximum_select_fusion.22), channel_id=1, source_target_pairs={{0,2},{1,3},{2,0},{3,1},{4,6},{5,7},{6,4},{7,5},{8,10},{9,11},{10,... | collective-permute-start | bytes 1572872 | tf_op jit(solution)/shard_map/ppermute | solution.py:36
  514.1 27.8 %collective-permute-start.45 = (bf16[512,1024]{1,0:T(8,128)(2,1)S(1)}, bf16[512,1024]{1,0:T(8,128)(2,1)S(1)}, u32[]{:S(2)}, u32[]{:S(2)}) collective-permute-start(bf16[512,1024]{1,0:T(8,128)(2,1)S(1)} %get-tuple-element.117), channel_id=1, source_target_pairs={{0,8},{16,24},{8,0},{24,16},{1,9},{17,25},{9,1},{25,17},{2,10},{18... | collective-permute-start | bytes 3145736 | tf_op jit(solution)/shard_map/ppermute | solution.py:123
  518.1 70.8 %collective-permute-start.40 = (bf16[2,2,2,64,2048]{4,3,0,1,2:T(8,128)(2,1)S(1)}, bf16[2,2,2,64,2048]{4,3,0,1,2:T(8,128)(2,1)S(1)}, u32[]{:S(2)}, u32[]{:S(2)}) collective-permute-start(bf16[2,2,2,64,2048]{4,3,0,1,2:T(8,128)(2,1)S(1)} %get-tuple-element.150), channel_id=1, source_target_pairs={{0,1},{1,0},{2,3},{3,2},{4,5},{5,4},{6,7},{7,6},{8,9},{9,8},{10,11... | collective-permute-start | bytes 6291464 | tf_op jit(solution)/shard_map/ppermute | solution.py:36
  521.3 43.1 %collective-permute-start.65 = (bf16[512,1024]{1,0:T(8,128)(2,1)S(1)}, bf16[512,1024]{1,0:T(8,128)(2,1)S(1)}, u32[]{:S(2)}, u32[]{:S(2)}) collective-permute-start(bf16[512,1024]{1,0:T(8,128)(2,1)S(1)} %get-tuple-element.111), channel_id=1, source_target_pairs={{0,8},{16,24},{8,0},{24,16},{1,9},{17,25},{9,1},{25,17},{2,10},{18... | collective-permute-start | bytes 3145736 | tf_op jit(solution)/shard_map/ppermute | solution.py:123
  522.0 60.9 %collective-permute-start.68 = (bf16[512,1024]{1,0:T(8,128)(2,1)S(1)}, bf16[512,1024]{1,0:T(8,128)(2,1)S(1)}, u32[]{:S(2)}, u32[]{:S(2)}) collective-permute-start(bf16[512,1024]{1,0:T(8,128)(2,1)S(1)} %broadcast_select_fusion), channel_id=1, source_target_pairs={{0,8},{16,24},{8,0},{24,16},{1,9},{17,25},{9,1},{25,17},{2,10},{18... | collective-permute-start | bytes 3145736 | tf_op jit(solution)/shard_map/ppermute | solution.py:123
  542.2 45.5 %collective-permute-start.59 = (bf16[512,1024]{1,0:T(8,128)(2,1)S(1)}, bf16[512,1024]{1,0:T(8,128)(2,1)S(1)}, u32[]{:S(2)}, u32[]{:S(2)}) collective-permute-start(bf16[512,1024]{1,0:T(8,128)(2,1)S(1)} %add_convert_fusion.9), channel_id=1, source_target_pairs={{8,16},{16,8},{9,17},{17,9},{10,18},{18,10},{11,19},{19,11},{12,20... | collective-permute-start | bytes 3145736 | tf_op jit(solution)/shard_map/ppermute | solution.py:123
  543.5 52.5 %collective-permute-start.58 = (bf16[2,2,2,64,2048]{4,3,0,1,2:T(8,128)(2,1)S(1)}, bf16[2,2,2,64,2048]{4,3,0,1,2:T(8,128)(2,1)S(1)}, u32[]{:S(2)}, u32[]{:S(2)}) collective-permute-start(bf16[2,2,2,64,2048]{4,3,0,1,2:T(8,128)(2,1)S(1)} %get-tuple-element.146), channel_id=1, source_target_pairs={{0,1},{1,0},{2,3},{3,2},{4,5},{5,4},{6,7},{7,6},{8,9},{9,8},{10,11... | collective-permute-start | bytes 6291464 | tf_op jit(solution)/shard_map/ppermute | solution.py:36
  569.1 24.9 %collective-permute-start.71 = (bf16[512,1024]{1,0:T(8,128)(2,1)S(1)}, bf16[512,1024]{1,0:T(8,128)(2,1)S(1)}, u32[]{:S(2)}, u32[]{:S(2)}) collective-permute-start(bf16[512,1024]{1,0:T(8,128)(2,1)S(1)} %add_convert_fusion.3), channel_id=1, source_target_pairs={{8,16},{16,8},{9,17},{17,9},{10,18},{18,10},{11,19},{19,11},{12,20... | collective-permute-start | bytes 3145736 | tf_op jit(solution)/shard_map/ppermute | solution.py:123
  584.1 31.3 %collective-permute-start.70 = (f32[108,128]{1,0:T(8,128)S(1)}, f32[108,128]{1,0:T(8,128)S(1)}, u32[]{:S(2)}, u32[]{:S(2)}) collective-permute-start(f32[108,128]{1,0:T(8,128)S(1)} %fusion.150), channel_id=1, source_target_pairs={{0,8},{16,24},{8,0},{24,16},{1,9},{17,25},{9,1},{25,17},{2,10},{18... | collective-permute-start | bytes 165896 | tf_op jit(solution)/shard_map/ppermute | solution.py:123
  588.8 26.5 %collective-permute-start.60 = (bf16[512,1024]{1,0:T(8,128)(2,1)S(1)}, bf16[512,1024]{1,0:T(8,128)(2,1)S(1)}, u32[]{:S(2)}, u32[]{:S(2)}) collective-permute-start(bf16[512,1024]{1,0:T(8,128)(2,1)S(1)} %add_convert_fusion.8), channel_id=1, source_target_pairs={{0,8},{16,24},{8,0},{24,16},{1,9},{17,25},{9,1},{25,17},{2,10},{18... | collective-permute-start | bytes 3145736 | tf_op jit(solution)/shard_map/ppermute | solution.py:123
  594.4 43.2 %collective-permute-start.72 = (bf16[512,1024]{1,0:T(8,128)(2,1)S(1)}, bf16[512,1024]{1,0:T(8,128)(2,1)}, u32[]{:S(2)}, u32[]{:S(2)}) collective-permute-start(bf16[512,1024]{1,0:T(8,128)(2,1)S(1)} %add_convert_fusion.2), channel_id=1, source_target_pairs={{0,8},{16,24},{8,0},{24,16},{1,9},{17,25},{9,1},{25,17},{2,10},{18... | collective-permute-start | bytes 3145736 | tf_op jit(solution)/shard_map/ppermute | solution.py:123
  600.4 54.5 %collective-permute-start.74 = (bf16[512,1024]{1,0:T(8,128)(2,1)}, bf16[512,1024]{1,0:T(8,128)(2,1)}, u32[]{:S(2)}, u32[]{:S(2)}) collective-permute-start(bf16[512,1024]{1,0:T(8,128)(2,1)} %add_convert_fusion), channel_id=1, source_target_pairs={{0,8},{16,24},{8,0},{24,16},{1,9},{17,25},{9,1},{25,17},{2,10},{18... | collective-permute-start | bytes 3145736 | tf_op jit(solution)/shard_map/ppermute | solution.py:123
  (120 other events, 1563.1 us)

commit v3 on v2

--- a/solution.py
+++ b/solution.py
@@ -422,9 +422,8 @@
     step = width // 4
     places = [(i, j) for i in range(0, hidden, step) for j in range(0, width, hidden)]
     for i, j in places:
-        bulk.feed(
-            dot(active[:, i : i + step], cotangent[:, j : j + hidden], ((0,), (0,))).astype(bf16)
-        )
+        part = dot(active[:, i : i + step], cotangent[:, j : j + hidden], ((0,), (0,)))
+        bulk.feed(part.astype(bf16))
     bulk.begin()
     for i in range(4):
         bulk.feed(
@@ -455,14 +454,8 @@
     own = grad_kv[MAX_DOCUMENT:]
     own, active = bulk.sync(own, active)
     mlp_part = dot(active, w_down, ((1,), (0,))).astype(bf16)
-    held = [own]
-
-    def sync_own(*values):
-        *values, held[0] = bulk.sync(*values, held[0])
-        return values
-
-    mlp_total = reduce_rows(mlp_part, at_calls(sync_own, 1)).astype(f32)
-    own = held[0]
+    mlp_total = reduce_rows(mlp_part, at_calls(bulk.sync, 1)).astype(f32)
+    own, got, mlp_total = bulk.sync(own, got, mlp_total)
     low = rows - MAX_DOCUMENT
     grad_kv = jnp.concatenate([own[:low], own[low:] + got.astype(f32)]).astype(bf16)
     grad_mixed = jnp.concatenate([grad_query, grad_kv], axis=1)
@@ -474,7 +467,6 @@
     for i in range(3):
         extra = rest[:, i * local_width : (i + 1) * local_width]
         bulk.feed(jnp.concatenate([parts[i], extra], axis=1))
-    grad_mixed, mlp_total = bulk.sync(grad_mixed, mlp_total)
     grad_b_qv = jnp.sum(grad_mixed.astype(f32), axis=0)
     grad_b_qv = [grad_b_qv[i * local_width : (i + 1) * local_width] for i in (0, 2)]
     back_part = dot(grad_mixed, w_flat, ((1,), (1,))).astype(bf16)

time: 669 us -> 651 us (0.973)
  starting transfers between devices: 238 us -> 223 us
    ppermute x30, starting transfers between devices: 189 us -> 170 us  [exchange(): return lax.ppermute(value, 'wide', pairs + [(b, a) for a, b in pairs])]
    unnamed x156 -> x162, local copies, waits for them, and re-layouts: 21.6 us -> 23.7 us
  transfers between devices with their start and end apart: 75 -> 75, of which waited for: 35 -> 34; matrix products, arithmetic and copies ran while one was open for 18% -> 18% of each run, Pallas kernels for 3% -> 3%
where the time goes in v3:
time: 651 us; the launch traced here: 643 us
  starting transfers between devices  223 us (34%)
  waiting for transfers between devices  197 us (30%)
  other arithmetic  84.8 us (13%)
  matrix products  61.3 us (9%)
  local copies, waits for them, and re-layouts  45.7 us (7%)
  Pallas kernels  27.7 us (4%)
    ppermute x30, starting transfers between devices, exchange(): return lax.ppermute(value, 'wide', pairs + [(b, a) for a, b in pairs])  170 us
    ppermute x43, waiting for transfers between devices, swap(): lax.ppermute(value, 'narrow', [(i, i ^ 1 << bit) for i in range(count)])  111 us
    ppermute x30, waiting for transfers between devices, exchange(): return lax.ppermute(value, 'wide', pairs + [(b, a) for a, b in pairs])  85.1 us
    dot_general x23, matrix products, dot(): return lax.dot_general(a, b, (dims, ((), ())), preferred_element_type=f32)  61.3 us
    ppermute x43, starting transfers between devices, swap(): lax.ppermute(value, 'narrow', [(i, i ^ 1 << bit) for i in range(count)])  45.3 us
    unnamed x162, local copies, waits for them, and re-layouts  23.7 us
    convert_element_type x35, other arithmetic, add_low(): return (a.astype(f32) + b.astype(f32)).astype(a.dtype)  16.9 us
    select_n x19, other arithmetic, pair(): jnp.where(narrow_bit(bit) == 0, jnp.stack([value, other], axis=dim), jnp....  16.1 us
  transfers between devices with their start and end apart: 75, of which 34 were waited for; matrix products, arithmetic and copies ran while one was open for 18% of the time, Pallas kernels for 3%

profile of v3, /device:TPU:0, one launch (start us, length us, event | category | flops | bytes accessed | tf_op | source)
XLA Modules:
  0.0 642.6 jit_solution(1338234979940398415)
XLA Ops:
  6.2 4.6 copy.54
  17.7 5.8 collective-permute-start
  24.6 4.6 fusion.54.q_ref
  29.2 9.4 %convolution_convert_fusion.4 = bf16[1024,1024]{1,0:T(8,128)(2,1)} fusion(bf16[1024,2048]{1,0:T(8,128)(2,1)} %param.32, bf16[1024,2048]{1,0:T(8,128)(2,1)} %param.28), kind=kOutput, calls=%fused_computation.85 | convolution fusion | flops 4296015872 | bytes 10485760 | tf_op jit(solution)/shard_map/dot_general | solution.py:251
  40.7 8.1 %attend.1 = bf16[1024,256]{1,0:T(8,128)(2,1)S(1)} custom-call(bf16[1024,256]{1,0:T(8,128)(2,1)S(1)} %copy-done.5, bf16[1792,512]{1,0:T(8,128)(2,1)S(1)} %pad_maximum_fusion.6.k_ref.v_ref, bf16[1792,512]{1,0:T(8,128)(2,1)S(1)} %pad_maximum_fusion.6.k_ref.v_ref, s32[1024,1]{1,0:T(8,128)S(1)} %copy.55.pos_ref, s32[4,1,1024]{2,1,0:T(1,128)S(1)} %reshape.1071.valid_ref), custom_call_target="tpu_custom_call" | custom-call | tf_op jit(solution)/shard_map/attend/pallas_call | solution.py:304
  67.5 10.0 %collective-permute-done.4 = bf16[2,64,2048]{2,1,0:T(8,128)(2,1)} collective-permute-done((bf16[2,64,2048]{2,1,0:T(8,128)(2,1)}, bf16[2,64,2048]{2,1,0:T(8,128)(2,1)}, u32[]{:S(2)}, u32[]{:S(2)}) %collective-permute-start.4) | collective-permute-done | bytes 524320 | tf_op jit(solution)/shard_map/ppermute | solution.py:36
  95.6 4.6 collective-permute-done.6
  107.2 5.6 collective-permute-done.7
  129.8 7.8 %convert_reduce_fusion.1 = (f32[1024]{0:T(1024)S(1)}, bf16[1024,1024]{1,0:T(8,128)(2,1)S(1)}, bf16[1024,1024]{1,0:T(8,128)(2,1)S(1)}) fusion(f32[1024]{0:T(1024)S(1)} %copy-done.75, bf16[1024,1024]{1,0:T(8,128)(2,1)S(1)} %copy-done.79, bf16[1024,2048]{1,0:T(8,128)(2,1)S(1)} %bitcast.281, bf16[2048,1024]{1,0:T(8,128)(2,1)S(1)} %copy-done.73), kind=kOutput, calls=%fused_computation.35 | convolution fusion | flops 4322229248 | bytes 14688256 | tf_op jit(solution)/shard_map/dot_general | solution.py:251
  137.6 5.0 convolution_convert_fusion.3
  155.4 6.6 %collective-permute-done.15 = bf16[2,64,2048]{2,1,0:T(8,128)(2,1)S(1)} collective-permute-done((bf16[2,64,2048]{2,1,0:T(8,128)(2,1)S(1)}, bf16[2,64,2048]{2,1,0:T(8,128)(2,1)S(1)}, u32[]{:S(2)}, u32[]{:S(2)}) %collective-permute-start.15) | collective-permute-done | bytes 524320 | tf_op jit(solution)/shard_map/ppermute | solution.py:36
  162.2 5.6 collective-permute-done.16
  167.9 9.5 %collective-permute-done.13 = bf16[512,1024]{1,0:T(8,128)(2,1)S(1)} collective-permute-done((bf16[512,1024]{1,0:T(8,128)(2,1)S(1)}, bf16[512,1024]{1,0:T(8,128)(2,1)S(1)}, u32[]{:S(2)}, u32[]{:S(2)}) %collective-permute-start.13) | collective-permute-done | bytes 1048608 | tf_op jit(solution)/shard_map/ppermute | solution.py:123
  211.8 7.3 %collective-permute-done.21 = bf16[2,64,2048]{2,1,0:T(8,128)(2,1)} collective-permute-done((bf16[2,64,2048]{2,1,0:T(8,128)(2,1)}, bf16[2,64,2048]{2,1,0:T(8,128)(2,1)}, u32[]{:S(2)}, u32[]{:S(2)}) %collective-permute-start.21) | collective-permute-done | bytes 524320 | tf_op jit(solution)/shard_map/ppermute | solution.py:36
  235.0 23.3 %collective-permute-start.27 = (bf16[512,1024]{1,0:T(8,128)(2,1)S(1)}, bf16[512,1024]{1,0:T(8,128)(2,1)S(1)}, u32[]{:S(2)}, u32[]{:S(2)}) collective-permute-start(bf16[512,1024]{1,0:T(8,128)(2,1)S(1)} %get-tuple-element.123), channel_id=1, source_target_pairs={{0,8},{16,24},{8,0},{24,16},{1,9},{17,25},{9,1},{25,17},{2,10},{18... | collective-permute-start | bytes 3145736 | tf_op jit(solution)/shard_map/ppermute | solution.py:123
  261.6 12.2 %attend_back.1 = (bf16[1024,256]{1,0:T(8,128)(2,1)S(1)}, f32[1792,256]{1,0:T(8,128)S(1)}, f32[1792,256]{1,0:T(8,128)S(1)}) custom-call(bf16[1024,256]{1,0:T(8,128)(2,1)S(1)} %copy-done.6, bf16[1792,512]{1,0:T(8,128)(2,1)S(1)} %pad_maximum_fusion.6.k_ref.v_ref, bf16[1792,512]{1,0:T(8,128)(2,1)S(1)} %pad_maximum_fusion.6.k_ref.v_ref, ...), custom_call_target="tpu_custom_call" | custom-call | tf_op jit(solution)/shard_map/attend_back/pallas_call | solution.py:320
  277.0 4.8 convolution_convert_fusion.2
  295.3 18.1 %collective-permute-start.25 = (bf16[512,1024]{1,0:T(8,128)(2,1)S(1)}, bf16[512,1024]{1,0:T(8,128)(2,1)S(1)}, u32[]{:S(2)}, u32[]{:S(2)}) collective-permute-start(bf16[512,1024]{1,0:T(8,128)(2,1)S(1)} %get-tuple-element.125), channel_id=1, source_target_pairs={{0,8},{16,24},{8,0},{24,16},{1,9},{17,25},{9,1},{25,17},{2,10},{18... | collective-permute-start | bytes 3145736 | tf_op jit(solution)/shard_map/ppermute | solution.py:123
  317.5 9.5 %collective-permute-done.32 = bf16[2,64,2048]{2,1,0:T(8,128)(2,1)S(1)} collective-permute-done((bf16[2,64,2048]{2,1,0:T(8,128)(2,1)S(1)}, bf16[2,64,2048]{2,1,0:T(8,128)(2,1)S(1)}, u32[]{:S(2)}, u32[]{:S(2)}) %collective-permute-start.32) | collective-permute-done | bytes 524320 | tf_op jit(solution)/shard_map/ppermute | solution.py:36
  326.9 26.7 %collective-permute-start.42 = (bf16[512,1024]{1,0:T(8,128)(2,1)S(1)}, bf16[512,1024]{1,0:T(8,128)(2,1)S(1)}, u32[]{:S(2)}, u32[]{:S(2)}) collective-permute-start(bf16[512,1024]{1,0:T(8,128)(2,1)S(1)} %get-tuple-element.119), channel_id=1, source_target_pairs={{0,8},{16,24},{8,0},{24,16},{1,9},{17,25},{9,1},{25,17},{2,10},{18... | collective-permute-start | bytes 3145736 | tf_op jit(solution)/shard_map/ppermute | solution.py:123
  355.7 5.5 collective-permute-done.35
  380.5 20.0 %collective-permute-start.49 = (bf16[512,1024]{1,0:T(8,128)(2,1)S(1)}, bf16[512,1024]{1,0:T(8,128)(2,1)S(1)}, u32[]{:S(2)}, u32[]{:S(2)}) collective-permute-start(bf16[512,1024]{1,0:T(8,128)(2,1)S(1)} %get-tuple-element.113), channel_id=1, source_target_pairs={{0,8},{16,24},{8,0},{24,16},{1,9},{17,25},{9,1},{25,17},{2,10},{18... | collective-permute-start | bytes 3145736 | tf_op jit(solution)/shard_map/ppermute | solution.py:123
  402.6 18.5 %collective-permute-start.47 = (bf16[512,1024]{1,0:T(8,128)(2,1)}, bf16[512,1024]{1,0:T(8,128)(2,1)S(1)}, u32[]{:S(2)}, u32[]{:S(2)}) collective-permute-start(bf16[512,1024]{1,0:T(8,128)(2,1)} %get-tuple-element.115), channel_id=1, source_target_pairs={{0,8},{16,24},{8,0},{24,16},{1,9},{17,25},{9,1},{25,17},{2,10},{18... | collective-permute-start | bytes 3145736 | tf_op jit(solution)/shard_map/ppermute | solution.py:123
  453.3 5.6 collective-permute-done.62
  479.9 6.3 collective-permute-done.39
  488.2 7.3 %collective-permute-done.37 = bf16[2,64,2048]{2,1,0:T(8,128)(2,1)S(1)} collective-permute-done((bf16[2,64,2048]{2,1,0:T(8,128)(2,1)S(1)}, bf16[2,64,2048]{2,1,0:T(8,128)(2,1)S(1)}, u32[]{:S(2)}, u32[]{:S(2)}) %collective-permute-start.37) | collective-permute-done | bytes 524320 | tf_op jit(solution)/shard_map/ppermute | solution.py:36
  503.7 16.8 %collective-permute-start.68 = (bf16[512,1024]{1,0:T(8,128)(2,1)S(1)}, bf16[512,1024]{1,0:T(8,128)(2,1)S(1)}, u32[]{:S(2)}, u32[]{:S(2)}) collective-permute-start(bf16[512,1024]{1,0:T(8,128)(2,1)S(1)} %broadcast_select_fusion), channel_id=1, source_target_pairs={{0,8},{16,24},{8,0},{24,16},{1,9},{17,25},{9,1},{25,17},{2,10},{18... | collective-permute-start | bytes 3145736 | tf_op jit(solution)/shard_map/ppermute | solution.py:123
  525.3 20.8 %collective-permute-done.65.refs_7_ = bf16[512,1024]{1,0:T(8,128)(2,1)S(1)} collective-permute-done((bf16[512,1024]{1,0:T(8,128)(2,1)S(1)}, bf16[512,1024]{1,0:T(8,128)(2,1)S(1)}, u32[]{:S(2)}, u32[]{:S(2)}) %collective-permute-start.65) | collective-permute-done | bytes 1048608 | tf_op jit(solution)/shard_map/ppermute | solution.py:123
  551.6 13.1 %collective-permute-done.68 = bf16[512,1024]{1,0:T(8,128)(2,1)S(1)} collective-permute-done((bf16[512,1024]{1,0:T(8,128)(2,1)S(1)}, bf16[512,1024]{1,0:T(8,128)(2,1)S(1)}, u32[]{:S(2)}, u32[]{:S(2)}) %collective-permute-start.68) | collective-permute-done | bytes 1048608 | tf_op jit(solution)/shard_map/ppermute | solution.py:123
  582.3 15.1 %collective-permute-start.74 = (bf16[512,1024]{1,0:T(8,128)(2,1)}, bf16[512,1024]{1,0:T(8,128)(2,1)}, u32[]{:S(2)}, u32[]{:S(2)}) collective-permute-start(bf16[512,1024]{1,0:T(8,128)(2,1)} %add_convert_fusion), channel_id=1, source_target_pairs={{0,8},{16,24},{8,0},{24,16},{1,9},{17,25},{9,1},{25,17},{2,10},{18... | collective-permute-start | bytes 3145736 | tf_op jit(solution)/shard_map/ppermute | solution.py:123
  601.7 18.0 %collective-permute-done.72 = bf16[512,1024]{1,0:T(8,128)(2,1)} collective-permute-done((bf16[512,1024]{1,0:T(8,128)(2,1)S(1)}, bf16[512,1024]{1,0:T(8,128)(2,1)}, u32[]{:S(2)}, u32[]{:S(2)}) %collective-permute-start.72) | collective-permute-done | bytes 1048608 | tf_op jit(solution)/shard_map/ppermute | solution.py:123
  621.3 15.9 %collective-permute-done.74 = bf16[512,1024]{1,0:T(8,128)(2,1)} collective-permute-done((bf16[512,1024]{1,0:T(8,128)(2,1)}, bf16[512,1024]{1,0:T(8,128)(2,1)}, u32[]{:S(2)}, u32[]{:S(2)}) %collective-permute-start.74) | collective-permute-done | bytes 1048608 | tf_op jit(solution)/shard_map/ppermute | solution.py:123
  (474 shorter events, 287.5 us)
Async XLA Ops:
  151.3 26.1 %collective-permute-start.13 = (bf16[512,1024]{1,0:T(8,128)(2,1)S(1)}, bf16[512,1024]{1,0:T(8,128)(2,1)S(1)}, u32[]{:S(2)}, u32[]{:S(2)}) collective-permute-start(bf16[512,1024]{1,0:T(8,128)(2,1)S(1)} %fusion.39), channel_id=1, source_target_pairs={{0,8},{16,24},{8,0},{24,16},{1,9},{17,25},{9,1},{25,17},{2,10},{18... | collective-permute-start | bytes 3145736 | tf_op jit(solution)/shard_map/ppermute | solution.py:123
  181.1 24.4 %collective-permute-start.12 = (bf16[512,1024]{1,0:T(8,128)(2,1)S(1)}, bf16[512,1024]{1,0:T(8,128)(2,1)S(1)}, u32[]{:S(2)}, u32[]{:S(2)}) collective-permute-start(bf16[512,1024]{1,0:T(8,128)(2,1)S(1)} %fusion.42), channel_id=1, source_target_pairs={{0,8},{16,24},{8,0},{24,16},{1,9},{17,25},{9,1},{25,17},{2,10},{18... | collective-permute-start | bytes 3145736 | tf_op jit(solution)/shard_map/ppermute | solution.py:123
  221.3 37.0 %collective-permute-start.23 = (bf16[2,2,2,64,2048]{4,3,1,2,0:T(8,128)(2,1)S(1)}, bf16[2,2,2,64,2048]{4,3,1,2,0:T(8,128)(2,1)S(1)}, u32[]{:S(2)}, u32[]{:S(2)}) collective-permute-start(bf16[2,2,2,64,2048]{4,3,1,2,0:T(8,128)(2,1)S(1)} %get-tuple-element.154), channel_id=1, source_target_pairs={{0,1},{1,0},{2,3},{3,2},{4,5},{5,4},{6,7},{7,6},{8,9},{9,8},{10,11... | collective-permute-start | bytes 6291464 | tf_op jit(solution)/shard_map/ppermute | solution.py:36
  225.2 36.4 %collective-permute-start.11 = (bf16[512,1024]{1,0:T(8,128)(2,1)S(1)}, bf16[512,1024]{1,0:T(8,128)(2,1)S(1)}, u32[]{:S(2)}, u32[]{:S(2)}) collective-permute-start(bf16[512,1024]{1,0:T(8,128)(2,1)S(1)} %fusion.36), channel_id=1, source_target_pairs={{0,8},{16,24},{8,0},{24,16},{1,9},{17,25},{9,1},{25,17},{2,10},{18... | collective-permute-start | bytes 3145736 | tf_op jit(solution)/shard_map/ppermute | solution.py:123
  232.6 52.2 %collective-permute-start.29 = (bf16[512,1024]{1,0:T(8,128)(2,1)S(1)}, bf16[512,1024]{1,0:T(8,128)(2,1)}, u32[]{:S(2)}, u32[]{:S(2)}) collective-permute-start(bf16[512,1024]{1,0:T(8,128)(2,1)S(1)} %add_convert_fusion.19), channel_id=1, source_target_pairs={{8,16},{16,8},{9,17},{17,9},{10,18},{18,10},{11,19},{19,11},{12,20... | collective-permute-start | bytes 3145736 | tf_op jit(solution)/shard_map/ppermute | solution.py:123
  235.0 40.9 %collective-permute-start.27 = (bf16[512,1024]{1,0:T(8,128)(2,1)S(1)}, bf16[512,1024]{1,0:T(8,128)(2,1)S(1)}, u32[]{:S(2)}, u32[]{:S(2)}) collective-permute-start(bf16[512,1024]{1,0:T(8,128)(2,1)S(1)} %get-tuple-element.123), channel_id=1, source_target_pairs={{0,8},{16,24},{8,0},{24,16},{1,9},{17,25},{9,1},{25,17},{2,10},{18... | collective-permute-start | bytes 3145736 | tf_op jit(solution)/shard_map/ppermute | solution.py:123
  282.1 31.3 %collective-permute-start.31 = (bf16[512,2048]{1,0:T(8,128)(2,1)S(1)}, bf16[512,2048]{1,0:T(8,128)(2,1)S(1)}, u32[]{:S(2)}, u32[]{:S(2)}) collective-permute-start(bf16[512,2048]{1,0:T(8,128)(2,1)S(1)} %dynamic-slice_bitcast_fusion.1), channel_id=1, source_target_pairs={{0,1},{1,0},{2,3},{3,2},{4,5},{5,4},{6,7},{7,6},{8,9},{9,8},{10,11... | collective-permute-start | bytes 6291464 | tf_op jit(solution)/shard_map/ppermute | solution.py:36
  286.7 67.2 %collective-permute-start.30 = (bf16[512,1024]{1,0:T(8,128)(2,1)S(1)}, bf16[512,1024]{1,0:T(8,128)(2,1)S(1)}, u32[]{:S(2)}, u32[]{:S(2)}) collective-permute-start(bf16[512,1024]{1,0:T(8,128)(2,1)S(1)} %get-tuple-element.121), channel_id=1, source_target_pairs={{0,8},{16,24},{8,0},{24,16},{1,9},{17,25},{9,1},{25,17},{2,10},{18... | collective-permute-start | bytes 3145736 | tf_op jit(solution)/shard_map/ppermute | solution.py:123
  290.2 73.1 %collective-permute-start.28 = (bf16[768,512]{1,0:T(8,128)(2,1)S(1)}, bf16[768,512]{1,0:T(8,128)(2,1)S(1)}, u32[]{:S(2)}, u32[]{:S(2)}) collective-permute-start(bf16[768,512]{1,0:T(8,128)(2,1)S(1)} %slice.404), channel_id=1, source_target_pairs={{8,0},{16,8},{24,16},{9,1},{17,9},{25,17},{10,2},{18,10},{26,18},{... | collective-permute-start | bytes 2359304 | tf_op jit(solution)/shard_map/ppermute | solution.py:453
  292.3 23.0 %collective-permute-start.41 = (bf16[512,1024]{1,0:T(8,128)(2,1)S(1)}, bf16[512,1024]{1,0:T(8,128)(2,1)S(1)}, u32[]{:S(2)}, u32[]{:S(2)}) collective-permute-start(bf16[512,1024]{1,0:T(8,128)(2,1)S(1)} %add_convert_fusion.17), channel_id=1, source_target_pairs={{8,16},{16,8},{9,17},{17,9},{10,18},{18,10},{11,19},{19,11},{12,20... | collective-permute-start | bytes 3145736 | tf_op jit(solution)/shard_map/ppermute | solution.py:123
  295.3 67.9 %collective-permute-start.25 = (bf16[512,1024]{1,0:T(8,128)(2,1)S(1)}, bf16[512,1024]{1,0:T(8,128)(2,1)S(1)}, u32[]{:S(2)}, u32[]{:S(2)}) collective-permute-start(bf16[512,1024]{1,0:T(8,128)(2,1)S(1)} %get-tuple-element.125), channel_id=1, source_target_pairs={{0,8},{16,24},{8,0},{24,16},{1,9},{17,25},{9,1},{25,17},{2,10},{18... | collective-permute-start | bytes 3145736 | tf_op jit(solution)/shard_map/ppermute | solution.py:123
  315.3 38.5 %collective-permute-start.33 = (bf16[2,64,2048]{2,1,0:T(8,128)(2,1)S(1)}, bf16[2,64,2048]{2,1,0:T(8,128)(2,1)S(1)}, u32[]{:S(2)}, u32[]{:S(2)}) collective-permute-start(bf16[2,64,2048]{2,1,0:T(8,128)(2,1)S(1)} %dynamic-slice_bitcast_fusion.6), channel_id=1, source_target_pairs={{0,4},{1,5},{2,6},{3,7},{4,0},{5,1},{6,2},{7,3},{8,12},{9,13},{10,... | collective-permute-start | bytes 1572872 | tf_op jit(solution)/shard_map/ppermute | solution.py:36
  326.9 94.9 %collective-permute-start.42 = (bf16[512,1024]{1,0:T(8,128)(2,1)S(1)}, bf16[512,1024]{1,0:T(8,128)(2,1)S(1)}, u32[]{:S(2)}, u32[]{:S(2)}) collective-permute-start(bf16[512,1024]{1,0:T(8,128)(2,1)S(1)} %get-tuple-element.119), channel_id=1, source_target_pairs={{0,8},{16,24},{8,0},{24,16},{1,9},{17,25},{9,1},{25,17},{2,10},{18... | collective-permute-start | bytes 3145736 | tf_op jit(solution)/shard_map/ppermute | solution.py:123
  371.6 49.4 %collective-permute-start.43 = (bf16[512,2048]{1,0:T(8,128)(2,1)S(1)}, bf16[512,2048]{1,0:T(8,128)(2,1)S(1)}, u32[]{:S(2)}, u32[]{:S(2)}) collective-permute-start(bf16[512,2048]{1,0:T(8,128)(2,1)S(1)} %dynamic-slice_bitcast_fusion), channel_id=1, source_target_pairs={{0,1},{1,0},{2,3},{3,2},{4,5},{5,4},{6,7},{7,6},{8,9},{9,8},{10,11... | collective-permute-start | bytes 6291464 | tf_op jit(solution)/shard_map/ppermute | solution.py:36
  372.9 27.5 %collective-permute-start.46 = (bf16[512,1024]{1,0:T(8,128)(2,1)S(1)}, bf16[512,1024]{1,0:T(8,128)(2,1)S(1)}, u32[]{:S(2)}, u32[]{:S(2)}) collective-permute-start(bf16[512,1024]{1,0:T(8,128)(2,1)S(1)} %add_convert_fusion.13), channel_id=1, source_target_pairs={{8,16},{16,8},{9,17},{17,9},{10,18},{18,10},{11,19},{19,11},{12,20... | collective-permute-start | bytes 3145736 | tf_op jit(solution)/shard_map/ppermute | solution.py:123
  380.5 61.6 %collective-permute-start.49 = (bf16[512,1024]{1,0:T(8,128)(2,1)S(1)}, bf16[512,1024]{1,0:T(8,128)(2,1)S(1)}, u32[]{:S(2)}, u32[]{:S(2)}) collective-permute-start(bf16[512,1024]{1,0:T(8,128)(2,1)S(1)} %get-tuple-element.113), channel_id=1, source_target_pairs={{0,8},{16,24},{8,0},{24,16},{1,9},{17,25},{9,1},{25,17},{2,10},{18... | collective-permute-start | bytes 3145736 | tf_op jit(solution)/shard_map/ppermute | solution.py:123
  402.6 68.8 %collective-permute-start.47 = (bf16[512,1024]{1,0:T(8,128)(2,1)}, bf16[512,1024]{1,0:T(8,128)(2,1)S(1)}, u32[]{:S(2)}, u32[]{:S(2)}) collective-permute-start(bf16[512,1024]{1,0:T(8,128)(2,1)} %get-tuple-element.115), channel_id=1, source_target_pairs={{0,8},{16,24},{8,0},{24,16},{1,9},{17,25},{9,1},{25,17},{2,10},{18... | collective-permute-start | bytes 3145736 | tf_op jit(solution)/shard_map/ppermute | solution.py:123
  425.7 48.2 %collective-permute-start.44 = (bf16[512,1024]{1,0:T(8,128)(2,1)}, bf16[512,1024]{1,0:T(8,128)(2,1)}, u32[]{:S(2)}, u32[]{:S(2)}) collective-permute-start(bf16[512,1024]{1,0:T(8,128)(2,1)} %add_convert_fusion.15), channel_id=1, source_target_pairs={{8,16},{16,8},{9,17},{17,9},{10,18},{18,10},{11,19},{19,11},{12,20... | collective-permute-start | bytes 3145736 | tf_op jit(solution)/shard_map/ppermute | solution.py:123
  463.2 36.9 %collective-permute-start.64 = (bf16[512,1024]{1,0:T(8,128)(2,1)}, bf16[512,1024]{1,0:T(8,128)(2,1)}, u32[]{:S(2)}, u32[]{:S(2)}) collective-permute-start(bf16[512,1024]{1,0:T(8,128)(2,1)} %add_convert_fusion.7), channel_id=1, source_target_pairs={{8,16},{16,8},{9,17},{17,9},{10,18},{18,10},{11,19},{19,11},{12,20... | collective-permute-start | bytes 3145736 | tf_op jit(solution)/shard_map/ppermute | solution.py:123
  471.4 53.8 %collective-permute-start.66 = (f32[108,128]{1,0:T(8,128)S(1)}, f32[108,128]{1,0:T(8,128)S(1)}, u32[]{:S(2)}, u32[]{:S(2)}) collective-permute-start(f32[108,128]{1,0:T(8,128)S(1)} %maximum_bitcast_fusion.3), channel_id=1, source_target_pairs={{0,8},{16,24},{8,0},{24,16},{1,9},{17,25},{9,1},{25,17},{2,10},{18... | collective-permute-start | bytes 165896 | tf_op jit(solution)/shard_map/ppermute | solution.py:123
  472.4 24.1 %collective-permute-start.56 = (bf16[2,64,2048]{2,1,0:T(8,128)(2,1)S(1)}, bf16[2,64,2048]{2,1,0:T(8,128)(2,1)S(1)}, u32[]{:S(2)}, u32[]{:S(2)}) collective-permute-start(bf16[2,64,2048]{2,1,0:T(8,128)(2,1)S(1)} %maximum_select_fusion.22), channel_id=1, source_target_pairs={{0,2},{1,3},{2,0},{3,1},{4,6},{5,7},{6,4},{7,5},{8,10},{9,11},{10,... | collective-permute-start | bytes 1572872 | tf_op jit(solution)/shard_map/ppermute | solution.py:36
  496.6 27.1 %collective-permute-start.45 = (bf16[512,1024]{1,0:T(8,128)(2,1)S(1)}, bf16[512,1024]{1,0:T(8,128)(2,1)S(1)}, u32[]{:S(2)}, u32[]{:S(2)}) collective-permute-start(bf16[512,1024]{1,0:T(8,128)(2,1)S(1)} %get-tuple-element.117), channel_id=1, source_target_pairs={{0,8},{16,24},{8,0},{24,16},{1,9},{17,25},{9,1},{25,17},{2,10},{18... | collective-permute-start | bytes 3145736 | tf_op jit(solution)/shard_map/ppermute | solution.py:123
  499.9 71.0 %collective-permute-start.40 = (bf16[2,2,2,64,2048]{4,3,0,1,2:T(8,128)(2,1)S(1)}, bf16[2,2,2,64,2048]{4,3,0,1,2:T(8,128)(2,1)S(1)}, u32[]{:S(2)}, u32[]{:S(2)}) collective-permute-start(bf16[2,2,2,64,2048]{4,3,0,1,2:T(8,128)(2,1)S(1)} %get-tuple-element.150), channel_id=1, source_target_pairs={{0,1},{1,0},{2,3},{3,2},{4,5},{5,4},{6,7},{7,6},{8,9},{9,8},{10,11... | collective-permute-start | bytes 6291464 | tf_op jit(solution)/shard_map/ppermute | solution.py:36
  503.1 43.1 %collective-permute-start.65 = (bf16[512,1024]{1,0:T(8,128)(2,1)S(1)}, bf16[512,1024]{1,0:T(8,128)(2,1)S(1)}, u32[]{:S(2)}, u32[]{:S(2)}) collective-permute-start(bf16[512,1024]{1,0:T(8,128)(2,1)S(1)} %get-tuple-element.111), channel_id=1, source_target_pairs={{0,8},{16,24},{8,0},{24,16},{1,9},{17,25},{9,1},{25,17},{2,10},{18... | collective-permute-start | bytes 3145736 | tf_op jit(solution)/shard_map/ppermute | solution.py:123
  503.7 60.9 %collective-permute-start.68 = (bf16[512,1024]{1,0:T(8,128)(2,1)S(1)}, bf16[512,1024]{1,0:T(8,128)(2,1)S(1)}, u32[]{:S(2)}, u32[]{:S(2)}) collective-permute-start(bf16[512,1024]{1,0:T(8,128)(2,1)S(1)} %broadcast_select_fusion), channel_id=1, source_target_pairs={{0,8},{16,24},{8,0},{24,16},{1,9},{17,25},{9,1},{25,17},{2,10},{18... | collective-permute-start | bytes 3145736 | tf_op jit(solution)/shard_map/ppermute | solution.py:123
  524.0 45.5 %collective-permute-start.59 = (bf16[512,1024]{1,0:T(8,128)(2,1)S(1)}, bf16[512,1024]{1,0:T(8,128)(2,1)S(1)}, u32[]{:S(2)}, u32[]{:S(2)}) collective-permute-start(bf16[512,1024]{1,0:T(8,128)(2,1)S(1)} %add_convert_fusion.9), channel_id=1, source_target_pairs={{8,16},{16,8},{9,17},{17,9},{10,18},{18,10},{11,19},{19,11},{12,20... | collective-permute-start | bytes 3145736 | tf_op jit(solution)/shard_map/ppermute | solution.py:123
  525.3 52.7 %collective-permute-start.58 = (bf16[2,2,2,64,2048]{4,3,0,1,2:T(8,128)(2,1)S(1)}, bf16[2,2,2,64,2048]{4,3,0,1,2:T(8,128)(2,1)S(1)}, u32[]{:S(2)}, u32[]{:S(2)}) collective-permute-start(bf16[2,2,2,64,2048]{4,3,0,1,2:T(8,128)(2,1)S(1)} %get-tuple-element.146), channel_id=1, source_target_pairs={{0,1},{1,0},{2,3},{3,2},{4,5},{5,4},{6,7},{7,6},{8,9},{9,8},{10,11... | collective-permute-start | bytes 6291464 | tf_op jit(solution)/shard_map/ppermute | solution.py:36
  550.9 25.2 %collective-permute-start.71 = (bf16[512,1024]{1,0:T(8,128)(2,1)S(1)}, bf16[512,1024]{1,0:T(8,128)(2,1)S(1)}, u32[]{:S(2)}, u32[]{:S(2)}) collective-permute-start(bf16[512,1024]{1,0:T(8,128)(2,1)S(1)} %add_convert_fusion.3), channel_id=1, source_target_pairs={{8,16},{16,8},{9,17},{17,9},{10,18},{18,10},{11,19},{19,11},{12,20... | collective-permute-start | bytes 3145736 | tf_op jit(solution)/shard_map/ppermute | solution.py:123
  565.8 31.5 %collective-permute-start.70 = (f32[108,128]{1,0:T(8,128)S(1)}, f32[108,128]{1,0:T(8,128)S(1)}, u32[]{:S(2)}, u32[]{:S(2)}) collective-permute-start(f32[108,128]{1,0:T(8,128)S(1)} %fusion.149), channel_id=1, source_target_pairs={{0,8},{16,24},{8,0},{24,16},{1,9},{17,25},{9,1},{25,17},{2,10},{18... | collective-permute-start | bytes 165896 | tf_op jit(solution)/shard_map/ppermute | solution.py:123
  570.9 26.5 %collective-permute-start.60 = (bf16[512,1024]{1,0:T(8,128)(2,1)S(1)}, bf16[512,1024]{1,0:T(8,128)(2,1)S(1)}, u32[]{:S(2)}, u32[]{:S(2)}) collective-permute-start(bf16[512,1024]{1,0:T(8,128)(2,1)S(1)} %add_convert_fusion.8), channel_id=1, source_target_pairs={{0,8},{16,24},{8,0},{24,16},{1,9},{17,25},{9,1},{25,17},{2,10},{18... | collective-permute-start | bytes 3145736 | tf_op jit(solution)/shard_map/ppermute | solution.py:123
  576.5 43.2 %collective-permute-start.72 = (bf16[512,1024]{1,0:T(8,128)(2,1)S(1)}, bf16[512,1024]{1,0:T(8,128)(2,1)}, u32[]{:S(2)}, u32[]{:S(2)}) collective-permute-start(bf16[512,1024]{1,0:T(8,128)(2,1)S(1)} %add_convert_fusion.2), channel_id=1, source_target_pairs={{0,8},{16,24},{8,0},{24,16},{1,9},{17,25},{9,1},{25,17},{2,10},{18... | collective-permute-start | bytes 3145736 | tf_op jit(solution)/shard_map/ppermute | solution.py:123
  582.3 54.9 %collective-permute-start.74 = (bf16[512,1024]{1,0:T(8,128)(2,1)}, bf16[512,1024]{1,0:T(8,128)(2,1)}, u32[]{:S(2)}, u32[]{:S(2)}) collective-permute-start(bf16[512,1024]{1,0:T(8,128)(2,1)} %add_convert_fusion), channel_id=1, source_target_pairs={{0,8},{16,24},{8,0},{24,16},{1,9},{17,25},{9,1},{25,17},{2,10},{18... | collective-permute-start | bytes 3145736 | tf_op jit(solution)/shard_map/ppermute | solution.py:123
  (123 other events, 1543.2 us)

commit v4 on v3

--- a/solution.py
+++ b/solution.py
@@ -176,9 +176,12 @@
         held, got = self.pair(k)
         return held if held is got else jnp.where(self.line.depth == 0, got, held)
 
-    def tiles(self, start, stop, per_row):
-        held, got = zip(*[self.pair(k) for k in range(start, stop)])
-        return tiled(self.edge(), held, got, per_row)
+    def tiles(self, which, count, per_row):
+        held, got = zip(*[self.pair(k) for k in which])
+        return tiled(self.edge(), held, got, count, per_row)
+
+    def last_tile(self, k, others):
+        return tiled(self.edge(), *[[value] for value in self.pair(k)], 4, 1, others)
 
     def start(self, kind, slot):
         plan = self.line.swaps(kind, slot, self.count)
@@ -339,19 +342,33 @@
                 out_ref[...] = part[...].astype(f32)
 
 
-def tiled(edge, held, got, per_row):
+def tiled(edge, held, got, count, per_row, others=None):
     rows, cols = held[0].shape
     parts = list(held) + list(got)
+    first = 0 if others is None else count - len(held)
     whole = pl.BlockSpec((rows, cols), lambda i: (0, 0), pipeline_mode=pl.Buffered(1))
+    specs = [pl.BlockSpec(memory_space=pltpu.SMEM)] + [whole for _ in parts]
+    args = [edge] + parts
+    kernel = tile_kernel
+    if others is not None:
+        specs.append(pl.BlockSpec(memory_space=pl.ANY))
+        args.append(others)
+
+        def kernel(*refs):
+            tile_kernel(*refs[:-2], refs[-1])
+
     return pl.pallas_call(
-        tile_kernel,
+        kernel,
         grid=(len(held),),
-        in_specs=[pl.BlockSpec(memory_space=pltpu.SMEM)] + [whole for _ in parts],
-        out_specs=pl.BlockSpec((rows, cols), lambda i: (i // per_row, i % per_row)),
-        out_shape=jax.ShapeDtypeStruct((len(held) // per_row * rows, per_row * cols), f32),
+        in_specs=specs,
+        out_specs=pl.BlockSpec(
+            (rows, cols), lambda i: ((i + first) // per_row, (i + first) % per_row)
+        ),
+        out_shape=jax.ShapeDtypeStruct((count // per_row * rows, per_row * cols), f32),
+        input_output_aliases={} if others is None else {len(args) - 1: 0},
         compiler_params=pltpu.CompilerParams(vmem_limit_bytes=16 << 20),
         name="tiled",
-    )(edge, *parts)
+    )(*args)
 
 
 def on_device(
@@ -425,17 +442,19 @@
         part = dot(active[:, i : i + step], cotangent[:, j : j + hidden], ((0,), (0,)))
         bulk.feed(part.astype(bf16))
     bulk.begin()
-    for i in range(4):
-        bulk.feed(
-            dot(normed_two[:, i * step : (i + 1) * step], grad_upper, ((0,), (0,))).astype(bf16)
-        )
+    ups = [
+        dot(normed_two[:, i * step : (i + 1) * step], grad_upper, ((0,), (0,))).astype(bf16)
+        for i in range(4)
+    ]
+    for part in ups[:3]:
+        bulk.feed(part)
     grad_b_up = jnp.sum(grad_upper.astype(f32), axis=0)
     back_part = dot(grad_upper, w_up, ((1,), (1,))).astype(bf16)
-    grad_norm_two = reduce_rows(back_part, at_calls(bulk.sync, 1)).astype(f32)
+    grad_norm_two = reduce_rows(back_part, at_calls(bulk.sync, 0, 2)).astype(f32)
     grad_resid, grad_ln2_gain, grad_ln2_bias = norm_back(grad_norm_two, raw_two, inv_two, ln2_gain)
     grad_out_rows = rows_of(cotangent).astype(f32)
     grad_mid = grad_out_rows + grad_resid
-    grad_mid_low = gather_rows(grad_mid.astype(bf16), at_calls(bulk.sync, 0))
+    grad_mid_low = gather_rows(grad_mid.astype(bf16), at_calls(bulk.sync, 1))
     grad_attended = dot(grad_mid_low, w_out, ((1,), (1,))).astype(bf16)
     bulk.feed(
         jnp.concatenate(
@@ -445,7 +464,6 @@
             ]
         ),
     )
-    (grad_attended,) = bulk.sync(grad_attended)
     grad_query, grad_keys, grad_vals = attend_back(
         query, keys_vals, grad_attended, pos, valid_windows
     )
@@ -454,7 +472,7 @@
     own = grad_kv[MAX_DOCUMENT:]
     own, active = bulk.sync(own, active)
     mlp_part = dot(active, w_down, ((1,), (0,))).astype(bf16)
-    mlp_total = reduce_rows(mlp_part, at_calls(bulk.sync, 1)).astype(f32)
+    mlp_total = reduce_rows(mlp_part, at_calls(bulk.sync, 0)).astype(f32)
     own, got, mlp_total = bulk.sync(own, got, mlp_total)
     low = rows - MAX_DOCUMENT
     grad_kv = jnp.concatenate([own[:low], own[low:] + got.astype(f32)]).astype(bf16)
@@ -467,6 +485,7 @@
     for i in range(3):
         extra = rest[:, i * local_width : (i + 1) * local_width]
         bulk.feed(jnp.concatenate([parts[i], extra], axis=1))
+    bulk.feed(ups[3])
     grad_b_qv = jnp.sum(grad_mixed.astype(f32), axis=0)
     grad_b_qv = [grad_b_qv[i * local_width : (i + 1) * local_width] for i in (0, 2)]
     back_part = dot(grad_mixed, w_flat, ((1,), (1,))).astype(bf16)
@@ -499,14 +518,14 @@
     grad_b_up = sums[6 * width : 6 * width + hidden]
     grad_b_qv = sums[6 * width + hidden :].reshape(2, local_width)
 
-    done = [None] * 8 + [bulk.result(k).astype(f32) for k in range(8, 12)]
+    done = [bulk.result(k).astype(f32) for k in range(7, 11)]
     per_row = width // hidden
-    grad_w_down = bulk.tiles(0, 4, per_row)
-    grad_w_up = bulk.tiles(4, 8, 1)
+    grad_w_down = bulk.tiles(range(4), 4, per_row)
+    grad_w_up = bulk.last_tile(11, bulk.tiles(range(4, 7), 4, 1))
     grad_w_out = jnp.concatenate(
-        [done[8][i * local_width : (i + 1) * local_width] for i in range(per_row)], axis=1
-    )
-    mixed_done = done[9:12]
+        [done[0][i * local_width : (i + 1) * local_width] for i in range(per_row)], axis=1
+    )
+    mixed_done = done[1:4]
     grad_w_qkv = jnp.stack(
         [
             jnp.concatenate(

time: 651 us -> 620 us (0.952)
  starting transfers between devices: 223 us -> 188 us
    ppermute x30, starting transfers between devices: 170 us -> 146 us  [exchange(): return lax.ppermute(value, 'wide', pairs + [(b, a) for a, b in pairs])]
    ppermute x30, waiting for transfers between devices: 85.1 us -> 72.8 us  [exchange(): return lax.ppermute(value, 'wide', pairs + [(b, a) for a, b in pairs])]
    ppermute x43, waiting for transfers between devices: 111 us -> 123 us  [swap(): lax.ppermute(value, 'narrow', [(i, i ^ 1 << bit) for i in range(count)])]
    ppermute x43, starting transfers between devices: 45.3 us -> 34.7 us  [swap(): lax.ppermute(value, 'narrow', [(i, i ^ 1 << bit) for i in range(count)])]
    select_n x19 -> x21, other arithmetic: 16.1 us -> 13.2 us  [pair(): jnp.where(narrow_bit(bit) == 0, jnp.stack([value, other], axis=dim), jnp....]
    unnamed x162 -> x152, local copies, waits for them, and re-layouts: 23.7 us -> 23.7 us
  transfers between devices with their start and end apart: 75 -> 75, of which waited for: 34 -> 38; matrix products, arithmetic and copies ran while one was open for 18% -> 20% of each run, Pallas kernels for 3% -> 3%
where the time goes in v4:
time: 620 us; the launch traced here: 611 us
  waiting for transfers between devices  198 us (32%)
  starting transfers between devices  188 us (30%)
  other arithmetic  84 us (14%)
  matrix products  62.8 us (10%)
  local copies, waits for them, and re-layouts  47.3 us (8%)
  Pallas kernels  28.1 us (5%)
    ppermute x30, starting transfers between devices, exchange(): return lax.ppermute(value, 'wide', pairs + [(b, a) for a, b in pairs])  146 us
    ppermute x43, waiting for transfers between devices, swap(): lax.ppermute(value, 'narrow', [(i, i ^ 1 << bit) for i in range(count)])  123 us
    ppermute x30, waiting for transfers between devices, exchange(): return lax.ppermute(value, 'wide', pairs + [(b, a) for a, b in pairs])  72.8 us
    dot_general x23, matrix products, dot(): return lax.dot_general(a, b, (dims, ((), ())), preferred_element_type=f32)  62.8 us
    ppermute x43, starting transfers between devices, swap(): lax.ppermute(value, 'narrow', [(i, i ^ 1 << bit) for i in range(count)])  34.7 us
    unnamed x152, local copies, waits for them, and re-layouts  23.7 us
    convert_element_type x35, other arithmetic, add_low(): return (a.astype(f32) + b.astype(f32)).astype(a.dtype)  20.1 us
    select_n x21, other arithmetic, pair(): jnp.where(narrow_bit(bit) == 0, jnp.stack([value, other], axis=dim), jnp....  13.2 us
  transfers between devices with their start and end apart: 75, of which 38 were waited for; matrix products, arithmetic and copies ran while one was open for 20% of the time, Pallas kernels for 3%

profile of v4, /device:TPU:0, one launch (start us, length us, event | category | flops | bytes accessed | tf_op | source)
XLA Modules:
  0.0 611.2 jit_solution(17787488410108262877)
XLA Ops:
  17.0 5.8 collective-permute-start
  28.6 9.4 %convolution_convert_fusion.4 = bf16[1024,1024]{1,0:T(8,128)(2,1)} fusion(bf16[1024,2048]{1,0:T(8,128)(2,1)} %param.32, bf16[1024,2048]{1,0:T(8,128)(2,1)} %param.28), kind=kOutput, calls=%fused_computation.85 | convolution fusion | flops 4296015872 | bytes 10485760 | tf_op jit(solution)/shard_map/dot_general | solution.py:254
  40.0 7.8 %attend.1 = bf16[1024,256]{1,0:T(8,128)(2,1)S(1)} custom-call(bf16[1024,256]{1,0:T(8,128)(2,1)S(1)} %copy-done.5, bf16[1792,512]{1,0:T(8,128)(2,1)S(1)} %pad_maximum_fusion.6.k_ref.v_ref, bf16[1792,512]{1,0:T(8,128)(2,1)S(1)} %pad_maximum_fusion.6.k_ref.v_ref, s32[1024,1]{1,0:T(8,128)S(1)} %copy.58.pos_ref, s32[4,1,1024]{2,1,0:T(1,128)S(1)} %reshape.1072.valid_ref), custom_call_target="tpu_custom_call" | custom-call | tf_op jit(solution)/shard_map/attend/pallas_call | solution.py:307
  66.5 10.0 %collective-permute-done.2 = bf16[2,64,2048]{2,1,0:T(8,128)(2,1)} collective-permute-done((bf16[2,64,2048]{2,1,0:T(8,128)(2,1)}, bf16[2,64,2048]{2,1,0:T(8,128)(2,1)}, u32[]{:S(2)}, u32[]{:S(2)}) %collective-permute-start.2) | collective-permute-done | bytes 524320 | tf_op jit(solution)/shard_map/ppermute | solution.py:36
  106.2 5.2 collective-permute-done.7
  129.7 7.8 %convert_reduce_fusion.1 = (f32[1024]{0:T(1024)S(1)}, bf16[1024,1024]{1,0:T(8,128)(2,1)S(1)}, bf16[1024,1024]{1,0:T(8,128)(2,1)S(1)}) fusion(f32[1024]{0:T(1024)S(1)} %copy-done.70, bf16[1024,1024]{1,0:T(8,128)(2,1)S(1)} %copy-done.74, bf16[1024,2048]{1,0:T(8,128)(2,1)S(1)} %bitcast.287, bf16[2048,1024]{1,0:T(8,128)(2,1)S(1)} %copy-done.68), kind=kOutput, calls=%fused_computation.35 | convolution fusion | flops 4322229248 | bytes 14688256 | tf_op jit(solution)/shard_map/dot_general | solution.py:254
  137.5 5.0 convolution_convert_fusion.3
  157.7 18.4 %collective-permute-done.13 = bf16[512,1024]{1,0:T(8,128)(2,1)} collective-permute-done((bf16[512,1024]{1,0:T(8,128)(2,1)}, bf16[512,1024]{1,0:T(8,128)(2,1)}, u32[]{:S(2)}, u32[]{:S(2)}) %collective-permute-start.13) | collective-permute-done | bytes 1048608 | tf_op jit(solution)/shard_map/ppermute | solution.py:123
  180.2 9.0 %collective-permute-done.17 = bf16[2,64,2048]{2,1,0:T(8,128)(2,1)S(1)} collective-permute-done((bf16[2,64,2048]{2,1,0:T(8,128)(2,1)S(1)}, bf16[2,64,2048]{2,1,0:T(8,128)(2,1)S(1)}, u32[]{:S(2)}, u32[]{:S(2)}) %collective-permute-start.17) | collective-permute-done | bytes 524320 | tf_op jit(solution)/shard_map/ppermute | solution.py:36
  217.1 6.6 %collective-permute-done.22 = bf16[2,64,2048]{2,1,0:T(8,128)(2,1)S(1)} collective-permute-done((bf16[2,64,2048]{2,1,0:T(8,128)(2,1)S(1)}, bf16[2,64,2048]{2,1,0:T(8,128)(2,1)S(1)}, u32[]{:S(2)}, u32[]{:S(2)}) %collective-permute-start.22) | collective-permute-done | bytes 524320 | tf_op jit(solution)/shard_map/ppermute | solution.py:36
  224.6 5.3 collective-permute-done.11
  239.1 24.6 %collective-permute-start.26 = (bf16[512,1024]{1,0:T(8,128)(2,1)S(1)}, bf16[512,1024]{1,0:T(8,128)(2,1)S(1)}, u32[]{:S(2)}, u32[]{:S(2)}) collective-permute-start(bf16[512,1024]{1,0:T(8,128)(2,1)S(1)} %get-tuple-element.119), channel_id=1, source_target_pairs={{0,8},{16,24},{8,0},{24,16},{1,9},{17,25},{9,1},{25,17},{2,10},{18... | collective-permute-start | bytes 3145736 | tf_op jit(solution)/shard_map/ppermute | solution.py:123
  267.5 12.2 %attend_back.1 = (bf16[1024,256]{1,0:T(8,128)(2,1)S(1)}, f32[1792,256]{1,0:T(8,128)S(1)}, f32[1792,256]{1,0:T(8,128)S(1)}) custom-call(bf16[1024,256]{1,0:T(8,128)(2,1)S(1)} %copy-done.6, bf16[1792,512]{1,0:T(8,128)(2,1)S(1)} %pad_maximum_fusion.6.k_ref.v_ref, bf16[1792,512]{1,0:T(8,128)(2,1)S(1)} %pad_maximum_fusion.6.k_ref.v_ref, ...), custom_call_target="tpu_custom_call" | custom-call | tf_op jit(solution)/shard_map/attend_back/pallas_call | solution.py:323
  280.5 5.7 collective-permute-done.26.refs_4_
  286.2 4.8 convolution_convert_fusion.2
  298.7 10.0 %collective-permute-start.24 = (bf16[512,1024]{1,0:T(8,128)(2,1)S(1)}, bf16[512,1024]{1,0:T(8,128)(2,1)S(1)}, u32[]{:S(2)}, u32[]{:S(2)}) collective-permute-start(bf16[512,1024]{1,0:T(8,128)(2,1)S(1)} %get-tuple-element.121), channel_id=1, source_target_pairs={{0,8},{16,24},{8,0},{24,16},{1,9},{17,25},{9,1},{25,17},{2,10},{18... | collective-permute-start | bytes 3145736 | tf_op jit(solution)/shard_map/ppermute | solution.py:123
  312.4 18.8 %collective-permute-start.42 = (bf16[512,1024]{1,0:T(8,128)(2,1)S(1)}, bf16[512,1024]{1,0:T(8,128)(2,1)S(1)}, u32[]{:S(2)}, u32[]{:S(2)}) collective-permute-start(bf16[512,1024]{1,0:T(8,128)(2,1)S(1)} %get-tuple-element.115), channel_id=1, source_target_pairs={{0,8},{16,24},{8,0},{24,16},{1,9},{17,25},{9,1},{25,17},{2,10},{18... | collective-permute-start | bytes 3145736 | tf_op jit(solution)/shard_map/ppermute | solution.py:123
  334.6 10.4 %collective-permute-done.32 = bf16[2,64,2048]{2,1,0:T(8,128)(2,1)S(1)} collective-permute-done((bf16[2,64,2048]{2,1,0:T(8,128)(2,1)S(1)}, bf16[2,64,2048]{2,1,0:T(8,128)(2,1)S(1)}, u32[]{:S(2)}, u32[]{:S(2)}) %collective-permute-start.32) | collective-permute-done | bytes 524320 | tf_op jit(solution)/shard_map/ppermute | solution.py:36
  346.8 5.6 collective-permute-done.33
  353.3 5.4 collective-permute-done.35
  375.9 4.9 collective-permute-start.49
  382.8 19.1 %collective-permute-start.47 = (bf16[512,1024]{1,0:T(8,128)(2,1)}, bf16[512,1024]{1,0:T(8,128)(2,1)S(1)}, u32[]{:S(2)}, u32[]{:S(2)}) collective-permute-start(bf16[512,1024]{1,0:T(8,128)(2,1)} %get-tuple-element.111), channel_id=1, source_target_pairs={{0,8},{16,24},{8,0},{24,16},{1,9},{17,25},{9,1},{25,17},{2,10},{18... | collective-permute-start | bytes 3145736 | tf_op jit(solution)/shard_map/ppermute | solution.py:123
  434.9 5.8 collective-permute-done.62
  462.2 4.9 collective-permute-done.57
  468.2 8.4 %collective-permute-done.39 = bf16[2,64,2048]{2,1,0:T(8,128)(2,1)S(1)} collective-permute-done((bf16[2,64,2048]{2,1,0:T(8,128)(2,1)S(1)}, bf16[2,64,2048]{2,1,0:T(8,128)(2,1)S(1)}, u32[]{:S(2)}, u32[]{:S(2)}) %collective-permute-start.39) | collective-permute-done | bytes 524320 | tf_op jit(solution)/shard_map/ppermute | solution.py:36
  485.3 6.1 collective-permute-done.45.refs_5_
  493.9 11.6 %collective-permute-start.68 = (bf16[512,1024]{1,0:T(8,128)(2,1)S(1)}, bf16[512,1024]{1,0:T(8,128)(2,1)S(1)}, u32[]{:S(2)}, u32[]{:S(2)}) collective-permute-start(bf16[512,1024]{1,0:T(8,128)(2,1)S(1)} %get-tuple-element.196), channel_id=1, source_target_pairs={{0,8},{16,24},{8,0},{24,16},{1,9},{17,25},{9,1},{25,17},{2,10},{18... | collective-permute-start | bytes 3145736 | tf_op jit(solution)/shard_map/ppermute | solution.py:123
  520.7 14.4 %collective-permute-done.68 = bf16[512,1024]{1,0:T(8,128)(2,1)S(1)} collective-permute-done((bf16[512,1024]{1,0:T(8,128)(2,1)S(1)}, bf16[512,1024]{1,0:T(8,128)(2,1)S(1)}, u32[]{:S(2)}, u32[]{:S(2)}) %collective-permute-start.68) | collective-permute-done | bytes 1048608 | tf_op jit(solution)/shard_map/ppermute | solution.py:123
  547.5 13.4 %collective-permute-start.72 = (bf16[512,1024]{1,0:T(8,128)(2,1)}, bf16[512,1024]{1,0:T(8,128)(2,1)}, u32[]{:S(2)}, u32[]{:S(2)}) collective-permute-start(bf16[512,1024]{1,0:T(8,128)(2,1)} %add_convert_fusion.2), channel_id=1, source_target_pairs={{0,8},{16,24},{8,0},{24,16},{1,9},{17,25},{9,1},{25,17},{2,10},{18... | collective-permute-start | bytes 3145736 | tf_op jit(solution)/shard_map/ppermute | solution.py:123
  564.3 13.9 %collective-permute-start.74 = (bf16[512,1024]{1,0:T(8,128)(2,1)S(1)}, bf16[512,1024]{1,0:T(8,128)(2,1)S(1)}, u32[]{:S(2)}, u32[]{:S(2)}) collective-permute-start(bf16[512,1024]{1,0:T(8,128)(2,1)S(1)} %add_convert_fusion.refs_1_), channel_id=1, source_target_pairs={{0,8},{16,24},{8,0},{24,16},{1,9},{17,25},{9,1},{25,17},{2,10},{18... | collective-permute-start | bytes 3145736 | tf_op jit(solution)/shard_map/ppermute | solution.py:123
  582.6 8.9 %collective-permute-done.72 = bf16[512,1024]{1,0:T(8,128)(2,1)} collective-permute-done((bf16[512,1024]{1,0:T(8,128)(2,1)}, bf16[512,1024]{1,0:T(8,128)(2,1)}, u32[]{:S(2)}, u32[]{:S(2)}) %collective-permute-start.72) | collective-permute-done | bytes 1048608 | tf_op jit(solution)/shard_map/ppermute | solution.py:123
  599.5 9.6 %collective-permute-done.74.refs_2_ = bf16[512,1024]{1,0:T(8,128)(2,1)S(1)} collective-permute-done((bf16[512,1024]{1,0:T(8,128)(2,1)S(1)}, bf16[512,1024]{1,0:T(8,128)(2,1)S(1)}, u32[]{:S(2)}, u32[]{:S(2)}) %collective-permute-start.74) | collective-permute-done | bytes 1048608 | tf_op jit(solution)/shard_map/ppermute | solution.py:123
  (466 shorter events, 299.3 us)
Async XLA Ops:
  17.0 21.7 %collective-permute-start = (bf16[768,512]{1,0:T(8,128)(2,1)S(1)}, bf16[768,512]{1,0:T(8,128)(2,1)}, u32[]{:S(2)}, u32[]{:S(2)}) collective-permute-start(bf16[768,512]{1,0:T(8,128)(2,1)S(1)} %slice.282), channel_id=1, source_target_pairs={{0,8},{8,16},{16,24},{1,9},{9,17},{17,25},{2,10},{10,18},{18,26},{... | collective-permute-start | bytes 2359304 | tf_op jit(solution)/shard_map/ppermute | solution.py:420
  149.2 26.9 %collective-permute-start.13 = (bf16[512,1024]{1,0:T(8,128)(2,1)}, bf16[512,1024]{1,0:T(8,128)(2,1)}, u32[]{:S(2)}, u32[]{:S(2)}) collective-permute-start(bf16[512,1024]{1,0:T(8,128)(2,1)} %fusion.39), channel_id=1, source_target_pairs={{0,8},{16,24},{8,0},{24,16},{1,9},{17,25},{9,1},{25,17},{2,10},{18... | collective-permute-start | bytes 3145736 | tf_op jit(solution)/shard_map/ppermute | solution.py:123
  155.1 46.1 %collective-permute-start.12 = (bf16[512,1024]{1,0:T(8,128)(2,1)S(1)}, bf16[512,1024]{1,0:T(8,128)(2,1)S(1)}, u32[]{:S(2)}, u32[]{:S(2)}) collective-permute-start(bf16[512,1024]{1,0:T(8,128)(2,1)S(1)} %fusion.42), channel_id=1, source_target_pairs={{0,8},{16,24},{8,0},{24,16},{1,9},{17,25},{9,1},{25,17},{2,10},{18... | collective-permute-start | bytes 3145736 | tf_op jit(solution)/shard_map/ppermute | solution.py:123
  230.2 34.7 %collective-permute-start.27 = (bf16[2,2,2,64,2048]{4,3,1,0,2:T(8,128)(2,1)S(1)}, bf16[2,2,2,64,2048]{4,3,1,0,2:T(8,128)(2,1)S(1)}, u32[]{:S(2)}, u32[]{:S(2)}) collective-permute-start(bf16[2,2,2,64,2048]{4,3,1,0,2:T(8,128)(2,1)S(1)} %get-tuple-element.150), channel_id=1, source_target_pairs={{0,1},{1,0},{2,3},{3,2},{4,5},{5,4},{6,7},{7,6},{8,9},{9,8},{10,11... | collective-permute-start | bytes 6291464 | tf_op jit(solution)/shard_map/ppermute | solution.py:36
  237.6 55.0 %collective-permute-start.29 = (bf16[512,1024]{1,0:T(8,128)(2,1)S(1)}, bf16[512,1024]{1,0:T(8,128)(2,1)S(1)}, u32[]{:S(2)}, u32[]{:S(2)}) collective-permute-start(bf16[512,1024]{1,0:T(8,128)(2,1)S(1)} %add_convert_fusion.19), channel_id=1, source_target_pairs={{8,16},{16,8},{9,17},{17,9},{10,18},{18,10},{11,19},{19,11},{12,20... | collective-permute-start | bytes 3145736 | tf_op jit(solution)/shard_map/ppermute | solution.py:123
  239.1 47.1 %collective-permute-start.26 = (bf16[512,1024]{1,0:T(8,128)(2,1)S(1)}, bf16[512,1024]{1,0:T(8,128)(2,1)S(1)}, u32[]{:S(2)}, u32[]{:S(2)}) collective-permute-start(bf16[512,1024]{1,0:T(8,128)(2,1)S(1)} %get-tuple-element.119), channel_id=1, source_target_pairs={{0,8},{16,24},{8,0},{24,16},{1,9},{17,25},{9,1},{25,17},{2,10},{18... | collective-permute-start | bytes 3145736 | tf_op jit(solution)/shard_map/ppermute | solution.py:123
  264.2 33.8 %collective-permute-start.23 = (bf16[512,1024]{1,0:T(8,128)(2,1)S(1)}, bf16[512,1024]{1,0:T(8,128)(2,1)S(1)}, u32[]{:S(2)}, u32[]{:S(2)}) collective-permute-start(bf16[512,1024]{1,0:T(8,128)(2,1)S(1)} %add_convert_fusion.23), channel_id=1, source_target_pairs={{8,16},{16,8},{9,17},{17,9},{10,18},{18,10},{11,19},{19,11},{12,20... | collective-permute-start | bytes 3145736 | tf_op jit(solution)/shard_map/ppermute | solution.py:123
  291.1 40.0 %collective-permute-start.31 = (bf16[512,2048]{1,0:T(8,128)(2,1)S(1)}, bf16[512,2048]{1,0:T(8,128)(2,1)S(1)}, u32[]{:S(2)}, u32[]{:S(2)}) collective-permute-start(bf16[512,2048]{1,0:T(8,128)(2,1)S(1)} %dynamic-slice_bitcast_fusion.1), channel_id=1, source_target_pairs={{0,1},{1,0},{2,3},{3,2},{4,5},{5,4},{6,7},{7,6},{8,9},{9,8},{10,11... | collective-permute-start | bytes 6291464 | tf_op jit(solution)/shard_map/ppermute | solution.py:36
  293.4 38.6 %collective-permute-start.30 = (bf16[512,1024]{1,0:T(8,128)(2,1)S(1)}, bf16[512,1024]{1,0:T(8,128)(2,1)S(1)}, u32[]{:S(2)}, u32[]{:S(2)}) collective-permute-start(bf16[512,1024]{1,0:T(8,128)(2,1)S(1)} %get-tuple-element.117), channel_id=1, source_target_pairs={{0,8},{16,24},{8,0},{24,16},{1,9},{17,25},{9,1},{25,17},{2,10},{18... | collective-permute-start | bytes 3145736 | tf_op jit(solution)/shard_map/ppermute | solution.py:123
  298.7 61.2 %collective-permute-start.24 = (bf16[512,1024]{1,0:T(8,128)(2,1)S(1)}, bf16[512,1024]{1,0:T(8,128)(2,1)S(1)}, u32[]{:S(2)}, u32[]{:S(2)}) collective-permute-start(bf16[512,1024]{1,0:T(8,128)(2,1)S(1)} %get-tuple-element.121), channel_id=1, source_target_pairs={{0,8},{16,24},{8,0},{24,16},{1,9},{17,25},{9,1},{25,17},{2,10},{18... | collective-permute-start | bytes 3145736 | tf_op jit(solution)/shard_map/ppermute | solution.py:123
  310.3 51.0 %collective-permute-start.28 = (bf16[768,512]{1,0:T(8,128)(2,1)S(1)}, bf16[768,512]{1,0:T(8,128)(2,1)S(1)}, u32[]{:S(2)}, u32[]{:S(2)}) collective-permute-start(bf16[768,512]{1,0:T(8,128)(2,1)S(1)} %slice.406), channel_id=1, source_target_pairs={{8,0},{16,8},{24,16},{9,1},{17,9},{25,17},{10,2},{18,10},{26,18},{... | collective-permute-start | bytes 2359304 | tf_op jit(solution)/shard_map/ppermute | solution.py:471
  312.4 90.3 %collective-permute-start.42 = (bf16[512,1024]{1,0:T(8,128)(2,1)S(1)}, bf16[512,1024]{1,0:T(8,128)(2,1)S(1)}, u32[]{:S(2)}, u32[]{:S(2)}) collective-permute-start(bf16[512,1024]{1,0:T(8,128)(2,1)S(1)} %get-tuple-element.115), channel_id=1, source_target_pairs={{0,8},{16,24},{8,0},{24,16},{1,9},{17,25},{9,1},{25,17},{2,10},{18... | collective-permute-start | bytes 3145736 | tf_op jit(solution)/shard_map/ppermute | solution.py:123
  345.0 30.0 %collective-permute-start.48 = (bf16[512,1024]{1,0:T(8,128)(2,1)S(1)}, bf16[512,1024]{1,0:T(8,128)(2,1)S(1)}, u32[]{:S(2)}, u32[]{:S(2)}) collective-permute-start(bf16[512,1024]{1,0:T(8,128)(2,1)S(1)} %add_convert_fusion.11), channel_id=1, source_target_pairs={{8,16},{16,8},{9,17},{17,9},{10,18},{18,10},{11,19},{19,11},{12,20... | collective-permute-start | bytes 3145736 | tf_op jit(solution)/shard_map/ppermute | solution.py:123
  368.5 33.3 %collective-permute-start.43 = (bf16[512,2048]{1,0:T(8,128)(2,1)S(1)}, bf16[512,2048]{1,0:T(8,128)(2,1)S(1)}, u32[]{:S(2)}, u32[]{:S(2)}) collective-permute-start(bf16[512,2048]{1,0:T(8,128)(2,1)S(1)} %dynamic-slice_bitcast_fusion), channel_id=1, source_target_pairs={{0,1},{1,0},{2,3},{3,2},{4,5},{5,4},{6,7},{7,6},{8,9},{9,8},{10,11... | collective-permute-start | bytes 6291464 | tf_op jit(solution)/shard_map/ppermute | solution.py:36
  375.9 47.9 %collective-permute-start.49 = (bf16[512,1024]{1,0:T(8,128)(2,1)S(1)}, bf16[512,1024]{1,0:T(8,128)(2,1)S(1)}, u32[]{:S(2)}, u32[]{:S(2)}) collective-permute-start(bf16[512,1024]{1,0:T(8,128)(2,1)S(1)} %get-tuple-element.109), channel_id=1, source_target_pairs={{0,8},{16,24},{8,0},{24,16},{1,9},{17,25},{9,1},{25,17},{2,10},{18... | collective-permute-start | bytes 3145736 | tf_op jit(solution)/shard_map/ppermute | solution.py:123
  382.8 69.0 %collective-permute-start.47 = (bf16[512,1024]{1,0:T(8,128)(2,1)}, bf16[512,1024]{1,0:T(8,128)(2,1)S(1)}, u32[]{:S(2)}, u32[]{:S(2)}) collective-permute-start(bf16[512,1024]{1,0:T(8,128)(2,1)} %get-tuple-element.111), channel_id=1, source_target_pairs={{0,8},{16,24},{8,0},{24,16},{1,9},{17,25},{9,1},{25,17},{2,10},{18... | collective-permute-start | bytes 3145736 | tf_op jit(solution)/shard_map/ppermute | solution.py:123
  406.3 50.9 %collective-permute-start.44 = (bf16[512,1024]{1,0:T(8,128)(2,1)}, bf16[512,1024]{1,0:T(8,128)(2,1)}, u32[]{:S(2)}, u32[]{:S(2)}) collective-permute-start(bf16[512,1024]{1,0:T(8,128)(2,1)} %add_convert_fusion.15), channel_id=1, source_target_pairs={{8,16},{16,8},{9,17},{17,9},{10,18},{18,10},{11,19},{19,11},{12,20... | collective-permute-start | bytes 3145736 | tf_op jit(solution)/shard_map/ppermute | solution.py:123
  445.1 37.0 %collective-permute-start.64 = (bf16[512,1024]{1,0:T(8,128)(2,1)}, bf16[512,1024]{1,0:T(8,128)(2,1)}, u32[]{:S(2)}, u32[]{:S(2)}) collective-permute-start(bf16[512,1024]{1,0:T(8,128)(2,1)} %add_convert_fusion.7), channel_id=1, source_target_pairs={{8,16},{16,8},{9,17},{17,9},{10,18},{18,10},{11,19},{19,11},{12,20... | collective-permute-start | bytes 3145736 | tf_op jit(solution)/shard_map/ppermute | solution.py:123
  455.8 26.1 %collective-permute-start.56 = (bf16[2,64,2048]{2,1,0:T(8,128)(2,1)S(1)}, bf16[2,64,2048]{2,1,0:T(8,128)(2,1)S(1)}, u32[]{:S(2)}, u32[]{:S(2)}) collective-permute-start(bf16[2,64,2048]{2,1,0:T(8,128)(2,1)S(1)} %maximum_select_fusion.24), channel_id=1, source_target_pairs={{0,2},{1,3},{2,0},{3,1},{4,6},{5,7},{6,4},{7,5},{8,10},{9,11},{10,... | collective-permute-start | bytes 1572872 | tf_op jit(solution)/shard_map/ppermute | solution.py:36
  467.0 24.4 %collective-permute-start.45 = (bf16[512,1024]{1,0:T(8,128)(2,1)S(1)}, bf16[512,1024]{1,0:T(8,128)(2,1)S(1)}, u32[]{:S(2)}, u32[]{:S(2)}) collective-permute-start(bf16[512,1024]{1,0:T(8,128)(2,1)S(1)} %get-tuple-element.113), channel_id=1, source_target_pairs={{0,8},{16,24},{8,0},{24,16},{1,9},{17,25},{9,1},{25,17},{2,10},{18... | collective-permute-start | bytes 3145736 | tf_op jit(solution)/shard_map/ppermute | solution.py:123
  478.8 31.9 %collective-permute-start.66 = (f32[108,128]{1,0:T(8,128)S(1)}, f32[108,128]{1,0:T(8,128)S(1)}, u32[]{:S(2)}, u32[]{:S(2)}) collective-permute-start(f32[108,128]{1,0:T(8,128)S(1)} %maximum_bitcast_fusion.3), channel_id=1, source_target_pairs={{0,8},{16,24},{8,0},{24,16},{1,9},{17,25},{9,1},{25,17},{2,10},{18... | collective-permute-start | bytes 165896 | tf_op jit(solution)/shard_map/ppermute | solution.py:123
  481.9 61.0 %collective-permute-start.40 = (bf16[2,2,2,64,2048]{4,3,0,1,2:T(8,128)(2,1)S(1)}, bf16[2,2,2,64,2048]{4,3,0,1,2:T(8,128)(2,1)S(1)}, u32[]{:S(2)}, u32[]{:S(2)}) collective-permute-start(bf16[2,2,2,64,2048]{4,3,0,1,2:T(8,128)(2,1)S(1)} %get-tuple-element.146), channel_id=1, source_target_pairs={{0,1},{1,0},{2,3},{3,2},{4,5},{5,4},{6,7},{7,6},{8,9},{9,8},{10,11... | collective-permute-start | bytes 6291464 | tf_op jit(solution)/shard_map/ppermute | solution.py:36
  485.2 29.8 %collective-permute-start.65 = (bf16[512,1024]{1,0:T(8,128)(2,1)S(1)}, bf16[512,1024]{1,0:T(8,128)(2,1)S(1)}, u32[]{:S(2)}, u32[]{:S(2)}) collective-permute-start(bf16[512,1024]{1,0:T(8,128)(2,1)S(1)} %broadcast_select_fusion.1), channel_id=1, source_target_pairs={{0,8},{16,24},{8,0},{24,16},{1,9},{17,25},{9,1},{25,17},{2,10},{18... | collective-permute-start | bytes 3145736 | tf_op jit(solution)/shard_map/ppermute | solution.py:123
  493.9 41.1 %collective-permute-start.68 = (bf16[512,1024]{1,0:T(8,128)(2,1)S(1)}, bf16[512,1024]{1,0:T(8,128)(2,1)S(1)}, u32[]{:S(2)}, u32[]{:S(2)}) collective-permute-start(bf16[512,1024]{1,0:T(8,128)(2,1)S(1)} %get-tuple-element.196), channel_id=1, source_target_pairs={{0,8},{16,24},{8,0},{24,16},{1,9},{17,25},{9,1},{25,17},{2,10},{18... | collective-permute-start | bytes 3145736 | tf_op jit(solution)/shard_map/ppermute | solution.py:123
  505.8 32.7 %collective-permute-start.59 = (bf16[512,1024]{1,0:T(8,128)(2,1)S(1)}, bf16[512,1024]{1,0:T(8,128)(2,1)S(1)}, u32[]{:S(2)}, u32[]{:S(2)}) collective-permute-start(bf16[512,1024]{1,0:T(8,128)(2,1)S(1)} %add_convert_fusion.9), channel_id=1, source_target_pairs={{8,16},{16,8},{9,17},{17,9},{10,18},{18,10},{11,19},{19,11},{12,20... | collective-permute-start | bytes 3145736 | tf_op jit(solution)/shard_map/ppermute | solution.py:123
  510.7 50.2 %collective-permute-start.58 = (bf16[2,2,2,64,2048]{4,3,0,1,2:T(8,128)(2,1)S(1)}, bf16[2,2,2,64,2048]{4,3,0,1,2:T(8,128)(2,1)S(1)}, u32[]{:S(2)}, u32[]{:S(2)}) collective-permute-start(bf16[2,2,2,64,2048]{4,3,0,1,2:T(8,128)(2,1)S(1)} %get-tuple-element.142), channel_id=1, source_target_pairs={{0,1},{1,0},{2,3},{3,2},{4,5},{5,4},{6,7},{7,6},{8,9},{9,8},{10,11... | collective-permute-start | bytes 6291464 | tf_op jit(solution)/shard_map/ppermute | solution.py:36
  519.9 26.2 %collective-permute-start.71 = (bf16[512,1024]{1,0:T(8,128)(2,1)S(1)}, bf16[512,1024]{1,0:T(8,128)(2,1)S(1)}, u32[]{:S(2)}, u32[]{:S(2)}) collective-permute-start(bf16[512,1024]{1,0:T(8,128)(2,1)S(1)} %add_convert_fusion.3), channel_id=1, source_target_pairs={{8,16},{16,8},{9,17},{17,9},{10,18},{18,10},{11,19},{19,11},{12,20... | collective-permute-start | bytes 3145736 | tf_op jit(solution)/shard_map/ppermute | solution.py:123
  535.4 28.5 %collective-permute-start.73 = (bf16[512,1024]{1,0:T(8,128)(2,1)S(1)}, bf16[512,1024]{1,0:T(8,128)(2,1)S(1)}, u32[]{:S(2)}, u32[]{:S(2)}) collective-permute-start(bf16[512,1024]{1,0:T(8,128)(2,1)S(1)} %add_convert_fusion.1), channel_id=1, source_target_pairs={{8,16},{16,8},{9,17},{17,9},{10,18},{18,10},{11,19},{19,11},{12,20... | collective-permute-start | bytes 3145736 | tf_op jit(solution)/shard_map/ppermute | solution.py:123
  538.5 39.8 %collective-permute-start.70 = (f32[108,128]{1,0:T(8,128)S(1)}, f32[108,128]{1,0:T(8,128)S(1)}, u32[]{:S(2)}, u32[]{:S(2)}) collective-permute-start(f32[108,128]{1,0:T(8,128)S(1)} %fusion.149), channel_id=1, source_target_pairs={{0,8},{16,24},{8,0},{24,16},{1,9},{17,25},{9,1},{25,17},{2,10},{18... | collective-permute-start | bytes 165896 | tf_op jit(solution)/shard_map/ppermute | solution.py:123
  542.9 35.4 %collective-permute-start.60 = (bf16[512,1024]{1,0:T(8,128)(2,1)S(1)}, bf16[512,1024]{1,0:T(8,128)(2,1)S(1)}, u32[]{:S(2)}, u32[]{:S(2)}) collective-permute-start(bf16[512,1024]{1,0:T(8,128)(2,1)S(1)} %add_convert_fusion.8), channel_id=1, source_target_pairs={{0,8},{16,24},{8,0},{24,16},{1,9},{17,25},{9,1},{25,17},{2,10},{18... | collective-permute-start | bytes 3145736 | tf_op jit(solution)/shard_map/ppermute | solution.py:123
  547.5 44.0 %collective-permute-start.72 = (bf16[512,1024]{1,0:T(8,128)(2,1)}, bf16[512,1024]{1,0:T(8,128)(2,1)}, u32[]{:S(2)}, u32[]{:S(2)}) collective-permute-start(bf16[512,1024]{1,0:T(8,128)(2,1)} %add_convert_fusion.2), channel_id=1, source_target_pairs={{0,8},{16,24},{8,0},{24,16},{1,9},{17,25},{9,1},{25,17},{2,10},{18... | collective-permute-start | bytes 3145736 | tf_op jit(solution)/shard_map/ppermute | solution.py:123
  564.3 44.7 %collective-permute-start.74 = (bf16[512,1024]{1,0:T(8,128)(2,1)S(1)}, bf16[512,1024]{1,0:T(8,128)(2,1)S(1)}, u32[]{:S(2)}, u32[]{:S(2)}) collective-permute-start(bf16[512,1024]{1,0:T(8,128)(2,1)S(1)} %add_convert_fusion.refs_1_), channel_id=1, source_target_pairs={{0,8},{16,24},{8,0},{24,16},{1,9},{17,25},{9,1},{25,17},{2,10},{18... | collective-permute-start | bytes 3145736 | tf_op jit(solution)/shard_map/ppermute | solution.py:123
  (118 other events, 1187.4 us)

commit v5 on v4

--- a/solution.py
+++ b/solution.py
@@ -250,6 +250,26 @@
     return (grad_in, jnp.sum(grad_out * normed_raw, axis=0), jnp.sum(grad_out, axis=0))
 
 
+def norm_kernel(x_ref, gain_ref, bias_ref, out_ref):
+    normed, _ = norm_stats(x_ref[...].astype(f32))
+    out_ref[...] = (normed * gain_ref[...] + bias_ref[...]).astype(bf16)
+
+
+def norm_rows(values, gain, bias):
+    rows, width = values.shape
+    block = pl.BlockSpec((128, width), lambda i: (i, 0))
+    param = pl.BlockSpec((1, width), lambda i: (0, 0))
+    return pl.pallas_call(
+        norm_kernel,
+        grid=(rows // 128,),
+        in_specs=[block, param, param],
+        out_specs=block,
+        out_shape=jax.ShapeDtypeStruct((rows, width), bf16),
+        compiler_params=pltpu.CompilerParams(vmem_limit_bytes=16 << 20),
+        name="norm_rows",
+    )(values, gain.reshape(1, width), bias.reshape(1, width))
+
+
 def dot(a, b, dims):
     return lax.dot_general(a, b, (dims, ((), ())), preferred_element_type=f32)
 
@@ -291,10 +311,11 @@
     dv_ref[window, :] += dot(probs.astype(bf16), out, ((0,), (0,)))
 
 
-def attend_specs(rows, heads):
+def attend_specs(rows):
     block = pl.BlockSpec((QUERY_BLOCK, HEAD_DIM), lambda h, i: (i, h))
-    keys = pl.BlockSpec((rows + MAX_DOCUMENT, HEAD_DIM), lambda h, i: (0, h))
-    vals = pl.BlockSpec((rows + MAX_DOCUMENT, HEAD_DIM), lambda h, i: (0, h + heads))
+    joined = (None, rows + MAX_DOCUMENT, HEAD_DIM)
+    keys = pl.BlockSpec(joined, lambda h, i: (0, 0, h))
+    vals = pl.BlockSpec(joined, lambda h, i: (1, 0, h))
     pos = pl.BlockSpec((QUERY_BLOCK, 1), lambda h, i: (i, 0))
     valid = pl.BlockSpec((1, 1, WINDOW), lambda h, i: (i, 0, 0))
     return block, keys, vals, pos, valid
@@ -303,7 +324,7 @@
 def attend(query, keys_vals, pos, valid):
     rows, width = query.shape
     heads = width // HEAD_DIM
-    block, keys_spec, vals_spec, pos_spec, valid_spec = attend_specs(rows, heads)
+    block, keys_spec, vals_spec, pos_spec, valid_spec = attend_specs(rows)
     return pl.pallas_call(
         attend_kernel,
         grid=(heads, rows // QUERY_BLOCK),
@@ -318,13 +339,14 @@
 def attend_back(query, keys_vals, out, pos, valid):
     rows, width = query.shape
     heads = width // HEAD_DIM
-    block, keys_spec, vals_spec, pos_spec, valid_spec = attend_specs(rows, heads)
+    block, keys_spec, vals_spec, pos_spec, valid_spec = attend_specs(rows)
     wide_shape = jax.ShapeDtypeStruct((rows + MAX_DOCUMENT, width), f32)
+    grad_spec = pl.BlockSpec((rows + MAX_DOCUMENT, HEAD_DIM), lambda h, i: (0, h))
     return pl.pallas_call(
         attend_back_kernel,
         grid=(heads, rows // QUERY_BLOCK),
         in_specs=[block, keys_spec, vals_spec, block, pos_spec, valid_spec],
-        out_specs=[block, keys_spec, keys_spec],
+        out_specs=[block, grad_spec, grad_spec],
         out_shape=[jax.ShapeDtypeStruct((rows, width), bf16), wide_shape, wide_shape],
         compiler_params=pltpu.CompilerParams(vmem_limit_bytes=24 << 20),
         name="attend_back",
@@ -410,18 +432,15 @@
         [valid_near[i : i + WINDOW] for i in range(0, rows, QUERY_BLOCK)]
     ).reshape(rows // QUERY_BLOCK, 1, WINDOW)
 
-    inputs = layer_entry_input.astype(f32)
-    raw_one, _ = norm_stats(inputs)
-    normed_one = (raw_one * ln1_gain + ln1_bias).astype(bf16)
-    w_flat = w_qkv.reshape(width, 3 * local_width)
-    mixed = dot(normed_one, w_flat[:, local_width:], ((1,), (0,)))
-    bias = jnp.concatenate([jnp.zeros_like(b_qv[1]), b_qv[1]])
-    keys_vals = (mixed + bias).astype(bf16)
-    halo = lax.ppermute(keys_vals[rows - MAX_DOCUMENT :], "wide", ahead)
-    query = (dot(normed_one, w_flat[:, :local_width], ((1,), (0,))) + b_qv[0]).astype(bf16)
+    normed_one = norm_rows(layer_entry_input, ln1_gain, ln1_bias)
+    mixed = dot(normed_one, w_qkv[:, 1:], ((1,), (0,))).transpose(1, 0, 2)
+    bias = jnp.stack([jnp.zeros_like(b_qv[1]), b_qv[1]])
+    keys_vals = (mixed + bias[:, None, :]).astype(bf16)
+    halo = lax.ppermute(keys_vals[:, rows - MAX_DOCUMENT :], "wide", ahead)
+    query = (dot(normed_one, w_qkv[:, 0], ((1,), (0,))) + b_qv[0]).astype(bf16)
     grad_active = dot(cotangent, w_down, ((1,), (1,))).astype(bf16)
     halo, query, grad_active = lax.optimization_barrier((halo, query, grad_active))
-    keys_vals = jnp.concatenate([halo, keys_vals])
+    keys_vals = jnp.concatenate([halo, keys_vals], axis=1)
     attended = attend(query, keys_vals, pos, valid_windows)
     attn_part = dot(attended, w_out, ((1,), (0,))).astype(bf16)
     attn_total = reduce_rows(attn_part).astype(f32)
@@ -488,7 +507,8 @@
     bulk.feed(ups[3])
     grad_b_qv = jnp.sum(grad_mixed.astype(f32), axis=0)
     grad_b_qv = [grad_b_qv[i * local_width : (i + 1) * local_width] for i in (0, 2)]
-    back_part = dot(grad_mixed, w_flat, ((1,), (1,))).astype(bf16)
+    grad_three = grad_mixed.reshape(rows, 3, local_width)
+    back_part = dot(grad_three, w_qkv, ((1, 2), (1, 2))).astype(bf16)
     output = gather_rows((after_attn + b_down + mlp_total).astype(bf16))
     grad_norm_one = reduce_rows(back_part, at_calls(bulk.sync, 0, 2)).astype(f32)
     raw_rows, inv_rows = norm_stats(inputs_rows)

time: 620 us -> 617 us (level)
  starting transfers between devices: 188 us -> 180 us
    ppermute x30, starting transfers between devices: 146 us -> 138 us  [exchange(): return lax.ppermute(value, 'wide', pairs + [(b, a) for a, b in pairs])]
    unnamed x152 -> x181, local copies, waits for them, and re-layouts: 23.7 us -> 23 us
  transfers between devices with their start and end apart: 75 -> 75, of which waited for: 38 -> 38; matrix products, arithmetic and copies ran while one was open for 20% -> 22% of each run, Pallas kernels for 3% -> 3%
where the time goes in v5:
time: 617 us; the launch traced here: 610 us
  waiting for transfers between devices  194 us (31%)
  starting transfers between devices  180 us (29%)
  other arithmetic  84.6 us (14%)
  matrix products  65.4 us (11%)
  local copies, waits for them, and re-layouts  49.8 us (8%)
  Pallas kernels  32.9 us (5%)
    ppermute x30, starting transfers between devices, exchange(): return lax.ppermute(value, 'wide', pairs + [(b, a) for a, b in pairs])  138 us
    ppermute x43, waiting for transfers between devices, swap(): lax.ppermute(value, 'narrow', [(i, i ^ 1 << bit) for i in range(count)])  119 us
    ppermute x30, waiting for transfers between devices, exchange(): return lax.ppermute(value, 'wide', pairs + [(b, a) for a, b in pairs])  72.7 us
    dot_general x23, matrix products, dot(): return lax.dot_general(a, b, (dims, ((), ())), preferred_element_type=f32)  65.4 us
    ppermute x43, starting transfers between devices, swap(): lax.ppermute(value, 'narrow', [(i, i ^ 1 << bit) for i in range(count)])  35 us
    unnamed x181, local copies, waits for them, and re-layouts  23 us
    convert_element_type x35, other arithmetic, add_low(): return (a.astype(f32) + b.astype(f32)).astype(a.dtype)  21.9 us
    select_n x8, other arithmetic, start(): value = jnp.where(self.line.depth == e, self.chunks[sent], value)  15.6 us
  transfers between devices with their start and end apart: 75, of which 38 were waited for; matrix products, arithmetic and copies ran while one was open for 22% of the time, Pallas kernels for 3%

profile of v5, /device:TPU:0, one launch (start us, length us, event | category | flops | bytes accessed | tf_op | source)
XLA Modules:
  0.0 609.8 jit_solution(2170387047431142032)
XLA Ops:
  11.7 5.8 collective-permute-start
  23.2 9.4 %convolution_convert_fusion.3 = bf16[1024,1024]{1,0:T(8,128)(2,1)} fusion(bf16[1024,2048]{1,0:T(8,128)(2,1)} %param.32, bf16[1024,2048]{1,0:T(8,128)(2,1)} %param.28), kind=kOutput, calls=%fused_computation.78 | convolution fusion | flops 4296015872 | bytes 10485760 | tf_op jit(solution)/shard_map/dot_general | solution.py:274
  34.7 8.2 %attend.1 = bf16[1024,256]{1,0:T(8,128)(2,1)S(1)} custom-call(bf16[1024,256]{1,0:T(8,128)(2,1)S(1)} %copy-done.18, bf16[2,1792,256]{2,1,0:T(8,128)(2,1)S(1)} %pad_maximum_fusion.6.k_ref.v_ref, bf16[2,1792,256]{2,1,0:T(8,128)(2,1)S(1)} %pad_maximum_fusion.6.k_ref.v_ref, s32[1024,1]{1,0:T(8,128)S(1)} %copy.59.pos_ref, s32[4,1,1024]{2,1,0:T(1,128)S(1)} %reshape.1066.valid_ref), custom_call_target="tpu_custom_call" | custom-call | tf_op jit(solution)/shard_map/attend/pallas_call | solution.py:328
  61.5 10.0 %collective-permute-done.2 = bf16[2,64,2048]{2,1,0:T(8,128)(2,1)} collective-permute-done((bf16[2,64,2048]{2,1,0:T(8,128)(2,1)}, bf16[2,64,2048]{2,1,0:T(8,128)(2,1)}, u32[]{:S(2)}, u32[]{:S(2)}) %collective-permute-start.2) | collective-permute-done | bytes 524320 | tf_op jit(solution)/shard_map/ppermute | solution.py:36
  89.6 4.7 collective-permute-done.6
  101.2 5.2 collective-permute-done.7
  124.5 7.8 %convert_reduce_fusion = (f32[1024]{0:T(1024)S(1)}, bf16[1024,1024]{1,0:T(8,128)(2,1)S(1)}, bf16[1024,1024]{1,0:T(8,128)(2,1)S(1)}) fusion(f32[1024]{0:T(1024)S(1)} %copy-done.85, bf16[1024,1024]{1,0:T(8,128)(2,1)S(1)} %copy-done.89, bf16[1024,2048]{1,0:T(8,128)(2,1)S(1)} %bitcast.308, bf16[2048,1024]{1,0:T(8,128)(2,1)S(1)} %copy-done.81), kind=kOutput, calls=%fused_computation.30 | convolution fusion | flops 4322229248 | bytes 14688256 | tf_op jit(solution)/shard_map/dot_general | solution.py:274
  132.3 5.0 convolution_convert_fusion.2
  152.6 18.4 %collective-permute-done.13 = bf16[512,1024]{1,0:T(8,128)(2,1)} collective-permute-done((bf16[512,1024]{1,0:T(8,128)(2,1)}, bf16[512,1024]{1,0:T(8,128)(2,1)}, u32[]{:S(2)}, u32[]{:S(2)}) %collective-permute-start.13) | collective-permute-done | bytes 1048608 | tf_op jit(solution)/shard_map/ppermute | solution.py:123
  175.0 9.0 %collective-permute-done.17 = bf16[2,64,2048]{2,1,0:T(8,128)(2,1)S(1)} collective-permute-done((bf16[2,64,2048]{2,1,0:T(8,128)(2,1)S(1)}, bf16[2,64,2048]{2,1,0:T(8,128)(2,1)S(1)}, u32[]{:S(2)}, u32[]{:S(2)}) %collective-permute-start.17) | collective-permute-done | bytes 524320 | tf_op jit(solution)/shard_map/ppermute | solution.py:36
  211.9 6.6 %collective-permute-done.22 = bf16[2,64,2048]{2,1,0:T(8,128)(2,1)S(1)} collective-permute-done((bf16[2,64,2048]{2,1,0:T(8,128)(2,1)S(1)}, bf16[2,64,2048]{2,1,0:T(8,128)(2,1)S(1)}, u32[]{:S(2)}, u32[]{:S(2)}) %collective-permute-start.22) | collective-permute-done | bytes 524320 | tf_op jit(solution)/shard_map/ppermute | solution.py:36
  219.4 5.4 collective-permute-done.11
  235.1 24.7 %collective-permute-start.26 = (bf16[512,1024]{1,0:T(8,128)(2,1)S(1)}, bf16[512,1024]{1,0:T(8,128)(2,1)S(1)}, u32[]{:S(2)}, u32[]{:S(2)}) collective-permute-start(bf16[512,1024]{1,0:T(8,128)(2,1)S(1)} %get-tuple-element.121), channel_id=1, source_target_pairs={{0,8},{16,24},{8,0},{24,16},{1,9},{17,25},{9,1},{25,17},{2,10},{18... | collective-permute-start | bytes 3145736 | tf_op jit(solution)/shard_map/ppermute | solution.py:123
  263.6 12.1 %attend_back.1 = (bf16[1024,256]{1,0:T(8,128)(2,1)S(1)}, f32[1792,256]{1,0:T(8,128)S(1)}, f32[1792,256]{1,0:T(8,128)S(1)}) custom-call(bf16[1024,256]{1,0:T(8,128)(2,1)S(1)} %copy-done.19, bf16[2,1792,256]{2,1,0:T(8,128)(2,1)S(1)} %pad_maximum_fusion.6.k_ref.v_ref, bf16[2,1792,256]{2,1,0:T(8,128)(2,1)S(1)} %pad_maximum_fusion.6.k_ref.v_ref, ...), custom_call_target="tpu_custom_call" | custom-call | tf_op jit(solution)/shard_map/attend_back/pallas_call | solution.py:345
  276.4 5.9 collective-permute-done.26.refs_4_
  282.3 4.7 convolution_convert_fusion.1
  296.9 7.9 %collective-permute-start.24 = (bf16[512,1024]{1,0:T(8,128)(2,1)S(1)}, bf16[512,1024]{1,0:T(8,128)(2,1)S(1)}, u32[]{:S(2)}, u32[]{:S(2)}) collective-permute-start(bf16[512,1024]{1,0:T(8,128)(2,1)S(1)} %get-tuple-element.123), channel_id=1, source_target_pairs={{0,8},{16,24},{8,0},{24,16},{1,9},{17,25},{9,1},{25,17},{2,10},{18... | collective-permute-start | bytes 3145736 | tf_op jit(solution)/shard_map/ppermute | solution.py:123
  311.4 16.2 %collective-permute-start.42 = (bf16[512,1024]{1,0:T(8,128)(2,1)}, bf16[512,1024]{1,0:T(8,128)(2,1)}, u32[]{:S(2)}, u32[]{:S(2)}) collective-permute-start(bf16[512,1024]{1,0:T(8,128)(2,1)} %get-tuple-element.117), channel_id=1, source_target_pairs={{0,8},{16,24},{8,0},{24,16},{1,9},{17,25},{9,1},{25,17},{2,10},{18... | collective-permute-start | bytes 3145736 | tf_op jit(solution)/shard_map/ppermute | solution.py:123
  331.0 10.4 %collective-permute-done.32 = bf16[2,64,2048]{2,1,0:T(8,128)(2,1)S(1)} collective-permute-done((bf16[2,64,2048]{2,1,0:T(8,128)(2,1)S(1)}, bf16[2,64,2048]{2,1,0:T(8,128)(2,1)S(1)}, u32[]{:S(2)}, u32[]{:S(2)}) %collective-permute-start.32) | collective-permute-done | bytes 524320 | tf_op jit(solution)/shard_map/ppermute | solution.py:36
  344.0 5.7 collective-permute-done.33
  350.3 5.8 collective-permute-done.35
  385.1 16.0 %collective-permute-start.47 = (bf16[512,1024]{1,0:T(8,128)(2,1)}, bf16[512,1024]{1,0:T(8,128)(2,1)S(1)}, u32[]{:S(2)}, u32[]{:S(2)}) collective-permute-start(bf16[512,1024]{1,0:T(8,128)(2,1)} %get-tuple-element.113), channel_id=1, source_target_pairs={{0,8},{16,24},{8,0},{24,16},{1,9},{17,25},{9,1},{25,17},{2,10},{18... | collective-permute-start | bytes 3145736 | tf_op jit(solution)/shard_map/ppermute | solution.py:123
  408.7 4.9 tiled.5
  434.2 5.5 collective-permute-done.62
  467.9 7.6 %collective-permute-done.39 = bf16[2,64,2048]{2,1,0:T(8,128)(2,1)S(1)} collective-permute-done((bf16[2,64,2048]{2,1,0:T(8,128)(2,1)S(1)}, bf16[2,64,2048]{2,1,0:T(8,128)(2,1)S(1)}, u32[]{:S(2)}, u32[]{:S(2)}) %collective-permute-start.39) | collective-permute-done | bytes 524320 | tf_op jit(solution)/shard_map/ppermute | solution.py:36
  484.2 6.9 %collective-permute-done.45.refs_5_ = bf16[512,1024]{1,0:T(8,128)(2,1)S(1)} collective-permute-done((bf16[512,1024]{1,0:T(8,128)(2,1)S(1)}, bf16[512,1024]{1,0:T(8,128)(2,1)S(1)}, u32[]{:S(2)}, u32[]{:S(2)}) %collective-permute-start.45) | collective-permute-done | bytes 1048608 | tf_op jit(solution)/shard_map/ppermute | solution.py:123
  493.6 11.5 %collective-permute-start.68 = (bf16[512,1024]{1,0:T(8,128)(2,1)S(1)}, bf16[512,1024]{1,0:T(8,128)(2,1)S(1)}, u32[]{:S(2)}, u32[]{:S(2)}) collective-permute-start(bf16[512,1024]{1,0:T(8,128)(2,1)S(1)} %get-tuple-element.198), channel_id=1, source_target_pairs={{0,8},{16,24},{8,0},{24,16},{1,9},{17,25},{9,1},{25,17},{2,10},{18... | collective-permute-start | bytes 3145736 | tf_op jit(solution)/shard_map/ppermute | solution.py:123
  520.3 13.7 %collective-permute-done.68 = bf16[512,1024]{1,0:T(8,128)(2,1)S(1)} collective-permute-done((bf16[512,1024]{1,0:T(8,128)(2,1)S(1)}, bf16[512,1024]{1,0:T(8,128)(2,1)S(1)}, u32[]{:S(2)}, u32[]{:S(2)}) %collective-permute-start.68) | collective-permute-done | bytes 1048608 | tf_op jit(solution)/shard_map/ppermute | solution.py:123
  546.1 14.2 %collective-permute-start.72 = (bf16[512,1024]{1,0:T(8,128)(2,1)}, bf16[512,1024]{1,0:T(8,128)(2,1)}, u32[]{:S(2)}, u32[]{:S(2)}) collective-permute-start(bf16[512,1024]{1,0:T(8,128)(2,1)} %add_convert_fusion.2), channel_id=1, source_target_pairs={{0,8},{16,24},{8,0},{24,16},{1,9},{17,25},{9,1},{25,17},{2,10},{18... | collective-permute-start | bytes 3145736 | tf_op jit(solution)/shard_map/ppermute | solution.py:123
  563.8 13.8 %collective-permute-start.74 = (bf16[512,1024]{1,0:T(8,128)(2,1)S(1)}, bf16[512,1024]{1,0:T(8,128)(2,1)S(1)}, u32[]{:S(2)}, u32[]{:S(2)}) collective-permute-start(bf16[512,1024]{1,0:T(8,128)(2,1)S(1)} %add_convert_fusion.refs_1_), channel_id=1, source_target_pairs={{0,8},{16,24},{8,0},{24,16},{1,9},{17,25},{9,1},{25,17},{2,10},{18... | collective-permute-start | bytes 3145736 | tf_op jit(solution)/shard_map/ppermute | solution.py:123
  582.0 8.2 %collective-permute-done.72 = bf16[512,1024]{1,0:T(8,128)(2,1)} collective-permute-done((bf16[512,1024]{1,0:T(8,128)(2,1)}, bf16[512,1024]{1,0:T(8,128)(2,1)}, u32[]{:S(2)}, u32[]{:S(2)}) %collective-permute-start.72) | collective-permute-done | bytes 1048608 | tf_op jit(solution)/shard_map/ppermute | solution.py:123
  598.1 9.9 %collective-permute-done.74.refs_2_ = bf16[512,1024]{1,0:T(8,128)(2,1)S(1)} collective-permute-done((bf16[512,1024]{1,0:T(8,128)(2,1)S(1)}, bf16[512,1024]{1,0:T(8,128)(2,1)S(1)}, u32[]{:S(2)}, u32[]{:S(2)}) %collective-permute-start.74) | collective-permute-done | bytes 1048608 | tf_op jit(solution)/shard_map/ppermute | solution.py:123
  (492 shorter events, 305.8 us)
Async XLA Ops:
  11.7 21.7 %collective-permute-start = (bf16[2,768,256]{2,1,0:T(8,128)(2,1)S(1)}, bf16[2,768,256]{2,1,0:T(8,128)(2,1)}, u32[]{:S(2)}, u32[]{:S(2)}) collective-permute-start(bf16[2,768,256]{2,1,0:T(8,128)(2,1)S(1)} %slice.281), channel_id=1, source_target_pairs={{0,8},{8,16},{16,24},{1,9},{9,17},{17,25},{2,10},{10,18},{18,26},{... | collective-permute-start | bytes 2359304 | tf_op jit(solution)/shard_map/ppermute | solution.py:439
  144.0 26.9 %collective-permute-start.13 = (bf16[512,1024]{1,0:T(8,128)(2,1)}, bf16[512,1024]{1,0:T(8,128)(2,1)}, u32[]{:S(2)}, u32[]{:S(2)}) collective-permute-start(bf16[512,1024]{1,0:T(8,128)(2,1)} %fusion.32), channel_id=1, source_target_pairs={{0,8},{16,24},{8,0},{24,16},{1,9},{17,25},{9,1},{25,17},{2,10},{18... | collective-permute-start | bytes 3145736 | tf_op jit(solution)/shard_map/ppermute | solution.py:123
  149.9 46.1 %collective-permute-start.12 = (bf16[512,1024]{1,0:T(8,128)(2,1)S(1)}, bf16[512,1024]{1,0:T(8,128)(2,1)S(1)}, u32[]{:S(2)}, u32[]{:S(2)}) collective-permute-start(bf16[512,1024]{1,0:T(8,128)(2,1)S(1)} %fusion.35), channel_id=1, source_target_pairs={{0,8},{16,24},{8,0},{24,16},{1,9},{17,25},{9,1},{25,17},{2,10},{18... | collective-permute-start | bytes 3145736 | tf_op jit(solution)/shard_map/ppermute | solution.py:123
  225.0 35.9 %collective-permute-start.27 = (bf16[2,2,2,64,2048]{4,3,1,0,2:T(8,128)(2,1)S(1)}, bf16[2,2,2,64,2048]{4,3,1,0,2:T(8,128)(2,1)S(1)}, u32[]{:S(2)}, u32[]{:S(2)}) collective-permute-start(bf16[2,2,2,64,2048]{4,3,1,0,2:T(8,128)(2,1)S(1)} %get-tuple-element.152), channel_id=1, source_target_pairs={{0,1},{1,0},{2,3},{3,2},{4,5},{5,4},{6,7},{7,6},{8,9},{9,8},{10,11... | collective-permute-start | bytes 6291464 | tf_op jit(solution)/shard_map/ppermute | solution.py:36
  232.7 56.2 %collective-permute-start.29 = (bf16[512,1024]{1,0:T(8,128)(2,1)S(1)}, bf16[512,1024]{1,0:T(8,128)(2,1)S(1)}, u32[]{:S(2)}, u32[]{:S(2)}) collective-permute-start(bf16[512,1024]{1,0:T(8,128)(2,1)S(1)} %add_convert_fusion.19), channel_id=1, source_target_pairs={{8,16},{16,8},{9,17},{17,9},{10,18},{18,10},{11,19},{19,11},{12,20... | collective-permute-start | bytes 3145736 | tf_op jit(solution)/shard_map/ppermute | solution.py:123
  235.1 47.2 %collective-permute-start.26 = (bf16[512,1024]{1,0:T(8,128)(2,1)S(1)}, bf16[512,1024]{1,0:T(8,128)(2,1)S(1)}, u32[]{:S(2)}, u32[]{:S(2)}) collective-permute-start(bf16[512,1024]{1,0:T(8,128)(2,1)S(1)} %get-tuple-element.121), channel_id=1, source_target_pairs={{0,8},{16,24},{8,0},{24,16},{1,9},{17,25},{9,1},{25,17},{2,10},{18... | collective-permute-start | bytes 3145736 | tf_op jit(solution)/shard_map/ppermute | solution.py:123
  260.2 34.9 %collective-permute-start.23 = (bf16[512,1024]{1,0:T(8,128)(2,1)S(1)}, bf16[512,1024]{1,0:T(8,128)(2,1)S(1)}, u32[]{:S(2)}, u32[]{:S(2)}) collective-permute-start(bf16[512,1024]{1,0:T(8,128)(2,1)S(1)} %add_convert_fusion.23), channel_id=1, source_target_pairs={{8,16},{16,8},{9,17},{17,9},{10,18},{18,10},{11,19},{19,11},{12,20... | collective-permute-start | bytes 3145736 | tf_op jit(solution)/shard_map/ppermute | solution.py:123
  287.2 40.4 %collective-permute-start.31 = (bf16[512,2048]{1,0:T(8,128)(2,1)S(1)}, bf16[512,2048]{1,0:T(8,128)(2,1)S(1)}, u32[]{:S(2)}, u32[]{:S(2)}) collective-permute-start(bf16[512,2048]{1,0:T(8,128)(2,1)S(1)} %dynamic-slice_bitcast_fusion.1), channel_id=1, source_target_pairs={{0,1},{1,0},{2,3},{3,2},{4,5},{5,4},{6,7},{7,6},{8,9},{9,8},{10,11... | collective-permute-start | bytes 6291464 | tf_op jit(solution)/shard_map/ppermute | solution.py:36
  290.6 37.8 %collective-permute-start.30 = (bf16[512,1024]{1,0:T(8,128)(2,1)S(1)}, bf16[512,1024]{1,0:T(8,128)(2,1)S(1)}, u32[]{:S(2)}, u32[]{:S(2)}) collective-permute-start(bf16[512,1024]{1,0:T(8,128)(2,1)S(1)} %get-tuple-element.119), channel_id=1, source_target_pairs={{0,8},{16,24},{8,0},{24,16},{1,9},{17,25},{9,1},{25,17},{2,10},{18... | collective-permute-start | bytes 3145736 | tf_op jit(solution)/shard_map/ppermute | solution.py:123
  296.9 60.4 %collective-permute-start.24 = (bf16[512,1024]{1,0:T(8,128)(2,1)S(1)}, bf16[512,1024]{1,0:T(8,128)(2,1)S(1)}, u32[]{:S(2)}, u32[]{:S(2)}) collective-permute-start(bf16[512,1024]{1,0:T(8,128)(2,1)S(1)} %get-tuple-element.123), channel_id=1, source_target_pairs={{0,8},{16,24},{8,0},{24,16},{1,9},{17,25},{9,1},{25,17},{2,10},{18... | collective-permute-start | bytes 3145736 | tf_op jit(solution)/shard_map/ppermute | solution.py:123
  308.0 50.4 %collective-permute-start.28 = (bf16[768,512]{1,0:T(8,128)(2,1)S(1)}, bf16[768,512]{1,0:T(8,128)(2,1)S(1)}, u32[]{:S(2)}, u32[]{:S(2)}) collective-permute-start(bf16[768,512]{1,0:T(8,128)(2,1)S(1)} %slice.408), channel_id=1, source_target_pairs={{8,0},{16,8},{24,16},{9,1},{17,9},{25,17},{10,2},{18,10},{26,18},{... | collective-permute-start | bytes 2359304 | tf_op jit(solution)/shard_map/ppermute | solution.py:490
  311.4 90.5 %collective-permute-start.42 = (bf16[512,1024]{1,0:T(8,128)(2,1)}, bf16[512,1024]{1,0:T(8,128)(2,1)}, u32[]{:S(2)}, u32[]{:S(2)}) collective-permute-start(bf16[512,1024]{1,0:T(8,128)(2,1)} %get-tuple-element.117), channel_id=1, source_target_pairs={{0,8},{16,24},{8,0},{24,16},{1,9},{17,25},{9,1},{25,17},{2,10},{18... | collective-permute-start | bytes 3145736 | tf_op jit(solution)/shard_map/ppermute | solution.py:123
  341.4 36.9 %collective-permute-start.48 = (bf16[512,1024]{1,0:T(8,128)(2,1)S(1)}, bf16[512,1024]{1,0:T(8,128)(2,1)}, u32[]{:S(2)}, u32[]{:S(2)}) collective-permute-start(bf16[512,1024]{1,0:T(8,128)(2,1)S(1)} %add_convert_fusion.11), channel_id=1, source_target_pairs={{8,16},{16,8},{9,17},{17,9},{10,18},{18,10},{11,19},{19,11},{12,20... | collective-permute-start | bytes 3145736 | tf_op jit(solution)/shard_map/ppermute | solution.py:123
  369.9 31.2 %collective-permute-start.43 = (bf16[512,2048]{1,0:T(8,128)(2,1)S(1)}, bf16[512,2048]{1,0:T(8,128)(2,1)S(1)}, u32[]{:S(2)}, u32[]{:S(2)}) collective-permute-start(bf16[512,2048]{1,0:T(8,128)(2,1)S(1)} %dynamic-slice_bitcast_fusion), channel_id=1, source_target_pairs={{0,1},{1,0},{2,3},{3,2},{4,5},{5,4},{6,7},{7,6},{8,9},{9,8},{10,11... | collective-permute-start | bytes 6291464 | tf_op jit(solution)/shard_map/ppermute | solution.py:36
  380.3 42.5 %collective-permute-start.49 = (bf16[512,1024]{1,0:T(8,128)(2,1)S(1)}, bf16[512,1024]{1,0:T(8,128)(2,1)S(1)}, u32[]{:S(2)}, u32[]{:S(2)}) collective-permute-start(bf16[512,1024]{1,0:T(8,128)(2,1)S(1)} %get-tuple-element.111), channel_id=1, source_target_pairs={{0,8},{16,24},{8,0},{24,16},{1,9},{17,25},{9,1},{25,17},{2,10},{18... | collective-permute-start | bytes 3145736 | tf_op jit(solution)/shard_map/ppermute | solution.py:123
  385.1 65.6 %collective-permute-start.47 = (bf16[512,1024]{1,0:T(8,128)(2,1)}, bf16[512,1024]{1,0:T(8,128)(2,1)S(1)}, u32[]{:S(2)}, u32[]{:S(2)}) collective-permute-start(bf16[512,1024]{1,0:T(8,128)(2,1)} %get-tuple-element.113), channel_id=1, source_target_pairs={{0,8},{16,24},{8,0},{24,16},{1,9},{17,25},{9,1},{25,17},{2,10},{18... | collective-permute-start | bytes 3145736 | tf_op jit(solution)/shard_map/ppermute | solution.py:123
  407.0 49.3 %collective-permute-start.44 = (bf16[512,1024]{1,0:T(8,128)(2,1)}, bf16[512,1024]{1,0:T(8,128)(2,1)}, u32[]{:S(2)}, u32[]{:S(2)}) collective-permute-start(bf16[512,1024]{1,0:T(8,128)(2,1)} %add_convert_fusion.15), channel_id=1, source_target_pairs={{8,16},{16,8},{9,17},{17,9},{10,18},{18,10},{11,19},{19,11},{12,20... | collective-permute-start | bytes 3145736 | tf_op jit(solution)/shard_map/ppermute | solution.py:123
  444.1 36.9 %collective-permute-start.64 = (bf16[512,1024]{1,0:T(8,128)(2,1)}, bf16[512,1024]{1,0:T(8,128)(2,1)}, u32[]{:S(2)}, u32[]{:S(2)}) collective-permute-start(bf16[512,1024]{1,0:T(8,128)(2,1)} %add_convert_fusion.7), channel_id=1, source_target_pairs={{8,16},{16,8},{9,17},{17,9},{10,18},{18,10},{11,19},{19,11},{12,20... | collective-permute-start | bytes 3145736 | tf_op jit(solution)/shard_map/ppermute | solution.py:123
  454.8 26.0 %collective-permute-start.56 = (bf16[2,64,2048]{2,1,0:T(8,128)(2,1)S(1)}, bf16[2,64,2048]{2,1,0:T(8,128)(2,1)S(1)}, u32[]{:S(2)}, u32[]{:S(2)}) collective-permute-start(bf16[2,64,2048]{2,1,0:T(8,128)(2,1)S(1)} %maximum_select_fusion.24), channel_id=1, source_target_pairs={{0,2},{1,3},{2,0},{3,1},{4,6},{5,7},{6,4},{7,5},{8,10},{9,11},{10,... | collective-permute-start | bytes 1572872 | tf_op jit(solution)/shard_map/ppermute | solution.py:36
  466.0 25.0 %collective-permute-start.45 = (bf16[512,1024]{1,0:T(8,128)(2,1)S(1)}, bf16[512,1024]{1,0:T(8,128)(2,1)S(1)}, u32[]{:S(2)}, u32[]{:S(2)}) collective-permute-start(bf16[512,1024]{1,0:T(8,128)(2,1)S(1)} %get-tuple-element.115), channel_id=1, source_target_pairs={{0,8},{16,24},{8,0},{24,16},{1,9},{17,25},{9,1},{25,17},{2,10},{18... | collective-permute-start | bytes 3145736 | tf_op jit(solution)/shard_map/ppermute | solution.py:123
  477.9 32.4 %collective-permute-start.66 = (f32[108,128]{1,0:T(8,128)S(1)}, f32[108,128]{1,0:T(8,128)S(1)}, u32[]{:S(2)}, u32[]{:S(2)}) collective-permute-start(f32[108,128]{1,0:T(8,128)S(1)} %maximum_bitcast_fusion.3), channel_id=1, source_target_pairs={{0,8},{16,24},{8,0},{24,16},{1,9},{17,25},{9,1},{25,17},{2,10},{18... | collective-permute-start | bytes 165896 | tf_op jit(solution)/shard_map/ppermute | solution.py:123
  480.7 60.8 %collective-permute-start.40 = (bf16[2,2,2,64,2048]{4,3,0,1,2:T(8,128)(2,1)S(1)}, bf16[2,2,2,64,2048]{4,3,0,1,2:T(8,128)(2,1)S(1)}, u32[]{:S(2)}, u32[]{:S(2)}) collective-permute-start(bf16[2,2,2,64,2048]{4,3,0,1,2:T(8,128)(2,1)S(1)} %get-tuple-element.148), channel_id=1, source_target_pairs={{0,1},{1,0},{2,3},{3,2},{4,5},{5,4},{6,7},{7,6},{8,9},{9,8},{10,11... | collective-permute-start | bytes 6291464 | tf_op jit(solution)/shard_map/ppermute | solution.py:36
  484.1 30.6 %collective-permute-start.65 = (bf16[512,1024]{1,0:T(8,128)(2,1)S(1)}, bf16[512,1024]{1,0:T(8,128)(2,1)S(1)}, u32[]{:S(2)}, u32[]{:S(2)}) collective-permute-start(bf16[512,1024]{1,0:T(8,128)(2,1)S(1)} %broadcast_select_fusion.1), channel_id=1, source_target_pairs={{0,8},{16,24},{8,0},{24,16},{1,9},{17,25},{9,1},{25,17},{2,10},{18... | collective-permute-start | bytes 3145736 | tf_op jit(solution)/shard_map/ppermute | solution.py:123
  493.6 40.4 %collective-permute-start.68 = (bf16[512,1024]{1,0:T(8,128)(2,1)S(1)}, bf16[512,1024]{1,0:T(8,128)(2,1)S(1)}, u32[]{:S(2)}, u32[]{:S(2)}) collective-permute-start(bf16[512,1024]{1,0:T(8,128)(2,1)S(1)} %get-tuple-element.198), channel_id=1, source_target_pairs={{0,8},{16,24},{8,0},{24,16},{1,9},{17,25},{9,1},{25,17},{2,10},{18... | collective-permute-start | bytes 3145736 | tf_op jit(solution)/shard_map/ppermute | solution.py:123
  505.4 31.9 %collective-permute-start.59 = (bf16[512,1024]{1,0:T(8,128)(2,1)S(1)}, bf16[512,1024]{1,0:T(8,128)(2,1)S(1)}, u32[]{:S(2)}, u32[]{:S(2)}) collective-permute-start(bf16[512,1024]{1,0:T(8,128)(2,1)S(1)} %add_convert_fusion.9), channel_id=1, source_target_pairs={{8,16},{16,8},{9,17},{17,9},{10,18},{18,10},{11,19},{19,11},{12,20... | collective-permute-start | bytes 3145736 | tf_op jit(solution)/shard_map/ppermute | solution.py:123
  510.3 50.1 %collective-permute-start.58 = (bf16[2,2,2,64,2048]{4,3,0,1,2:T(8,128)(2,1)S(1)}, bf16[2,2,2,64,2048]{4,3,0,1,2:T(8,128)(2,1)S(1)}, u32[]{:S(2)}, u32[]{:S(2)}) collective-permute-start(bf16[2,2,2,64,2048]{4,3,0,1,2:T(8,128)(2,1)S(1)} %get-tuple-element.144), channel_id=1, source_target_pairs={{0,1},{1,0},{2,3},{3,2},{4,5},{5,4},{6,7},{7,6},{8,9},{9,8},{10,11... | collective-permute-start | bytes 6291464 | tf_op jit(solution)/shard_map/ppermute | solution.py:36
  519.6 25.2 %collective-permute-start.71 = (bf16[512,1024]{1,0:T(8,128)(2,1)S(1)}, bf16[512,1024]{1,0:T(8,128)(2,1)S(1)}, u32[]{:S(2)}, u32[]{:S(2)}) collective-permute-start(bf16[512,1024]{1,0:T(8,128)(2,1)S(1)} %add_convert_fusion.3), channel_id=1, source_target_pairs={{8,16},{16,8},{9,17},{17,9},{10,18},{18,10},{11,19},{19,11},{12,20... | collective-permute-start | bytes 3145736 | tf_op jit(solution)/shard_map/ppermute | solution.py:123
  534.4 29.0 %collective-permute-start.73 = (bf16[512,1024]{1,0:T(8,128)(2,1)S(1)}, bf16[512,1024]{1,0:T(8,128)(2,1)S(1)}, u32[]{:S(2)}, u32[]{:S(2)}) collective-permute-start(bf16[512,1024]{1,0:T(8,128)(2,1)S(1)} %add_convert_fusion.1), channel_id=1, source_target_pairs={{8,16},{16,8},{9,17},{17,9},{10,18},{18,10},{11,19},{19,11},{12,20... | collective-permute-start | bytes 3145736 | tf_op jit(solution)/shard_map/ppermute | solution.py:123
  537.3 40.3 %collective-permute-start.70 = (f32[108,128]{1,0:T(8,128)S(1)}, f32[108,128]{1,0:T(8,128)S(1)}, u32[]{:S(2)}, u32[]{:S(2)}) collective-permute-start(f32[108,128]{1,0:T(8,128)S(1)} %fusion.156), channel_id=1, source_target_pairs={{0,8},{16,24},{8,0},{24,16},{1,9},{17,25},{9,1},{25,17},{2,10},{18... | collective-permute-start | bytes 165896 | tf_op jit(solution)/shard_map/ppermute | solution.py:123
  541.5 36.1 %collective-permute-start.60 = (bf16[512,1024]{1,0:T(8,128)(2,1)S(1)}, bf16[512,1024]{1,0:T(8,128)(2,1)S(1)}, u32[]{:S(2)}, u32[]{:S(2)}) collective-permute-start(bf16[512,1024]{1,0:T(8,128)(2,1)S(1)} %add_convert_fusion.8), channel_id=1, source_target_pairs={{0,8},{16,24},{8,0},{24,16},{1,9},{17,25},{9,1},{25,17},{2,10},{18... | collective-permute-start | bytes 3145736 | tf_op jit(solution)/shard_map/ppermute | solution.py:123
  546.1 44.0 %collective-permute-start.72 = (bf16[512,1024]{1,0:T(8,128)(2,1)}, bf16[512,1024]{1,0:T(8,128)(2,1)}, u32[]{:S(2)}, u32[]{:S(2)}) collective-permute-start(bf16[512,1024]{1,0:T(8,128)(2,1)} %add_convert_fusion.2), channel_id=1, source_target_pairs={{0,8},{16,24},{8,0},{24,16},{1,9},{17,25},{9,1},{25,17},{2,10},{18... | collective-permute-start | bytes 3145736 | tf_op jit(solution)/shard_map/ppermute | solution.py:123
  563.8 44.1 %collective-permute-start.74 = (bf16[512,1024]{1,0:T(8,128)(2,1)S(1)}, bf16[512,1024]{1,0:T(8,128)(2,1)S(1)}, u32[]{:S(2)}, u32[]{:S(2)}) collective-permute-start(bf16[512,1024]{1,0:T(8,128)(2,1)S(1)} %add_convert_fusion.refs_1_), channel_id=1, source_target_pairs={{0,8},{16,24},{8,0},{24,16},{1,9},{17,25},{9,1},{25,17},{2,10},{18... | collective-permute-start | bytes 3145736 | tf_op jit(solution)/shard_map/ppermute | solution.py:123
  (133 other events, 1264.2 us)

commit v6 on v5

--- a/solution.py
+++ b/solution.py
@@ -156,6 +156,7 @@
         self.line = line
         self.count = count
         self.chunks = []
+        self.owed = None
         self.final = {}
         self.flying = {}
         self.turn = 0
@@ -165,6 +166,8 @@
 
     def feed(self, chunk):
         self.chunks.append(chunk)
+        if self.owed == len(self.chunks) - 1:
+            self.start(0, self.owed)
 
     def edge(self):
         return (self.line.depth == 0).astype(jnp.int32).reshape(1)
@@ -225,7 +228,10 @@
         self.take(0, n, held[: len(outer)])
         self.start(1, n)
         self.take(1, n - 1, self.waiting(1, n - 1))
-        self.start(0, n + 2)
+        if len(self.chunks) <= n + 2 < self.count:
+            self.owed = n + 2
+        else:
+            self.start(0, n + 2)
         return held[len(outer) :]
 
     def finish(self):
@@ -473,7 +479,7 @@
     grad_resid, grad_ln2_gain, grad_ln2_bias = norm_back(grad_norm_two, raw_two, inv_two, ln2_gain)
     grad_out_rows = rows_of(cotangent).astype(f32)
     grad_mid = grad_out_rows + grad_resid
-    grad_mid_low = gather_rows(grad_mid.astype(bf16), at_calls(bulk.sync, 1))
+    grad_mid_low = gather_rows(grad_mid.astype(bf16), at_calls(bulk.sync, 0))
     grad_attended = dot(grad_mid_low, w_out, ((1,), (1,))).astype(bf16)
     bulk.feed(
         jnp.concatenate(
@@ -483,6 +489,7 @@
             ]
         ),
     )
+    (grad_attended,) = bulk.sync(grad_attended)
     grad_query, grad_keys, grad_vals = attend_back(
         query, keys_vals, grad_attended, pos, valid_windows
     )
@@ -491,7 +498,7 @@
     own = grad_kv[MAX_DOCUMENT:]
     own, active = bulk.sync(own, active)
     mlp_part = dot(active, w_down, ((1,), (0,))).astype(bf16)
-    mlp_total = reduce_rows(mlp_part, at_calls(bulk.sync, 0)).astype(f32)
+    mlp_total = reduce_rows(mlp_part, at_calls(bulk.sync, 1)).astype(f32)
     own, got, mlp_total = bulk.sync(own, got, mlp_total)
     low = rows - MAX_DOCUMENT
     grad_kv = jnp.concatenate([own[:low], own[low:] + got.astype(f32)]).astype(bf16)
@@ -510,7 +517,8 @@
     grad_three = grad_mixed.reshape(rows, 3, local_width)
     back_part = dot(grad_three, w_qkv, ((1, 2), (1, 2))).astype(bf16)
     output = gather_rows((after_attn + b_down + mlp_total).astype(bf16))
-    grad_norm_one = reduce_rows(back_part, at_calls(bulk.sync, 0, 2)).astype(f32)
+    (back_part,) = bulk.sync(back_part)
+    grad_norm_one = reduce_rows(back_part, at_calls(bulk.sync, 1, 2)).astype(f32)
     raw_rows, inv_rows = norm_stats(inputs_rows)
     grad_resid, grad_ln1_gain, grad_ln1_bias = norm_back(
         grad_norm_one, raw_rows, inv_rows, ln1_gain

time: 617 us -> 638 us (1.034)
  starting transfers between devices: 180 us -> 212 us
    ppermute x30, starting transfers between devices: 138 us -> 168 us  [exchange(): return lax.ppermute(value, 'wide', pairs + [(b, a) for a, b in pairs])]
    ppermute x30, waiting for transfers between devices: 72.7 us -> 90.5 us  [exchange(): return lax.ppermute(value, 'wide', pairs + [(b, a) for a, b in pairs])]
    ppermute x43, waiting for transfers between devices: 119 us -> 103 us  [swap(): lax.ppermute(value, 'narrow', [(i, i ^ 1 << bit) for i in range(count)])]
    unnamed x181 -> x203, local copies, waits for them, and re-layouts: 23 us -> 19.9 us
    select_n x21 -> x19, other arithmetic: 13 us -> 14.1 us  [pair(): jnp.where(narrow_bit(bit) == 0, jnp.stack([value, other], axis=dim), jnp....]
  transfers between devices with their start and end apart: 75 -> 75, of which waited for: 38 -> 36; matrix products, arithmetic and copies ran while one was open for 22% -> 21% of each run, Pallas kernels for 3% -> 3%
where the time goes in v6:
time: 638 us; the launch traced here: 631 us
  starting transfers between devices  212 us (33%)
  waiting for transfers between devices  194 us (30%)
  other arithmetic  84.8 us (13%)
  matrix products  61.9 us (10%)
  local copies, waits for them, and re-layouts  44 us (7%)
  Pallas kernels  31.6 us (5%)
    ppermute x30, starting transfers between devices, exchange(): return lax.ppermute(value, 'wide', pairs + [(b, a) for a, b in pairs])  168 us
    ppermute x43, waiting for transfers between devices, swap(): lax.ppermute(value, 'narrow', [(i, i ^ 1 << bit) for i in range(count)])  103 us
    ppermute x30, waiting for transfers between devices, exchange(): return lax.ppermute(value, 'wide', pairs + [(b, a) for a, b in pairs])  90.5 us
    dot_general x23, matrix products, dot(): return lax.dot_general(a, b, (dims, ((), ())), preferred_element_type=f32)  61.9 us
    ppermute x43, starting transfers between devices, swap(): lax.ppermute(value, 'narrow', [(i, i ^ 1 << bit) for i in range(count)])  36.5 us
    convert_element_type x35, other arithmetic, add_low(): return (a.astype(f32) + b.astype(f32)).astype(a.dtype)  22.7 us
    unnamed x203, local copies, waits for them, and re-layouts  19.9 us
    select_n x8, other arithmetic, start(): value = jnp.where(self.line.depth == e, self.chunks[sent], value)  15.7 us
  transfers between devices with their start and end apart: 75, of which 36 were waited for; matrix products, arithmetic and copies ran while one was open for 21% of the time, Pallas kernels for 3%

profile of v6, /device:TPU:0, one launch (start us, length us, event | category | flops | bytes accessed | tf_op | source)
XLA Modules:
  0.0 631.2 jit_solution(6213373431610752311)
XLA Ops:
  11.7 5.8 collective-permute-start
  17.7 4.6 fusion.56.q_ref
  23.2 9.4 %convolution_convert_fusion.3 = bf16[1024,1024]{1,0:T(8,128)(2,1)} fusion(bf16[1024,2048]{1,0:T(8,128)(2,1)} %param.32, bf16[1024,2048]{1,0:T(8,128)(2,1)} %param.28), kind=kOutput, calls=%fused_computation.78 | convolution fusion | flops 4296015872 | bytes 10485760 | tf_op jit(solution)/shard_map/dot_general | solution.py:280
  34.7 8.1 %attend.1 = bf16[1024,256]{1,0:T(8,128)(2,1)S(1)} custom-call(bf16[1024,256]{1,0:T(8,128)(2,1)S(1)} %copy-done.22, bf16[2,1792,256]{2,1,0:T(8,128)(2,1)S(1)} %pad_maximum_fusion.6.k_ref.v_ref, bf16[2,1792,256]{2,1,0:T(8,128)(2,1)S(1)} %pad_maximum_fusion.6.k_ref.v_ref, s32[1024,1]{1,0:T(8,128)S(1)} %copy.57.pos_ref, s32[4,1,1024]{2,1,0:T(1,128)S(1)} %reshape.1066.valid_ref), custom_call_target="tpu_custom_call" | custom-call | tf_op jit(solution)/shard_map/attend/pallas_call | solution.py:334
  61.4 10.0 %collective-permute-done.2 = bf16[2,64,2048]{2,1,0:T(8,128)(2,1)} collective-permute-done((bf16[2,64,2048]{2,1,0:T(8,128)(2,1)}, bf16[2,64,2048]{2,1,0:T(8,128)(2,1)}, u32[]{:S(2)}, u32[]{:S(2)}) %collective-permute-start.2) | collective-permute-done | bytes 524320 | tf_op jit(solution)/shard_map/ppermute | solution.py:36
  89.5 4.7 collective-permute-done.6
  101.2 5.2 collective-permute-done.7
  124.5 7.8 %convert_reduce_fusion = (f32[1024]{0:T(1024)S(1)}, bf16[1024,1024]{1,0:T(8,128)(2,1)S(1)}, bf16[1024,1024]{1,0:T(8,128)(2,1)S(1)}) fusion(f32[1024]{0:T(1024)S(1)} %copy-done.96, bf16[1024,1024]{1,0:T(8,128)(2,1)S(1)} %copy-done.100, bf16[1024,2048]{1,0:T(8,128)(2,1)S(1)} %bitcast.302, bf16[2048,1024]{1,0:T(8,128)(2,1)S(1)} %copy-done.92), kind=kOutput, calls=%fused_computation.30 | convolution fusion | flops 4322229248 | bytes 14688256 | tf_op jit(solution)/shard_map/dot_general | solution.py:280
  132.4 5.0 convolution_convert_fusion.2
  145.9 21.7 %collective-permute-done.11 = bf16[512,1024]{1,0:T(8,128)(2,1)S(1)} collective-permute-done((bf16[512,1024]{1,0:T(8,128)(2,1)S(1)}, bf16[512,1024]{1,0:T(8,128)(2,1)S(1)}, u32[]{:S(2)}, u32[]{:S(2)}) %collective-permute-start.11) | collective-permute-done | bytes 1048608 | tf_op jit(solution)/shard_map/ppermute | solution.py:123
  174.2 7.2 %collective-permute-done.19 = bf16[2,64,2048]{2,1,0:T(8,128)(2,1)S(1)} collective-permute-done((bf16[2,64,2048]{2,1,0:T(8,128)(2,1)S(1)}, bf16[2,64,2048]{2,1,0:T(8,128)(2,1)S(1)}, u32[]{:S(2)}, u32[]{:S(2)}) %collective-permute-start.19) | collective-permute-done | bytes 524320 | tf_op jit(solution)/shard_map/ppermute | solution.py:36
  182.3 5.8 collective-permute-done.17
  203.2 4.6 collective-permute-done.22
  217.1 8.3 %collective-permute-done.23 = bf16[2,64,2048]{2,1,0:T(8,128)(2,1)S(1)} collective-permute-done((bf16[2,64,2048]{2,1,0:T(8,128)(2,1)S(1)}, bf16[2,64,2048]{2,1,0:T(8,128)(2,1)S(1)}, u32[]{:S(2)}, u32[]{:S(2)}) %collective-permute-start.23) | collective-permute-done | bytes 524320 | tf_op jit(solution)/shard_map/ppermute | solution.py:36
  237.1 24.4 %collective-permute-start.14 = (bf16[512,1024]{1,0:T(8,128)(2,1)S(1)}, bf16[512,1024]{1,0:T(8,128)(2,1)S(1)}, u32[]{:S(2)}, u32[]{:S(2)}) collective-permute-start(bf16[512,1024]{1,0:T(8,128)(2,1)S(1)} %get-tuple-element.135), channel_id=1, source_target_pairs={{0,8},{16,24},{8,0},{24,16},{1,9},{17,25},{9,1},{25,17},{2,10},{18... | collective-permute-start | bytes 3145736 | tf_op jit(solution)/shard_map/ppermute | solution.py:123
  265.9 18.0 %collective-permute-start.29 = (bf16[512,1024]{1,0:T(8,128)(2,1)S(1)}, bf16[512,1024]{1,0:T(8,128)(2,1)S(1)}, u32[]{:S(2)}, u32[]{:S(2)}) collective-permute-start(bf16[512,1024]{1,0:T(8,128)(2,1)S(1)} %get-tuple-element.131), channel_id=1, source_target_pairs={{0,8},{16,24},{8,0},{24,16},{1,9},{17,25},{9,1},{25,17},{2,10},{18... | collective-permute-start | bytes 3145736 | tf_op jit(solution)/shard_map/ppermute | solution.py:123
  286.5 12.1 %attend_back.1 = (bf16[1024,256]{1,0:T(8,128)(2,1)S(1)}, f32[1792,256]{1,0:T(8,128)S(1)}, f32[1792,256]{1,0:T(8,128)S(1)}) custom-call(bf16[1024,256]{1,0:T(8,128)(2,1)S(1)} %copy-done.23, bf16[2,1792,256]{2,1,0:T(8,128)(2,1)S(1)} %pad_maximum_fusion.6.k_ref.v_ref, bf16[2,1792,256]{2,1,0:T(8,128)(2,1)S(1)} %pad_maximum_fusion.6.k_ref.v_ref, ...), custom_call_target="tpu_custom_call" | custom-call | tf_op jit(solution)/shard_map/attend_back/pallas_call | solution.py:351
  299.3 4.9 collective-permute-done.29.refs_5_
  304.2 4.7 convolution_convert_fusion.1
  323.0 18.1 %collective-permute-start.27 = (bf16[512,1024]{1,0:T(8,128)(2,1)S(1)}, bf16[512,1024]{1,0:T(8,128)(2,1)S(1)}, u32[]{:S(2)}, u32[]{:S(2)}) collective-permute-start(bf16[512,1024]{1,0:T(8,128)(2,1)S(1)} %get-tuple-element.133), channel_id=1, source_target_pairs={{0,8},{16,24},{8,0},{24,16},{1,9},{17,25},{9,1},{25,17},{2,10},{18... | collective-permute-start | bytes 3145736 | tf_op jit(solution)/shard_map/ppermute | solution.py:123
  346.4 8.4 %collective-permute-done.35 = bf16[2,64,2048]{2,1,0:T(8,128)(2,1)S(1)} collective-permute-done((bf16[2,64,2048]{2,1,0:T(8,128)(2,1)S(1)}, bf16[2,64,2048]{2,1,0:T(8,128)(2,1)S(1)}, u32[]{:S(2)}, u32[]{:S(2)}) %collective-permute-start.35) | collective-permute-done | bytes 524320 | tf_op jit(solution)/shard_map/ppermute | solution.py:36
  354.9 26.9 %collective-permute-start.46 = (bf16[512,1024]{1,0:T(8,128)(2,1)}, bf16[512,1024]{1,0:T(8,128)(2,1)S(1)}, u32[]{:S(2)}, u32[]{:S(2)}) collective-permute-start(bf16[512,1024]{1,0:T(8,128)(2,1)} %get-tuple-element.125), channel_id=1, source_target_pairs={{0,8},{16,24},{8,0},{24,16},{1,9},{17,25},{9,1},{25,17},{2,10},{18... | collective-permute-start | bytes 3145736 | tf_op jit(solution)/shard_map/ppermute | solution.py:123
  384.9 4.5 collective-permute-done.36
  421.7 11.0 %collective-permute-start.44 = (bf16[512,1024]{1,0:T(8,128)(2,1)S(1)}, bf16[512,1024]{1,0:T(8,128)(2,1)S(1)}, u32[]{:S(2)}, u32[]{:S(2)}) collective-permute-start(bf16[512,1024]{1,0:T(8,128)(2,1)S(1)} %get-tuple-element.127), channel_id=1, source_target_pairs={{0,8},{16,24},{8,0},{24,16},{1,9},{17,25},{9,1},{25,17},{2,10},{18... | collective-permute-start | bytes 3145736 | tf_op jit(solution)/shard_map/ppermute | solution.py:123
  434.3 16.7 %collective-permute-start.55 = (bf16[512,1024]{1,0:T(8,128)(2,1)S(1)}, bf16[512,1024]{1,0:T(8,128)(2,1)S(1)}, u32[]{:S(2)}, u32[]{:S(2)}) collective-permute-start(bf16[512,1024]{1,0:T(8,128)(2,1)S(1)} %get-tuple-element.123), channel_id=1, source_target_pairs={{0,8},{16,24},{8,0},{24,16},{1,9},{17,25},{9,1},{25,17},{2,10},{18... | collective-permute-start | bytes 3145736 | tf_op jit(solution)/shard_map/ppermute | solution.py:123
  455.8 14.5 %collective-permute-start.53 = (bf16[512,1024]{1,0:T(8,128)(2,1)}, bf16[512,1024]{1,0:T(8,128)(2,1)}, u32[]{:S(2)}, u32[]{:S(2)}) collective-permute-start(bf16[512,1024]{1,0:T(8,128)(2,1)} %broadcast_select_fusion.1), channel_id=1, source_target_pairs={{0,8},{16,24},{8,0},{24,16},{1,9},{17,25},{9,1},{25,17},{2,10},{18... | collective-permute-start | bytes 3145736 | tf_op jit(solution)/shard_map/ppermute | solution.py:123
  501.3 6.0 collective-permute-done.58
  536.5 5.2 collective-permute-start.51
  548.7 16.9 %collective-permute-done.51 = bf16[512,1024]{1,0:T(8,128)(2,1)S(1)} collective-permute-done((bf16[512,1024]{1,0:T(8,128)(2,1)S(1)}, bf16[512,1024]{1,0:T(8,128)(2,1)S(1)}, u32[]{:S(2)}, u32[]{:S(2)}) %collective-permute-start.51) | collective-permute-done | bytes 1048608 | tf_op jit(solution)/shard_map/ppermute | solution.py:123
  569.7 18.4 %collective-permute-done.69 = bf16[512,1024]{1,0:T(8,128)(2,1)S(1)} collective-permute-done((bf16[512,1024]{1,0:T(8,128)(2,1)S(1)}, bf16[512,1024]{1,0:T(8,128)(2,1)S(1)}, u32[]{:S(2)}, u32[]{:S(2)}) %collective-permute-start.69) | collective-permute-done | bytes 1048608 | tf_op jit(solution)/shard_map/ppermute | solution.py:123
  589.2 17.9 %collective-permute-done.72 = bf16[512,1024]{1,0:T(8,128)(2,1)S(1)} collective-permute-done((bf16[512,1024]{1,0:T(8,128)(2,1)S(1)}, bf16[512,1024]{1,0:T(8,128)(2,1)S(1)}, u32[]{:S(2)}, u32[]{:S(2)}) %collective-permute-start.72) | collective-permute-done | bytes 1048608 | tf_op jit(solution)/shard_map/ppermute | solution.py:123
  620.0 7.5 %collective-permute-done.64.refs_2_ = bf16[512,1024]{1,0:T(8,128)(2,1)S(1)} collective-permute-done((bf16[512,1024]{1,0:T(8,128)(2,1)S(1)}, bf16[512,1024]{1,0:T(8,128)(2,1)S(1)}, u32[]{:S(2)}, u32[]{:S(2)}) %collective-permute-start.64) | collective-permute-done | bytes 1048608 | tf_op jit(solution)/shard_map/ppermute | solution.py:123
  (512 shorter events, 283.5 us)
Async XLA Ops:
  140.9 26.7 %collective-permute-start.11 = (bf16[512,1024]{1,0:T(8,128)(2,1)S(1)}, bf16[512,1024]{1,0:T(8,128)(2,1)S(1)}, u32[]{:S(2)}, u32[]{:S(2)}) collective-permute-start(bf16[512,1024]{1,0:T(8,128)(2,1)S(1)} %fusion.35), channel_id=1, source_target_pairs={{0,8},{16,24},{8,0},{24,16},{1,9},{17,25},{9,1},{25,17},{2,10},{18... | collective-permute-start | bytes 3145736 | tf_op jit(solution)/shard_map/ppermute | solution.py:123
  144.9 49.8 %collective-permute-start.16 = (bf16[512,1024]{1,0:T(8,128)(2,1)S(1)}, bf16[512,1024]{1,0:T(8,128)(2,1)S(1)}, u32[]{:S(2)}, u32[]{:S(2)}) collective-permute-start(bf16[512,1024]{1,0:T(8,128)(2,1)S(1)} %fusion.32), channel_id=1, source_target_pairs={{0,8},{16,24},{8,0},{24,16},{1,9},{17,25},{9,1},{25,17},{2,10},{18... | collective-permute-start | bytes 3145736 | tf_op jit(solution)/shard_map/ppermute | solution.py:123
  171.4 40.7 %collective-permute-start.15 = (bf16[512,1024]{1,0:T(8,128)(2,1)}, bf16[512,1024]{1,0:T(8,128)(2,1)}, u32[]{:S(2)}, u32[]{:S(2)}) collective-permute-start(bf16[512,1024]{1,0:T(8,128)(2,1)} %fusion.38), channel_id=1, source_target_pairs={{0,8},{16,24},{8,0},{24,16},{1,9},{17,25},{9,1},{25,17},{2,10},{18... | collective-permute-start | bytes 3145736 | tf_op jit(solution)/shard_map/ppermute | solution.py:123
  228.7 55.2 %collective-permute-start.25 = (bf16[2,2,2,64,2048]{4,3,1,2,0:T(8,128)(2,1)S(1)}, bf16[2,2,2,64,2048]{4,3,1,2,0:T(8,128)(2,1)S(1)}, u32[]{:S(2)}, u32[]{:S(2)}) collective-permute-start(bf16[2,2,2,64,2048]{4,3,1,2,0:T(8,128)(2,1)S(1)} %get-tuple-element.164), channel_id=1, source_target_pairs={{0,1},{1,0},{2,3},{3,2},{4,5},{5,4},{6,7},{7,6},{8,9},{9,8},{10,11... | collective-permute-start | bytes 6291464 | tf_op jit(solution)/shard_map/ppermute | solution.py:36
  231.6 32.6 %collective-permute-start.28 = (bf16[512,1024]{1,0:T(8,128)(2,1)S(1)}, bf16[512,1024]{1,0:T(8,128)(2,1)S(1)}, u32[]{:S(2)}, u32[]{:S(2)}) collective-permute-start(bf16[512,1024]{1,0:T(8,128)(2,1)S(1)} %add_convert_fusion.19), channel_id=1, source_target_pairs={{8,16},{16,8},{9,17},{17,9},{10,18},{18,10},{11,19},{19,11},{12,20... | collective-permute-start | bytes 3145736 | tf_op jit(solution)/shard_map/ppermute | solution.py:123
  237.1 49.4 %collective-permute-start.14 = (bf16[512,1024]{1,0:T(8,128)(2,1)S(1)}, bf16[512,1024]{1,0:T(8,128)(2,1)S(1)}, u32[]{:S(2)}, u32[]{:S(2)}) collective-permute-start(bf16[512,1024]{1,0:T(8,128)(2,1)S(1)} %get-tuple-element.135), channel_id=1, source_target_pairs={{0,8},{16,24},{8,0},{24,16},{1,9},{17,25},{9,1},{25,17},{2,10},{18... | collective-permute-start | bytes 3145736 | tf_op jit(solution)/shard_map/ppermute | solution.py:123
  263.5 46.9 %collective-permute-start.31 = (bf16[512,1024]{1,0:T(8,128)(2,1)S(1)}, bf16[512,1024]{1,0:T(8,128)(2,1)S(1)}, u32[]{:S(2)}, u32[]{:S(2)}) collective-permute-start(bf16[512,1024]{1,0:T(8,128)(2,1)S(1)} %add_convert_fusion.17), channel_id=1, source_target_pairs={{8,16},{16,8},{9,17},{17,9},{10,18},{18,10},{11,19},{19,11},{12,20... | collective-permute-start | bytes 3145736 | tf_op jit(solution)/shard_map/ppermute | solution.py:123
  265.9 38.3 %collective-permute-start.29 = (bf16[512,1024]{1,0:T(8,128)(2,1)S(1)}, bf16[512,1024]{1,0:T(8,128)(2,1)S(1)}, u32[]{:S(2)}, u32[]{:S(2)}) collective-permute-start(bf16[512,1024]{1,0:T(8,128)(2,1)S(1)} %get-tuple-element.131), channel_id=1, source_target_pairs={{0,8},{16,24},{8,0},{24,16},{1,9},{17,25},{9,1},{25,17},{2,10},{18... | collective-permute-start | bytes 3145736 | tf_op jit(solution)/shard_map/ppermute | solution.py:123
  309.1 31.9 %collective-permute-start.33 = (bf16[512,2048]{1,0:T(8,128)(2,1)S(1)}, bf16[512,2048]{1,0:T(8,128)(2,1)S(1)}, u32[]{:S(2)}, u32[]{:S(2)}) collective-permute-start(bf16[512,2048]{1,0:T(8,128)(2,1)S(1)} %dynamic-slice_bitcast_fusion.1), channel_id=1, source_target_pairs={{0,1},{1,0},{2,3},{3,2},{4,5},{5,4},{6,7},{7,6},{8,9},{9,8},{10,11... | collective-permute-start | bytes 6291464 | tf_op jit(solution)/shard_map/ppermute | solution.py:36
  312.2 69.8 %collective-permute-start.32 = (bf16[512,1024]{1,0:T(8,128)(2,1)S(1)}, bf16[512,1024]{1,0:T(8,128)(2,1)S(1)}, u32[]{:S(2)}, u32[]{:S(2)}) collective-permute-start(bf16[512,1024]{1,0:T(8,128)(2,1)S(1)} %get-tuple-element.129), channel_id=1, source_target_pairs={{0,8},{16,24},{8,0},{24,16},{1,9},{17,25},{9,1},{25,17},{2,10},{18... | collective-permute-start | bytes 3145736 | tf_op jit(solution)/shard_map/ppermute | solution.py:123
  316.8 75.5 %collective-permute-start.30 = (bf16[768,512]{1,0:T(8,128)(2,1)S(1)}, bf16[768,512]{1,0:T(8,128)(2,1)S(1)}, u32[]{:S(2)}, u32[]{:S(2)}) collective-permute-start(bf16[768,512]{1,0:T(8,128)(2,1)S(1)} %slice.406), channel_id=1, source_target_pairs={{8,0},{16,8},{24,16},{9,1},{17,9},{25,17},{10,2},{18,10},{26,18},{... | collective-permute-start | bytes 2359304 | tf_op jit(solution)/shard_map/ppermute | solution.py:497
  318.9 24.0 %collective-permute-start.45 = (bf16[512,1024]{1,0:T(8,128)(2,1)S(1)}, bf16[512,1024]{1,0:T(8,128)(2,1)S(1)}, u32[]{:S(2)}, u32[]{:S(2)}) collective-permute-start(bf16[512,1024]{1,0:T(8,128)(2,1)S(1)} %add_convert_fusion.13), channel_id=1, source_target_pairs={{8,16},{16,8},{9,17},{17,9},{10,18},{18,10},{11,19},{19,11},{12,20... | collective-permute-start | bytes 3145736 | tf_op jit(solution)/shard_map/ppermute | solution.py:123
  323.0 69.4 %collective-permute-start.27 = (bf16[512,1024]{1,0:T(8,128)(2,1)S(1)}, bf16[512,1024]{1,0:T(8,128)(2,1)S(1)}, u32[]{:S(2)}, u32[]{:S(2)}) collective-permute-start(bf16[512,1024]{1,0:T(8,128)(2,1)S(1)} %get-tuple-element.133), channel_id=1, source_target_pairs={{0,8},{16,24},{8,0},{24,16},{1,9},{17,25},{9,1},{25,17},{2,10},{18... | collective-permute-start | bytes 3145736 | tf_op jit(solution)/shard_map/ppermute | solution.py:123
  342.9 39.0 %collective-permute-start.34 = (bf16[2,64,2048]{2,1,0:T(8,128)(2,1)S(1)}, bf16[2,64,2048]{2,1,0:T(8,128)(2,1)S(1)}, u32[]{:S(2)}, u32[]{:S(2)}) collective-permute-start(bf16[2,64,2048]{2,1,0:T(8,128)(2,1)S(1)} %dynamic-slice_bitcast_fusion.7), channel_id=1, source_target_pairs={{0,2},{1,3},{2,0},{3,1},{4,6},{5,7},{6,4},{7,5},{8,10},{9,11},{10,... | collective-permute-start | bytes 1572872 | tf_op jit(solution)/shard_map/ppermute | solution.py:36
  354.9 49.8 %collective-permute-start.46 = (bf16[512,1024]{1,0:T(8,128)(2,1)}, bf16[512,1024]{1,0:T(8,128)(2,1)S(1)}, u32[]{:S(2)}, u32[]{:S(2)}) collective-permute-start(bf16[512,1024]{1,0:T(8,128)(2,1)} %get-tuple-element.125), channel_id=1, source_target_pairs={{0,8},{16,24},{8,0},{24,16},{1,9},{17,25},{9,1},{25,17},{2,10},{18... | collective-permute-start | bytes 3145736 | tf_op jit(solution)/shard_map/ppermute | solution.py:123
  389.4 28.8 %collective-permute-start.43 = (bf16[512,1024]{1,0:T(8,128)(2,1)}, bf16[512,1024]{1,0:T(8,128)(2,1)}, u32[]{:S(2)}, u32[]{:S(2)}) collective-permute-start(bf16[512,1024]{1,0:T(8,128)(2,1)} %add_convert_fusion.15), channel_id=1, source_target_pairs={{8,16},{16,8},{9,17},{17,9},{10,18},{18,10},{11,19},{19,11},{12,20... | collective-permute-start | bytes 3145736 | tf_op jit(solution)/shard_map/ppermute | solution.py:123
  404.9 46.1 %collective-permute-start.47 = (bf16[512,2048]{1,0:T(8,128)(2,1)S(1)}, bf16[512,2048]{1,0:T(8,128)(2,1)S(1)}, u32[]{:S(2)}, u32[]{:S(2)}) collective-permute-start(bf16[512,2048]{1,0:T(8,128)(2,1)S(1)} %dynamic-slice_bitcast_fusion), channel_id=1, source_target_pairs={{0,1},{1,0},{2,3},{3,2},{4,5},{5,4},{6,7},{7,6},{8,9},{9,8},{10,11... | collective-permute-start | bytes 6291464 | tf_op jit(solution)/shard_map/ppermute | solution.py:36
  406.3 26.4 %collective-permute-start.54 = (bf16[512,1024]{1,0:T(8,128)(2,1)S(1)}, bf16[512,1024]{1,0:T(8,128)(2,1)S(1)}, u32[]{:S(2)}, u32[]{:S(2)}) collective-permute-start(bf16[512,1024]{1,0:T(8,128)(2,1)S(1)} %add_convert_fusion.7), channel_id=1, source_target_pairs={{8,16},{16,8},{9,17},{17,9},{10,18},{18,10},{11,19},{19,11},{12,20... | collective-permute-start | bytes 3145736 | tf_op jit(solution)/shard_map/ppermute | solution.py:123
  409.8 44.5 %collective-permute-start.52 = (bf16[512,1024]{1,0:T(8,128)(2,1)S(1)}, bf16[512,1024]{1,0:T(8,128)(2,1)S(1)}, u32[]{:S(2)}, u32[]{:S(2)}) collective-permute-start(bf16[512,1024]{1,0:T(8,128)(2,1)S(1)} %add_convert_fusion.9), channel_id=1, source_target_pairs={{8,16},{16,8},{9,17},{17,9},{10,18},{18,10},{11,19},{19,11},{12,20... | collective-permute-start | bytes 3145736 | tf_op jit(solution)/shard_map/ppermute | solution.py:123
  421.7 49.0 %collective-permute-start.44 = (bf16[512,1024]{1,0:T(8,128)(2,1)S(1)}, bf16[512,1024]{1,0:T(8,128)(2,1)S(1)}, u32[]{:S(2)}, u32[]{:S(2)}) collective-permute-start(bf16[512,1024]{1,0:T(8,128)(2,1)S(1)} %get-tuple-element.127), channel_id=1, source_target_pairs={{0,8},{16,24},{8,0},{24,16},{1,9},{17,25},{9,1},{25,17},{2,10},{18... | collective-permute-start | bytes 3145736 | tf_op jit(solution)/shard_map/ppermute | solution.py:123
  434.3 44.9 %collective-permute-start.55 = (bf16[512,1024]{1,0:T(8,128)(2,1)S(1)}, bf16[512,1024]{1,0:T(8,128)(2,1)S(1)}, u32[]{:S(2)}, u32[]{:S(2)}) collective-permute-start(bf16[512,1024]{1,0:T(8,128)(2,1)S(1)} %get-tuple-element.123), channel_id=1, source_target_pairs={{0,8},{16,24},{8,0},{24,16},{1,9},{17,25},{9,1},{25,17},{2,10},{18... | collective-permute-start | bytes 3145736 | tf_op jit(solution)/shard_map/ppermute | solution.py:123
  455.8 52.8 %collective-permute-start.53 = (bf16[512,1024]{1,0:T(8,128)(2,1)}, bf16[512,1024]{1,0:T(8,128)(2,1)}, u32[]{:S(2)}, u32[]{:S(2)}) collective-permute-start(bf16[512,1024]{1,0:T(8,128)(2,1)} %broadcast_select_fusion.1), channel_id=1, source_target_pairs={{0,8},{16,24},{8,0},{24,16},{1,9},{17,25},{9,1},{25,17},{2,10},{18... | collective-permute-start | bytes 3145736 | tf_op jit(solution)/shard_map/ppermute | solution.py:123
  474.2 46.9 %collective-permute-start.50 = (bf16[512,1024]{1,0:T(8,128)(2,1)}, bf16[512,1024]{1,0:T(8,128)(2,1)}, u32[]{:S(2)}, u32[]{:S(2)}) collective-permute-start(bf16[512,1024]{1,0:T(8,128)(2,1)} %add_convert_fusion.11), channel_id=1, source_target_pairs={{8,16},{16,8},{9,17},{17,9},{10,18},{18,10},{11,19},{19,11},{12,20... | collective-permute-start | bytes 3145736 | tf_op jit(solution)/shard_map/ppermute | solution.py:123
  484.6 58.2 %collective-permute-start.68 = (bf16[512,1024]{1,0:T(8,128)(2,1)}, bf16[512,1024]{1,0:T(8,128)(2,1)}, u32[]{:S(2)}, u32[]{:S(2)}) collective-permute-start(bf16[512,1024]{1,0:T(8,128)(2,1)} %add_convert_fusion.3), channel_id=1, source_target_pairs={{8,16},{16,8},{9,17},{17,9},{10,18},{18,10},{11,19},{19,11},{12,20... | collective-permute-start | bytes 3145736 | tf_op jit(solution)/shard_map/ppermute | solution.py:123
  508.7 60.9 %collective-permute-start.70 = (f32[108,128]{1,0:T(8,128)S(1)}, f32[108,128]{1,0:T(8,128)S(1)}, u32[]{:S(2)}, u32[]{:S(2)}) collective-permute-start(f32[108,128]{1,0:T(8,128)S(1)} %maximum_bitcast_fusion.3), channel_id=1, source_target_pairs={{0,8},{16,24},{8,0},{24,16},{1,9},{17,25},{9,1},{25,17},{2,10},{18... | collective-permute-start | bytes 165896 | tf_op jit(solution)/shard_map/ppermute | solution.py:123
  514.4 33.8 %collective-permute-start.71 = (bf16[512,1024]{1,0:T(8,128)(2,1)S(1)}, bf16[512,1024]{1,0:T(8,128)(2,1)S(1)}, u32[]{:S(2)}, u32[]{:S(2)}) collective-permute-start(bf16[512,1024]{1,0:T(8,128)(2,1)S(1)} %add_convert_fusion.1), channel_id=1, source_target_pairs={{8,16},{16,8},{9,17},{17,9},{10,18},{18,10},{11,19},{19,11},{12,20... | collective-permute-start | bytes 3145736 | tf_op jit(solution)/shard_map/ppermute | solution.py:123
  536.5 29.2 %collective-permute-start.51 = (bf16[512,1024]{1,0:T(8,128)(2,1)S(1)}, bf16[512,1024]{1,0:T(8,128)(2,1)S(1)}, u32[]{:S(2)}, u32[]{:S(2)}) collective-permute-start(bf16[512,1024]{1,0:T(8,128)(2,1)S(1)} %get-tuple-element.208), channel_id=1, source_target_pairs={{0,8},{16,24},{8,0},{24,16},{1,9},{17,25},{9,1},{25,17},{2,10},{18... | collective-permute-start | bytes 3145736 | tf_op jit(solution)/shard_map/ppermute | solution.py:123
  542.6 71.4 %collective-permute-start.42 = (bf16[2,2,2,64,2048]{4,3,0,1,2:T(8,128)(2,1)S(1)}, bf16[2,2,2,64,2048]{4,3,0,1,2:T(8,128)(2,1)S(1)}, u32[]{:S(2)}, u32[]{:S(2)}) collective-permute-start(bf16[2,2,2,64,2048]{4,3,0,1,2:T(8,128)(2,1)S(1)} %get-tuple-element.160), channel_id=1, source_target_pairs={{0,1},{1,0},{2,3},{3,2},{4,5},{5,4},{6,7},{7,6},{8,9},{9,8},{10,11... | collective-permute-start | bytes 6291464 | tf_op jit(solution)/shard_map/ppermute | solution.py:36
  544.8 43.4 %collective-permute-start.69 = (bf16[512,1024]{1,0:T(8,128)(2,1)S(1)}, bf16[512,1024]{1,0:T(8,128)(2,1)S(1)}, u32[]{:S(2)}, u32[]{:S(2)}) collective-permute-start(bf16[512,1024]{1,0:T(8,128)(2,1)S(1)} %add_convert_fusion.2), channel_id=1, source_target_pairs={{0,8},{16,24},{8,0},{24,16},{1,9},{17,25},{9,1},{25,17},{2,10},{18... | collective-permute-start | bytes 3145736 | tf_op jit(solution)/shard_map/ppermute | solution.py:123
  548.6 58.5 %collective-permute-start.72 = (bf16[512,1024]{1,0:T(8,128)(2,1)S(1)}, bf16[512,1024]{1,0:T(8,128)(2,1)S(1)}, u32[]{:S(2)}, u32[]{:S(2)}) collective-permute-start(bf16[512,1024]{1,0:T(8,128)(2,1)S(1)} %add_convert_fusion), channel_id=1, source_target_pairs={{0,8},{16,24},{8,0},{24,16},{1,9},{17,25},{9,1},{25,17},{2,10},{18... | collective-permute-start | bytes 3145736 | tf_op jit(solution)/shard_map/ppermute | solution.py:123
  566.1 44.3 %collective-permute-start.63 = (bf16[512,1024]{1,0:T(8,128)(2,1)S(1)}, bf16[512,1024]{1,0:T(8,128)(2,1)S(1)}, u32[]{:S(2)}, u32[]{:S(2)}) collective-permute-start(bf16[512,1024]{1,0:T(8,128)(2,1)S(1)} %add_convert_fusion.5), channel_id=1, source_target_pairs={{8,16},{16,8},{9,17},{17,9},{10,18},{18,10},{11,19},{19,11},{12,20... | collective-permute-start | bytes 3145736 | tf_op jit(solution)/shard_map/ppermute | solution.py:123
  569.6 47.4 %collective-permute-start.62 = (bf16[2,2,2,64,2048]{4,3,0,1,2:T(8,128)(2,1)S(1)}, bf16[2,2,2,64,2048]{4,3,0,1,2:T(8,128)(2,1)S(1)}, u32[]{:S(2)}, u32[]{:S(2)}) collective-permute-start(bf16[2,2,2,64,2048]{4,3,0,1,2:T(8,128)(2,1)S(1)} %get-tuple-element.156), channel_id=1, source_target_pairs={{0,1},{1,0},{2,3},{3,2},{4,5},{5,4},{6,7},{7,6},{8,9},{9,8},{10,11... | collective-permute-start | bytes 6291464 | tf_op jit(solution)/shard_map/ppermute | solution.py:36
  (144 other events, 1448.8 us)

commit v7 on v6

--- a/solution.py
+++ b/solution.py
@@ -139,7 +139,7 @@
             plan.append((e, sent, got, add))
         return plan
 
-    def whole(self, value, sync):
+    def whole(self, value, sync, middle):
         stream = Stream(self, 1)
         stream.feed(value)
         for slot in range(stream.slots()):
@@ -147,7 +147,7 @@
                 stream.start(kind, slot)
                 got = stream.waiting(kind, slot)
                 if got:
-                    stream.take(kind, slot, sync(*got))
+                    stream.take(kind, slot, (middle if kind else sync)(*got))
         return stream.result(0)
 
 
@@ -498,8 +498,14 @@
     own = grad_kv[MAX_DOCUMENT:]
     own, active = bulk.sync(own, active)
     mlp_part = dot(active, w_down, ((1,), (0,))).astype(bf16)
-    mlp_total = reduce_rows(mlp_part, at_calls(bulk.sync, 1)).astype(f32)
-    own, got, mlp_total = bulk.sync(own, got, mlp_total)
+    held = [own, got]
+
+    def sync_held(*values):
+        *values, held[0], held[1] = bulk.sync(*values, *held)
+        return values
+
+    mlp_total = reduce_rows(mlp_part, at_calls(sync_held, 1)).astype(f32)
+    own, got = held
     low = rows - MAX_DOCUMENT
     grad_kv = jnp.concatenate([own[:low], own[low:] + got.astype(f32)]).astype(bf16)
     grad_mixed = jnp.concatenate([grad_query, grad_kv], axis=1)
@@ -512,6 +518,7 @@
         extra = rest[:, i * local_width : (i + 1) * local_width]
         bulk.feed(jnp.concatenate([parts[i], extra], axis=1))
     bulk.feed(ups[3])
+    grad_mixed, mlp_total = bulk.sync(grad_mixed, mlp_total)
     grad_b_qv = jnp.sum(grad_mixed.astype(f32), axis=0)
     grad_b_qv = [grad_b_qv[i * local_width : (i + 1) * local_width] for i in (0, 2)]
     grad_three = grad_mixed.reshape(rows, 3, local_width)
@@ -538,7 +545,14 @@
         )
     )
     sums = jnp.concatenate([sums.reshape(-1), grad_b_up] + grad_b_qv)
-    sums = line.whole(sums.reshape(-1, 128), bulk.sync).reshape(-1)
+    ready = [grad_input]
+
+    def sync_ready(value):
+        value, ready[0] = bulk.sync(value, ready[0])
+        return (value,)
+
+    sums = line.whole(sums.reshape(-1, 128), bulk.sync, sync_ready).reshape(-1)
+    (grad_input,) = ready
     bulk.finish()
     grad_ln2_gain, grad_ln2_bias, grad_b_out, grad_b_down, grad_ln1_gain, grad_ln1_bias = sums[
         : 6 * width

time: 638 us -> 650 us (1.019)
  starting transfers between devices: 212 us -> 238 us
  waiting for transfers between devices: 194 us -> 173 us
    ppermute x30, starting transfers between devices: 168 us -> 193 us  [exchange(): return lax.ppermute(value, 'wide', pairs + [(b, a) for a, b in pairs])]
    ppermute x30, waiting for transfers between devices: 90.5 us -> 72.2 us  [exchange(): return lax.ppermute(value, 'wide', pairs + [(b, a) for a, b in pairs])]
    unnamed x203 -> x199, local copies, waits for them, and re-layouts: 19.9 us -> 21.6 us
  transfers between devices with their start and end apart: 75 -> 75, of which waited for: 36 -> 33; matrix products, arithmetic and copies ran while one was open for 21% -> 21% of each run, Pallas kernels for 3% -> 3%
where the time goes in v7:
time: 650 us; the launch traced here: 643 us
  starting transfers between devices  238 us (37%)
  waiting for transfers between devices  173 us (27%)
  other arithmetic  85.5 us (13%)
  matrix products  66.4 us (10%)
  local copies, waits for them, and re-layouts  46.1 us (7%)
  Pallas kernels  31.3 us (5%)
    ppermute x30, starting transfers between devices, exchange(): return lax.ppermute(value, 'wide', pairs + [(b, a) for a, b in pairs])  193 us
    ppermute x43, waiting for transfers between devices, swap(): lax.ppermute(value, 'narrow', [(i, i ^ 1 << bit) for i in range(count)])  100 us
    ppermute x30, waiting for transfers between devices, exchange(): return lax.ppermute(value, 'wide', pairs + [(b, a) for a, b in pairs])  72.2 us
    dot_general x23, matrix products, dot(): return lax.dot_general(a, b, (dims, ((), ())), preferred_element_type=f32)  66.4 us
    ppermute x43, starting transfers between devices, swap(): lax.ppermute(value, 'narrow', [(i, i ^ 1 << bit) for i in range(count)])  37 us
    unnamed x199, local copies, waits for them, and re-layouts  21.6 us
    convert_element_type x35, other arithmetic, add_low(): return (a.astype(f32) + b.astype(f32)).astype(a.dtype)  21.1 us
    select_n x8, other arithmetic, start(): value = jnp.where(self.line.depth == e, self.chunks[sent], value)  15.4 us
  transfers between devices with their start and end apart: 75, of which 33 were waited for; matrix products, arithmetic and copies ran while one was open for 21% of the time, Pallas kernels for 3%

profile of v7, /device:TPU:0, one launch (start us, length us, event | category | flops | bytes accessed | tf_op | source)
XLA Modules:
  0.0 643.1 jit_solution(16811609583364865293)
XLA Ops:
  11.7 5.8 collective-permute-start
  23.2 9.4 %convolution_convert_fusion.3 = bf16[1024,1024]{1,0:T(8,128)(2,1)} fusion(bf16[1024,2048]{1,0:T(8,128)(2,1)} %param.32, bf16[1024,2048]{1,0:T(8,128)(2,1)} %param.28), kind=kOutput, calls=%fused_computation.78 | convolution fusion | flops 4296015872 | bytes 10485760 | tf_op jit(solution)/shard_map/dot_general | solution.py:280
  34.7 7.8 %attend.1 = bf16[1024,256]{1,0:T(8,128)(2,1)S(1)} custom-call(bf16[1024,256]{1,0:T(8,128)(2,1)S(1)} %copy-done.22, bf16[2,1792,256]{2,1,0:T(8,128)(2,1)S(1)} %pad_maximum_fusion.6.k_ref.v_ref, bf16[2,1792,256]{2,1,0:T(8,128)(2,1)S(1)} %pad_maximum_fusion.6.k_ref.v_ref, s32[1024,1]{1,0:T(8,128)S(1)} %copy.57.pos_ref, s32[4,1,1024]{2,1,0:T(1,128)S(1)} %reshape.1066.valid_ref), custom_call_target="tpu_custom_call" | custom-call | tf_op jit(solution)/shard_map/attend/pallas_call | solution.py:334
  61.1 10.0 %collective-permute-done.2 = bf16[2,64,2048]{2,1,0:T(8,128)(2,1)} collective-permute-done((bf16[2,64,2048]{2,1,0:T(8,128)(2,1)}, bf16[2,64,2048]{2,1,0:T(8,128)(2,1)}, u32[]{:S(2)}, u32[]{:S(2)}) %collective-permute-start.2) | collective-permute-done | bytes 524320 | tf_op jit(solution)/shard_map/ppermute | solution.py:36
  100.9 5.2 collective-permute-done.7
  124.3 7.8 %convert_reduce_fusion = (f32[1024]{0:T(1024)S(1)}, bf16[1024,1024]{1,0:T(8,128)(2,1)S(1)}, bf16[1024,1024]{1,0:T(8,128)(2,1)S(1)}) fusion(f32[1024]{0:T(1024)S(1)} %copy-done.94, bf16[1024,1024]{1,0:T(8,128)(2,1)S(1)} %copy-done.98, bf16[1024,2048]{1,0:T(8,128)(2,1)S(1)} %bitcast.298, bf16[2048,1024]{1,0:T(8,128)(2,1)S(1)} %copy-done.91), kind=kOutput, calls=%fused_computation.30 | convolution fusion | flops 4322229248 | bytes 14688256 | tf_op jit(solution)/shard_map/dot_general | solution.py:280
  132.1 5.2 convolution_convert_fusion.2
  145.9 21.7 %collective-permute-done.11 = bf16[512,1024]{1,0:T(8,128)(2,1)S(1)} collective-permute-done((bf16[512,1024]{1,0:T(8,128)(2,1)S(1)}, bf16[512,1024]{1,0:T(8,128)(2,1)S(1)}, u32[]{:S(2)}, u32[]{:S(2)}) %collective-permute-start.11) | collective-permute-done | bytes 1048608 | tf_op jit(solution)/shard_map/ppermute | solution.py:123
  174.2 7.2 %collective-permute-done.19 = bf16[2,64,2048]{2,1,0:T(8,128)(2,1)S(1)} collective-permute-done((bf16[2,64,2048]{2,1,0:T(8,128)(2,1)S(1)}, bf16[2,64,2048]{2,1,0:T(8,128)(2,1)S(1)}, u32[]{:S(2)}, u32[]{:S(2)}) %collective-permute-start.19) | collective-permute-done | bytes 524320 | tf_op jit(solution)/shard_map/ppermute | solution.py:36
  182.3 5.8 collective-permute-done.17
  217.1 8.3 %collective-permute-done.23 = bf16[2,64,2048]{2,1,0:T(8,128)(2,1)S(1)} collective-permute-done((bf16[2,64,2048]{2,1,0:T(8,128)(2,1)S(1)}, bf16[2,64,2048]{2,1,0:T(8,128)(2,1)S(1)}, u32[]{:S(2)}, u32[]{:S(2)}) %collective-permute-start.23) | collective-permute-done | bytes 524320 | tf_op jit(solution)/shard_map/ppermute | solution.py:36
  237.1 24.4 %collective-permute-start.14 = (bf16[512,1024]{1,0:T(8,128)(2,1)S(1)}, bf16[512,1024]{1,0:T(8,128)(2,1)S(1)}, u32[]{:S(2)}, u32[]{:S(2)}) collective-permute-start(bf16[512,1024]{1,0:T(8,128)(2,1)S(1)} %get-tuple-element.137), channel_id=1, source_target_pairs={{0,8},{16,24},{8,0},{24,16},{1,9},{17,25},{9,1},{25,17},{2,10},{18... | collective-permute-start | bytes 3145736 | tf_op jit(solution)/shard_map/ppermute | solution.py:123
  265.9 18.0 %collective-permute-start.31 = (bf16[512,1024]{1,0:T(8,128)(2,1)S(1)}, bf16[512,1024]{1,0:T(8,128)(2,1)S(1)}, u32[]{:S(2)}, u32[]{:S(2)}) collective-permute-start(bf16[512,1024]{1,0:T(8,128)(2,1)S(1)} %get-tuple-element.131), channel_id=1, source_target_pairs={{0,8},{16,24},{8,0},{24,16},{1,9},{17,25},{9,1},{25,17},{2,10},{18... | collective-permute-start | bytes 3145736 | tf_op jit(solution)/shard_map/ppermute | solution.py:123
  286.5 12.1 %attend_back.1 = (bf16[1024,256]{1,0:T(8,128)(2,1)S(1)}, f32[1792,256]{1,0:T(8,128)S(1)}, f32[1792,256]{1,0:T(8,128)S(1)}) custom-call(bf16[1024,256]{1,0:T(8,128)(2,1)S(1)} %copy-done.23, bf16[2,1792,256]{2,1,0:T(8,128)(2,1)S(1)} %pad_maximum_fusion.6.k_ref.v_ref, bf16[2,1792,256]{2,1,0:T(8,128)(2,1)S(1)} %pad_maximum_fusion.6.k_ref.v_ref, ...), custom_call_target="tpu_custom_call" | custom-call | tf_op jit(solution)/shard_map/attend_back/pallas_call | solution.py:351
  299.3 4.9 collective-permute-done.31.refs_5_
  322.7 18.4 %collective-permute-start.27 = (bf16[512,1024]{1,0:T(8,128)(2,1)S(1)}, bf16[512,1024]{1,0:T(8,128)(2,1)S(1)}, u32[]{:S(2)}, u32[]{:S(2)}) collective-permute-start(bf16[512,1024]{1,0:T(8,128)(2,1)S(1)} %get-tuple-element.135), channel_id=1, source_target_pairs={{0,8},{16,24},{8,0},{24,16},{1,9},{17,25},{9,1},{25,17},{2,10},{18... | collective-permute-start | bytes 3145736 | tf_op jit(solution)/shard_map/ppermute | solution.py:123
  346.5 8.4 %collective-permute-done.34 = bf16[2,64,2048]{2,1,0:T(8,128)(2,1)S(1)} collective-permute-done((bf16[2,64,2048]{2,1,0:T(8,128)(2,1)S(1)}, bf16[2,64,2048]{2,1,0:T(8,128)(2,1)S(1)}, u32[]{:S(2)}, u32[]{:S(2)}) %collective-permute-start.34) | collective-permute-done | bytes 524320 | tf_op jit(solution)/shard_map/ppermute | solution.py:36
  354.9 26.9 %collective-permute-start.44 = (bf16[512,1024]{1,0:T(8,128)(2,1)}, bf16[512,1024]{1,0:T(8,128)(2,1)S(1)}, u32[]{:S(2)}, u32[]{:S(2)}) collective-permute-start(bf16[512,1024]{1,0:T(8,128)(2,1)} %get-tuple-element.129), channel_id=1, source_target_pairs={{0,8},{16,24},{8,0},{24,16},{1,9},{17,25},{9,1},{25,17},{2,10},{18... | collective-permute-start | bytes 3145736 | tf_op jit(solution)/shard_map/ppermute | solution.py:123
  401.0 5.8 bitcast_convert_fusion
  422.6 13.4 %collective-permute-start.50 = (bf16[512,1024]{1,0:T(8,128)(2,1)S(1)}, bf16[512,1024]{1,0:T(8,128)(2,1)S(1)}, u32[]{:S(2)}, u32[]{:S(2)}) collective-permute-start(bf16[512,1024]{1,0:T(8,128)(2,1)S(1)} %get-tuple-element.125), channel_id=1, source_target_pairs={{0,8},{16,24},{8,0},{24,16},{1,9},{17,25},{9,1},{25,17},{2,10},{18... | collective-permute-start | bytes 3145736 | tf_op jit(solution)/shard_map/ppermute | solution.py:123
  437.6 16.2 %collective-permute-start.48 = (bf16[512,1024]{1,0:T(8,128)(2,1)S(1)}, bf16[512,1024]{1,0:T(8,128)(2,1)S(1)}, u32[]{:S(2)}, u32[]{:S(2)}) collective-permute-start(bf16[512,1024]{1,0:T(8,128)(2,1)S(1)} %get-tuple-element.127), channel_id=1, source_target_pairs={{0,8},{16,24},{8,0},{24,16},{1,9},{17,25},{9,1},{25,17},{2,10},{18... | collective-permute-start | bytes 3145736 | tf_op jit(solution)/shard_map/ppermute | solution.py:123
  458.5 15.6 %collective-permute-start.46 = (bf16[512,1024]{1,0:T(8,128)(2,1)}, bf16[512,1024]{1,0:T(8,128)(2,1)}, u32[]{:S(2)}, u32[]{:S(2)}) collective-permute-start(bf16[512,1024]{1,0:T(8,128)(2,1)} %broadcast_select_fusion.3), channel_id=1, source_target_pairs={{0,8},{16,24},{8,0},{24,16},{1,9},{17,25},{9,1},{25,17},{2,10},{18... | collective-permute-start | bytes 3145736 | tf_op jit(solution)/shard_map/ppermute | solution.py:123
  494.1 5.4 collective-permute-done.61
  511.8 4.9 collective-permute-start.65
  529.1 11.1 %collective-permute-done.41 = bf16[2,64,2048]{2,1,0:T(8,128)(2,1)S(1)} collective-permute-done((bf16[2,64,2048]{2,1,0:T(8,128)(2,1)S(1)}, bf16[2,64,2048]{2,1,0:T(8,128)(2,1)S(1)}, u32[]{:S(2)}, u32[]{:S(2)}) %collective-permute-start.41) | collective-permute-done | bytes 524320 | tf_op jit(solution)/shard_map/ppermute | solution.py:36
  543.1 6.2 collective-permute-start.68
  553.5 5.2 collective-permute-start.64
  559.0 13.0 %collective-permute-start.59 = (bf16[512,1024]{1,0:T(8,128)(2,1)S(1)}, bf16[512,1024]{1,0:T(8,128)(2,1)S(1)}, u32[]{:S(2)}, u32[]{:S(2)}) collective-permute-start(bf16[512,1024]{1,0:T(8,128)(2,1)S(1)} %add_convert_fusion.6), channel_id=1, source_target_pairs={{0,8},{16,24},{8,0},{24,16},{1,9},{17,25},{9,1},{25,17},{2,10},{18... | collective-permute-start | bytes 3145736 | tf_op jit(solution)/shard_map/ppermute | solution.py:123
  577.4 18.4 %collective-permute-done.64 = bf16[512,1024]{1,0:T(8,128)(2,1)S(1)} collective-permute-done((bf16[512,1024]{1,0:T(8,128)(2,1)S(1)}, bf16[512,1024]{1,0:T(8,128)(2,1)S(1)}, u32[]{:S(2)}, u32[]{:S(2)}) %collective-permute-start.64) | collective-permute-done | bytes 1048608 | tf_op jit(solution)/shard_map/ppermute | solution.py:123
  600.3 6.8 %collective-permute-start.73 = (bf16[512,1024]{1,0:T(8,128)(2,1)S(1)}, bf16[512,1024]{1,0:T(8,128)(2,1)S(1)}, u32[]{:S(2)}, u32[]{:S(2)}) collective-permute-start(bf16[512,1024]{1,0:T(8,128)(2,1)S(1)} %add_convert_fusion.refs_1_), channel_id=1, source_target_pairs={{0,8},{16,24},{8,0},{24,16},{1,9},{17,25},{9,1},{25,17},{2,10},{18... | collective-permute-start | bytes 3145736 | tf_op jit(solution)/shard_map/ppermute | solution.py:123
  610.1 8.2 %collective-permute-done.59 = bf16[512,1024]{1,0:T(8,128)(2,1)S(1)} collective-permute-done((bf16[512,1024]{1,0:T(8,128)(2,1)S(1)}, bf16[512,1024]{1,0:T(8,128)(2,1)S(1)}, u32[]{:S(2)}, u32[]{:S(2)}) %collective-permute-start.59) | collective-permute-done | bytes 1048608 | tf_op jit(solution)/shard_map/ppermute | solution.py:123
  624.2 14.6 %collective-permute-done.73.refs_2_ = bf16[512,1024]{1,0:T(8,128)(2,1)S(1)} collective-permute-done((bf16[512,1024]{1,0:T(8,128)(2,1)S(1)}, bf16[512,1024]{1,0:T(8,128)(2,1)S(1)}, u32[]{:S(2)}, u32[]{:S(2)}) %collective-permute-start.73) | collective-permute-done | bytes 1048608 | tf_op jit(solution)/shard_map/ppermute | solution.py:123
  (509 shorter events, 287.7 us)
Async XLA Ops:
  140.9 26.7 %collective-permute-start.11 = (bf16[512,1024]{1,0:T(8,128)(2,1)S(1)}, bf16[512,1024]{1,0:T(8,128)(2,1)S(1)}, u32[]{:S(2)}, u32[]{:S(2)}) collective-permute-start(bf16[512,1024]{1,0:T(8,128)(2,1)S(1)} %fusion.35), channel_id=1, source_target_pairs={{0,8},{16,24},{8,0},{24,16},{1,9},{17,25},{9,1},{25,17},{2,10},{18... | collective-permute-start | bytes 3145736 | tf_op jit(solution)/shard_map/ppermute | solution.py:123
  144.9 49.8 %collective-permute-start.16 = (bf16[512,1024]{1,0:T(8,128)(2,1)S(1)}, bf16[512,1024]{1,0:T(8,128)(2,1)S(1)}, u32[]{:S(2)}, u32[]{:S(2)}) collective-permute-start(bf16[512,1024]{1,0:T(8,128)(2,1)S(1)} %fusion.32), channel_id=1, source_target_pairs={{0,8},{16,24},{8,0},{24,16},{1,9},{17,25},{9,1},{25,17},{2,10},{18... | collective-permute-start | bytes 3145736 | tf_op jit(solution)/shard_map/ppermute | solution.py:123
  171.4 40.7 %collective-permute-start.15 = (bf16[512,1024]{1,0:T(8,128)(2,1)}, bf16[512,1024]{1,0:T(8,128)(2,1)}, u32[]{:S(2)}, u32[]{:S(2)}) collective-permute-start(bf16[512,1024]{1,0:T(8,128)(2,1)} %fusion.38), channel_id=1, source_target_pairs={{0,8},{16,24},{8,0},{24,16},{1,9},{17,25},{9,1},{25,17},{2,10},{18... | collective-permute-start | bytes 3145736 | tf_op jit(solution)/shard_map/ppermute | solution.py:123
  228.7 55.2 %collective-permute-start.25 = (bf16[2,2,2,64,2048]{4,3,1,2,0:T(8,128)(2,1)S(1)}, bf16[2,2,2,64,2048]{4,3,1,2,0:T(8,128)(2,1)S(1)}, u32[]{:S(2)}, u32[]{:S(2)}) collective-permute-start(bf16[2,2,2,64,2048]{4,3,1,2,0:T(8,128)(2,1)S(1)} %get-tuple-element.166), channel_id=1, source_target_pairs={{0,1},{1,0},{2,3},{3,2},{4,5},{5,4},{6,7},{7,6},{8,9},{9,8},{10,11... | collective-permute-start | bytes 6291464 | tf_op jit(solution)/shard_map/ppermute | solution.py:36
  231.6 32.7 %collective-permute-start.30 = (bf16[512,1024]{1,0:T(8,128)(2,1)S(1)}, bf16[512,1024]{1,0:T(8,128)(2,1)S(1)}, u32[]{:S(2)}, u32[]{:S(2)}) collective-permute-start(bf16[512,1024]{1,0:T(8,128)(2,1)S(1)} %add_convert_fusion.17), channel_id=1, source_target_pairs={{8,16},{16,8},{9,17},{17,9},{10,18},{18,10},{11,19},{19,11},{12,20... | collective-permute-start | bytes 3145736 | tf_op jit(solution)/shard_map/ppermute | solution.py:123
  237.1 49.3 %collective-permute-start.14 = (bf16[512,1024]{1,0:T(8,128)(2,1)S(1)}, bf16[512,1024]{1,0:T(8,128)(2,1)S(1)}, u32[]{:S(2)}, u32[]{:S(2)}) collective-permute-start(bf16[512,1024]{1,0:T(8,128)(2,1)S(1)} %get-tuple-element.137), channel_id=1, source_target_pairs={{0,8},{16,24},{8,0},{24,16},{1,9},{17,25},{9,1},{25,17},{2,10},{18... | collective-permute-start | bytes 3145736 | tf_op jit(solution)/shard_map/ppermute | solution.py:123
  263.5 46.9 %collective-permute-start.28 = (bf16[512,1024]{1,0:T(8,128)(2,1)S(1)}, bf16[512,1024]{1,0:T(8,128)(2,1)S(1)}, u32[]{:S(2)}, u32[]{:S(2)}) collective-permute-start(bf16[512,1024]{1,0:T(8,128)(2,1)S(1)} %add_convert_fusion.19), channel_id=1, source_target_pairs={{8,16},{16,8},{9,17},{17,9},{10,18},{18,10},{11,19},{19,11},{12,20... | collective-permute-start | bytes 3145736 | tf_op jit(solution)/shard_map/ppermute | solution.py:123
  265.9 38.3 %collective-permute-start.31 = (bf16[512,1024]{1,0:T(8,128)(2,1)S(1)}, bf16[512,1024]{1,0:T(8,128)(2,1)S(1)}, u32[]{:S(2)}, u32[]{:S(2)}) collective-permute-start(bf16[512,1024]{1,0:T(8,128)(2,1)S(1)} %get-tuple-element.131), channel_id=1, source_target_pairs={{0,8},{16,24},{8,0},{24,16},{1,9},{17,25},{9,1},{25,17},{2,10},{18... | collective-permute-start | bytes 3145736 | tf_op jit(solution)/shard_map/ppermute | solution.py:123
  309.1 32.0 %collective-permute-start.32 = (bf16[512,2048]{1,0:T(8,128)(2,1)S(1)}, bf16[512,2048]{1,0:T(8,128)(2,1)S(1)}, u32[]{:S(2)}, u32[]{:S(2)}) collective-permute-start(bf16[512,2048]{1,0:T(8,128)(2,1)S(1)} %dynamic-slice_bitcast_fusion.1), channel_id=1, source_target_pairs={{0,1},{1,0},{2,3},{3,2},{4,5},{5,4},{6,7},{7,6},{8,9},{9,8},{10,11... | collective-permute-start | bytes 6291464 | tf_op jit(solution)/shard_map/ppermute | solution.py:36
  312.2 70.0 %collective-permute-start.29 = (bf16[512,1024]{1,0:T(8,128)(2,1)S(1)}, bf16[512,1024]{1,0:T(8,128)(2,1)S(1)}, u32[]{:S(2)}, u32[]{:S(2)}) collective-permute-start(bf16[512,1024]{1,0:T(8,128)(2,1)S(1)} %get-tuple-element.133), channel_id=1, source_target_pairs={{0,8},{16,24},{8,0},{24,16},{1,9},{17,25},{9,1},{25,17},{2,10},{18... | collective-permute-start | bytes 3145736 | tf_op jit(solution)/shard_map/ppermute | solution.py:123
  316.8 65.4 %collective-permute-start.35 = (bf16[768,512]{1,0:T(8,128)(2,1)S(1)}, bf16[768,512]{1,0:T(8,128)(2,1)S(1)}, u32[]{:S(2)}, u32[]{:S(2)}) collective-permute-start(bf16[768,512]{1,0:T(8,128)(2,1)S(1)} %slice.406), channel_id=1, source_target_pairs={{8,0},{16,8},{24,16},{9,1},{17,9},{25,17},{10,2},{18,10},{26,18},{... | collective-permute-start | bytes 2359304 | tf_op jit(solution)/shard_map/ppermute | solution.py:497
  318.7 24.2 %collective-permute-start.43 = (bf16[512,1024]{1,0:T(8,128)(2,1)S(1)}, bf16[512,1024]{1,0:T(8,128)(2,1)S(1)}, u32[]{:S(2)}, u32[]{:S(2)}) collective-permute-start(bf16[512,1024]{1,0:T(8,128)(2,1)S(1)} %add_convert_fusion.15), channel_id=1, source_target_pairs={{8,16},{16,8},{9,17},{17,9},{10,18},{18,10},{11,19},{19,11},{12,20... | collective-permute-start | bytes 3145736 | tf_op jit(solution)/shard_map/ppermute | solution.py:123
  322.7 75.3 %collective-permute-start.27 = (bf16[512,1024]{1,0:T(8,128)(2,1)S(1)}, bf16[512,1024]{1,0:T(8,128)(2,1)S(1)}, u32[]{:S(2)}, u32[]{:S(2)}) collective-permute-start(bf16[512,1024]{1,0:T(8,128)(2,1)S(1)} %get-tuple-element.135), channel_id=1, source_target_pairs={{0,8},{16,24},{8,0},{24,16},{1,9},{17,25},{9,1},{25,17},{2,10},{18... | collective-permute-start | bytes 3145736 | tf_op jit(solution)/shard_map/ppermute | solution.py:123
  342.9 39.0 %collective-permute-start.33 = (bf16[2,64,2048]{2,1,0:T(8,128)(2,1)S(1)}, bf16[2,64,2048]{2,1,0:T(8,128)(2,1)S(1)}, u32[]{:S(2)}, u32[]{:S(2)}) collective-permute-start(bf16[2,64,2048]{2,1,0:T(8,128)(2,1)S(1)} %dynamic-slice_bitcast_fusion.7), channel_id=1, source_target_pairs={{0,2},{1,3},{2,0},{3,1},{4,6},{5,7},{6,4},{7,5},{8,10},{9,11},{10,... | collective-permute-start | bytes 1572872 | tf_op jit(solution)/shard_map/ppermute | solution.py:36
  354.9 51.9 %collective-permute-start.44 = (bf16[512,1024]{1,0:T(8,128)(2,1)}, bf16[512,1024]{1,0:T(8,128)(2,1)S(1)}, u32[]{:S(2)}, u32[]{:S(2)}) collective-permute-start(bf16[512,1024]{1,0:T(8,128)(2,1)} %get-tuple-element.129), channel_id=1, source_target_pairs={{0,8},{16,24},{8,0},{24,16},{1,9},{17,25},{9,1},{25,17},{2,10},{18... | collective-permute-start | bytes 3145736 | tf_op jit(solution)/shard_map/ppermute | solution.py:123
  391.9 26.7 %collective-permute-start.49 = (bf16[512,1024]{1,0:T(8,128)(2,1)}, bf16[512,1024]{1,0:T(8,128)(2,1)}, u32[]{:S(2)}, u32[]{:S(2)}) collective-permute-start(bf16[512,1024]{1,0:T(8,128)(2,1)} %add_convert_fusion.9), channel_id=1, source_target_pairs={{8,16},{16,8},{9,17},{17,9},{10,18},{18,10},{11,19},{19,11},{12,20... | collective-permute-start | bytes 3145736 | tf_op jit(solution)/shard_map/ppermute | solution.py:123
  407.1 46.7 %collective-permute-start.51 = (bf16[512,2048]{1,0:T(8,128)(2,1)S(1)}, bf16[512,2048]{1,0:T(8,128)(2,1)S(1)}, u32[]{:S(2)}, u32[]{:S(2)}) collective-permute-start(bf16[512,2048]{1,0:T(8,128)(2,1)S(1)} %dynamic-slice_bitcast_fusion), channel_id=1, source_target_pairs={{0,1},{1,0},{2,3},{3,2},{4,5},{5,4},{6,7},{7,6},{8,9},{9,8},{10,11... | collective-permute-start | bytes 6291464 | tf_op jit(solution)/shard_map/ppermute | solution.py:36
  411.0 25.0 %collective-permute-start.47 = (bf16[512,1024]{1,0:T(8,128)(2,1)S(1)}, bf16[512,1024]{1,0:T(8,128)(2,1)S(1)}, u32[]{:S(2)}, u32[]{:S(2)}) collective-permute-start(bf16[512,1024]{1,0:T(8,128)(2,1)S(1)} %add_convert_fusion.11), channel_id=1, source_target_pairs={{8,16},{16,8},{9,17},{17,9},{10,18},{18,10},{11,19},{19,11},{12,20... | collective-permute-start | bytes 3145736 | tf_op jit(solution)/shard_map/ppermute | solution.py:123
  412.4 44.6 %collective-permute-start.45 = (bf16[512,1024]{1,0:T(8,128)(2,1)S(1)}, bf16[512,1024]{1,0:T(8,128)(2,1)S(1)}, u32[]{:S(2)}, u32[]{:S(2)}) collective-permute-start(bf16[512,1024]{1,0:T(8,128)(2,1)S(1)} %add_convert_fusion.13), channel_id=1, source_target_pairs={{8,16},{16,8},{9,17},{17,9},{10,18},{18,10},{11,19},{19,11},{12,20... | collective-permute-start | bytes 3145736 | tf_op jit(solution)/shard_map/ppermute | solution.py:123
  422.6 51.8 %collective-permute-start.50 = (bf16[512,1024]{1,0:T(8,128)(2,1)S(1)}, bf16[512,1024]{1,0:T(8,128)(2,1)S(1)}, u32[]{:S(2)}, u32[]{:S(2)}) collective-permute-start(bf16[512,1024]{1,0:T(8,128)(2,1)S(1)} %get-tuple-element.125), channel_id=1, source_target_pairs={{0,8},{16,24},{8,0},{24,16},{1,9},{17,25},{9,1},{25,17},{2,10},{18... | collective-permute-start | bytes 3145736 | tf_op jit(solution)/shard_map/ppermute | solution.py:123
  437.6 44.9 %collective-permute-start.48 = (bf16[512,1024]{1,0:T(8,128)(2,1)S(1)}, bf16[512,1024]{1,0:T(8,128)(2,1)S(1)}, u32[]{:S(2)}, u32[]{:S(2)}) collective-permute-start(bf16[512,1024]{1,0:T(8,128)(2,1)S(1)} %get-tuple-element.127), channel_id=1, source_target_pairs={{0,8},{16,24},{8,0},{24,16},{1,9},{17,25},{9,1},{25,17},{2,10},{18... | collective-permute-start | bytes 3145736 | tf_op jit(solution)/shard_map/ppermute | solution.py:123
  458.5 53.3 %collective-permute-start.46 = (bf16[512,1024]{1,0:T(8,128)(2,1)}, bf16[512,1024]{1,0:T(8,128)(2,1)}, u32[]{:S(2)}, u32[]{:S(2)}) collective-permute-start(bf16[512,1024]{1,0:T(8,128)(2,1)} %broadcast_select_fusion.3), channel_id=1, source_target_pairs={{0,8},{16,24},{8,0},{24,16},{1,9},{17,25},{9,1},{25,17},{2,10},{18... | collective-permute-start | bytes 3145736 | tf_op jit(solution)/shard_map/ppermute | solution.py:123
  478.0 46.5 %collective-permute-start.67 = (bf16[512,1024]{1,0:T(8,128)(2,1)}, bf16[512,1024]{1,0:T(8,128)(2,1)}, u32[]{:S(2)}, u32[]{:S(2)}) collective-permute-start(bf16[512,1024]{1,0:T(8,128)(2,1)} %add_convert_fusion.3), channel_id=1, source_target_pairs={{8,16},{16,8},{9,17},{17,9},{10,18},{18,10},{11,19},{19,11},{12,20... | collective-permute-start | bytes 3145736 | tf_op jit(solution)/shard_map/ppermute | solution.py:123
  506.7 45.1 %collective-permute-start.63 = (bf16[512,1024]{1,0:T(8,128)(2,1)}, bf16[512,1024]{1,0:T(8,128)(2,1)S(1)}, u32[]{:S(2)}, u32[]{:S(2)}) collective-permute-start(bf16[512,1024]{1,0:T(8,128)(2,1)} %add_convert_fusion.5), channel_id=1, source_target_pairs={{8,16},{16,8},{9,17},{17,9},{10,18},{18,10},{11,19},{19,11},{12,20... | collective-permute-start | bytes 3145736 | tf_op jit(solution)/shard_map/ppermute | solution.py:123
  511.8 64.8 %collective-permute-start.65 = (f32[108,128]{1,0:T(8,128)S(1)}, f32[108,128]{1,0:T(8,128)S(1)}, u32[]{:S(2)}, u32[]{:S(2)}) collective-permute-start(f32[108,128]{1,0:T(8,128)S(1)} %maximum_bitcast_fusion.3), channel_id=1, source_target_pairs={{0,8},{16,24},{8,0},{24,16},{1,9},{17,25},{9,1},{25,17},{2,10},{18... | collective-permute-start | bytes 165896 | tf_op jit(solution)/shard_map/ppermute | solution.py:123
  516.8 26.3 %collective-permute-start.70 = (bf16[2,64,2048]{2,1,0:T(8,128)(2,1)S(1)}, bf16[2,64,2048]{2,1,0:T(8,128)(2,1)S(1)}, u32[]{:S(2)}, u32[]{:S(2)}) collective-permute-start(bf16[2,64,2048]{2,1,0:T(8,128)(2,1)S(1)} %maximum_select_fusion.23), channel_id=1, source_target_pairs={{0,4},{1,5},{2,6},{3,7},{4,0},{5,1},{6,2},{7,3},{8,12},{9,13},{10,... | collective-permute-start | bytes 1572872 | tf_op jit(solution)/shard_map/ppermute | solution.py:36
  543.1 30.2 %collective-permute-start.68 = (bf16[512,1024]{1,0:T(8,128)(2,1)S(1)}, bf16[512,1024]{1,0:T(8,128)(2,1)S(1)}, u32[]{:S(2)}, u32[]{:S(2)}) collective-permute-start(bf16[512,1024]{1,0:T(8,128)(2,1)S(1)} %get-tuple-element.210), channel_id=1, source_target_pairs={{0,8},{16,24},{8,0},{24,16},{1,9},{17,25},{9,1},{25,17},{2,10},{18... | collective-permute-start | bytes 3145736 | tf_op jit(solution)/shard_map/ppermute | solution.py:123
  551.6 45.2 %collective-permute-start.42 = (bf16[2,2,2,64,2048]{4,3,0,1,2:T(8,128)(2,1)S(1)}, bf16[2,2,2,64,2048]{4,3,0,1,2:T(8,128)(2,1)S(1)}, u32[]{:S(2)}, u32[]{:S(2)}) collective-permute-start(bf16[2,2,2,64,2048]{4,3,0,1,2:T(8,128)(2,1)S(1)} %get-tuple-element.162), channel_id=1, source_target_pairs={{0,1},{1,0},{2,3},{3,2},{4,5},{5,4},{6,7},{7,6},{8,9},{9,8},{10,11... | collective-permute-start | bytes 6291464 | tf_op jit(solution)/shard_map/ppermute | solution.py:36
  553.5 42.4 %collective-permute-start.64 = (bf16[512,1024]{1,0:T(8,128)(2,1)S(1)}, bf16[512,1024]{1,0:T(8,128)(2,1)S(1)}, u32[]{:S(2)}, u32[]{:S(2)}) collective-permute-start(bf16[512,1024]{1,0:T(8,128)(2,1)S(1)} %add_convert_fusion.4), channel_id=1, source_target_pairs={{0,8},{16,24},{8,0},{24,16},{1,9},{17,25},{9,1},{25,17},{2,10},{18... | collective-permute-start | bytes 3145736 | tf_op jit(solution)/shard_map/ppermute | solution.py:123
  559.0 59.3 %collective-permute-start.59 = (bf16[512,1024]{1,0:T(8,128)(2,1)S(1)}, bf16[512,1024]{1,0:T(8,128)(2,1)S(1)}, u32[]{:S(2)}, u32[]{:S(2)}) collective-permute-start(bf16[512,1024]{1,0:T(8,128)(2,1)S(1)} %add_convert_fusion.6), channel_id=1, source_target_pairs={{0,8},{16,24},{8,0},{24,16},{1,9},{17,25},{9,1},{25,17},{2,10},{18... | collective-permute-start | bytes 3145736 | tf_op jit(solution)/shard_map/ppermute | solution.py:123
  573.9 33.2 %collective-permute-start.71 = (bf16[2,2,2,64,2048]{4,3,0,1,2:T(8,128)(2,1)S(1)}, bf16[2,2,2,64,2048]{4,3,0,1,2:T(8,128)(2,1)S(1)}, u32[]{:S(2)}, u32[]{:S(2)}) collective-permute-start(bf16[2,2,2,64,2048]{4,3,0,1,2:T(8,128)(2,1)S(1)} %get-tuple-element.158), channel_id=1, source_target_pairs={{0,1},{1,0},{2,3},{3,2},{4,5},{5,4},{6,7},{7,6},{8,9},{9,8},{10,11... | collective-permute-start | bytes 6291464 | tf_op jit(solution)/shard_map/ppermute | solution.py:36
  600.3 38.5 %collective-permute-start.73 = (bf16[512,1024]{1,0:T(8,128)(2,1)S(1)}, bf16[512,1024]{1,0:T(8,128)(2,1)S(1)}, u32[]{:S(2)}, u32[]{:S(2)}) collective-permute-start(bf16[512,1024]{1,0:T(8,128)(2,1)S(1)} %add_convert_fusion.refs_1_), channel_id=1, source_target_pairs={{0,8},{16,24},{8,0},{24,16},{1,9},{17,25},{9,1},{25,17},{2,10},{18... | collective-permute-start | bytes 3145736 | tf_op jit(solution)/shard_map/ppermute | solution.py:123
  (142 other events, 1632.0 us)
